TPU v7x, 512 devices: a whole 4x4x16 slice. The times are simulated.
512 devices in a mesh: page: 16 (over z), blk: 32 (over y, x, core).
Axes of the slice: x: 4, y: 4, z: 16, core: 2. Of those that a mesh axis runs over, the one named last changes fastest.
Arguments:
- queries: bfloat16 [64, 2, 32, 128], P(None, None, 'blk'), may hold values from -192 to 192
- prompt_kv: bfloat16 [256, 64, 32, 256], P('page', None, 'blk'), may hold values from -36 to 36
- tail_kv: bfloat16 [64, 256, 32, 256], P('page', None, 'blk'), may hold values from -36 to 36
- page_table: int32 [4, 64], replicated, may hold values from 0 to 255, as said below
- prompt_len: int32 [4], replicated, may hold values from 1 to 4096, 10240 in all
- tail_len: int32 [64], replicated, may hold values from 0 to 254, as said below
- sample_prompt: int32 [64], replicated, may hold values from 0 to 3, as said below
- stream_in: bfloat16 [64, 2, 7168], P(None, None, 'blk'), may hold values from -6 to 6
- w_out: bfloat16 [4096, 7168], P('blk'), may hold values from -0.09375 to 0.09375
- b_out: bfloat16 [7168], replicated, may hold values from -3 to 3
- ln_gain: bfloat16 [7168], P('page'), may hold values from 0.25 to 1.75
- ln_bias: bfloat16 [7168], P('page'), may hold values from -3 to 3
- w_up: bfloat16 [7168, 28672], P('page', 'blk'), may hold values from -0.0625 to 0.0625
- b_up: bfloat16 [28672], P('blk'), may hold values from -3 to 3
- w_down: bfloat16 [28672, 7168], P('blk', 'page'), may hold values from -0.046875 to 0.046875
- b_down: bfloat16 [7168], P(('page', 'blk')), may hold values from -3 to 3
- w_score: bfloat16 [7168], P(('page', 'blk')), may hold values from -0.0625 to 0.0625
Outputs:
- layer_output: bfloat16 [64, 2, 7168], P(None, None, ('page', 'blk'))
- sample_score: float32 [64, 2], replicated
Inputs may be any that keep to these rules, and one draw needn't show every extreme that they name: `page_table`: every slot number appears exactly once in the table. `tail_len`: some sample reaches the largest value. `sample_prompt`: each prompt has exactly 16 samples.
All inputs are finite; a program needn't handle non-finite values.
Results may differ from a plain program's by a relative error of at most 0.03.
Values may be sent and summed in bfloat16 or wider, within the bound.
A program may use at most 64 MiB of HBM per device.

v0:
```python
import math

import jax
import jax.numpy as jnp
from jax import lax
from jax.sharding import PartitionSpec as P

NEGATIVE = -1e30


def combined_all(value, axis, join):
    pieces = jax.tree.map(lambda part: lax.all_gather(part, axis), value)
    head = jax.tree.map(lambda part: part[0], pieces)
    tail = jax.tree.map(lambda part: part[1:], pieces)
    subtotal, _ = lax.scan(lambda subtotal, share: (join(subtotal, share), None), head, tail)
    return subtotal


def join_partials(earlier, later):
    highest = jnp.maximum(earlier[0], later[0])
    left_scale = jnp.exp(earlier[0] - highest)
    right_scale = jnp.exp(later[0] - highest)
    return (
        highest,
        earlier[1] * left_scale + later[1] * right_scale,
        earlier[2] * left_scale[..., None] + later[2] * right_scale[..., None],
    )


def softmax_part(scores, visible):
    masked = jnp.where(visible, scores, NEGATIVE)
    highest = jnp.max(masked, axis=-1)
    weights = jnp.where(visible, jnp.exp(scores - highest[..., None]), 0.0)
    return (highest, jnp.sum(weights, axis=-1), weights.astype(jnp.bfloat16))


def body(
    queries,
    prompt_kv,
    tail_kv,
    page_table,
    prompt_len,
    tail_len,
    sample_prompt,
    stream_in,
    w_out,
    b_out,
    ln_gain,
    ln_bias,
    w_up,
    b_up,
    w_down,
    b_down,
    w_score,
):
    samples, new_count, heads_dev, head_dim = queries.shape
    slots_dev, page_len = (prompt_kv.shape[0], prompt_kv.shape[1])
    own_count, tail_max = (tail_kv.shape[0], tail_kv.shape[1])
    prompts, pages_max = page_table.shape
    page_pos = lax.axis_index("page")
    blk_pos = lax.axis_index("blk")
    inv_sqrt = 1.0 / math.sqrt(head_dim)
    entries = page_table.reshape(-1)
    slot_ids = page_pos * slots_dev + jnp.arange(slots_dev, dtype=jnp.int32)
    matched = (entries[:, None] == slot_ids[None, :]).astype(jnp.int32)
    owner_index = jnp.sum(matched * jnp.arange(entries.shape[0], dtype=jnp.int32)[:, None], axis=0)
    slot_prompt = owner_index // pages_max
    slot_page = owner_index % pages_max
    prompt_pick = (slot_prompt[:, None] == jnp.arange(prompts, dtype=jnp.int32)[None, :]).astype(
        jnp.int32
    )
    slot_limit = jnp.sum(prompt_pick * prompt_len[None, :], axis=1)
    key_pos = slot_page[:, None] * page_len + jnp.arange(page_len, dtype=jnp.int32)[None, :]
    key_live = (key_pos < slot_limit[:, None]).reshape(-1)
    key_prompt = jnp.repeat(slot_prompt, page_len)
    prompt_visible = ((sample_prompt[:, None] == key_prompt[None, :]) & key_live[None, :])[
        :, None, None, :
    ]
    cache_rows = prompt_kv.reshape(slots_dev * page_len, heads_dev, 2 * head_dim)
    prompt_scores = (
        jnp.einsum(
            "snhd,khd->snhk",
            queries,
            cache_rows[:, :, :head_dim],
            preferred_element_type=jnp.float32,
        )
        * inv_sqrt
    )
    high_p, sum_p, weights_p = softmax_part(prompt_scores, prompt_visible)
    mixed_p = jnp.einsum(
        "snhk,khd->snhd", weights_p, cache_rows[:, :, head_dim:], preferred_element_type=jnp.float32
    )
    first_row = page_pos * own_count
    own_queries = lax.dynamic_slice_in_dim(queries, first_row, own_count, 0)
    own_lengths = lax.dynamic_slice_in_dim(tail_len, first_row, own_count, 0)
    tail_scores = (
        jnp.einsum(
            "snhd,sthd->snht",
            own_queries,
            tail_kv[..., :head_dim],
            preferred_element_type=jnp.float32,
        )
        * inv_sqrt
    )
    reach_pos = own_lengths[:, None] + jnp.arange(new_count, dtype=jnp.int32)[None, :]
    tail_visible = (
        jnp.arange(tail_max, dtype=jnp.int32)[None, None, None, :] <= reach_pos[:, :, None, None]
    )
    high_t, sum_t, weights_t = softmax_part(tail_scores, tail_visible)
    mixed_t = jnp.einsum(
        "snht,sthd->snhd", weights_t, tail_kv[..., head_dim:], preferred_element_type=jnp.float32
    )
    high_t = lax.dynamic_update_slice_in_dim(
        jnp.full(high_p.shape, NEGATIVE, jnp.float32), high_t, first_row, 0
    )
    sum_t = lax.dynamic_update_slice_in_dim(
        jnp.zeros(sum_p.shape, jnp.float32), sum_t, first_row, 0
    )
    mixed_t = lax.dynamic_update_slice_in_dim(
        jnp.zeros(mixed_p.shape, jnp.float32), mixed_t, first_row, 0
    )
    partial_value = join_partials((high_p, sum_p, mixed_p), (high_t, sum_t, mixed_t))
    merged = combined_all(partial_value, "page", join_partials)
    weight_sum, weighted = (merged[1], merged[2])
    attention = (
        (weighted / weight_sum[..., None])
        .astype(jnp.bfloat16)
        .reshape(samples * new_count, heads_dev * head_dim)
    )
    contrib = jnp.dot(attention, w_out, preferred_element_type=jnp.float32)
    slice_width = stream_in.shape[2]
    column = blk_pos * slice_width
    own_stream = stream_in.reshape(samples * new_count, slice_width).astype(jnp.float32)
    contrib = lax.dynamic_update_slice_in_dim(
        contrib, lax.dynamic_slice_in_dim(contrib, column, slice_width, 1) + own_stream, column, 1
    )
    summed = lax.psum(contrib, "blk")
    residual = (summed + b_out.astype(jnp.float32)).astype(jnp.bfloat16)
    residual_f = residual.astype(jnp.float32)
    row_mean = jnp.mean(residual_f, axis=-1, keepdims=True)
    centred = residual_f - row_mean
    inverse_std = lax.rsqrt(jnp.mean(centred * centred, axis=-1, keepdims=True) + 1e-05)
    feature_count = ln_gain.shape[0]
    first_col = page_pos * feature_count
    normed = (
        lax.dynamic_slice_in_dim(centred, first_col, feature_count, 1)
        * inverse_std
        * ln_gain.astype(jnp.float32)
        + ln_bias.astype(jnp.float32)
    ).astype(jnp.bfloat16)
    up_part = jnp.dot(normed, w_up, preferred_element_type=jnp.float32).astype(jnp.bfloat16)
    hidden_sum = lax.psum(up_part, "page").astype(jnp.float32)
    hidden = jnp.maximum(hidden_sum + b_up.astype(jnp.float32), 0.0).astype(jnp.bfloat16)
    projected = jnp.dot(hidden, w_down, preferred_element_type=jnp.float32)
    out_share = lax.psum_scatter(projected, "blk", scatter_dimension=1, tiled=True)
    piece_width = b_down.shape[0]
    out_column = first_col + blk_pos * piece_width
    output = (
        out_share
        + lax.dynamic_slice_in_dim(residual_f, out_column, piece_width, 1)
        + b_down.astype(jnp.float32)
    ).astype(jnp.bfloat16)
    score_part = jnp.sum(output.astype(jnp.float32) * w_score.astype(jnp.float32), axis=-1)
    row_score = lax.psum(score_part, ("page", "blk"))
    return (output.reshape(samples, new_count, piece_width), row_score.reshape(samples, new_count))


def solution(mesh):
    placed = (
        P(None, None, "blk", None),
        P("page", None, "blk", None),
        P("page", None, "blk", None),
        P(),
        P(),
        P(),
        P(),
        P(None, None, "blk"),
        P("blk", None),
        P(),
        P("page"),
        P("page"),
        P("page", "blk"),
        P("blk"),
        P("blk", "page"),
        P(("page", "blk")),
        P(("page", "blk")),
    )
    return jax.shard_map(
        body,
        mesh=mesh,
        in_specs=placed,
        out_specs=(P(None, None, ("page", "blk")), P()),
        check_vma=False,
    )
```

profile of v0, /device:TPU:1, one launch (start us, length us, event | category | flops | bytes accessed | tf_op | source)
XLA Modules:
  0.0 637.5 jit_solution(366933933234473874)
XLA Ops:
  7.2 0.9 dynamic_slice.26
  8.2 1.2 select_reduce_fusion.2
  9.7 1.2 fusion.14
  10.9 0.8 eq.50
  11.9 0.7 select_reduce_fusion.3
  13.2 0.8 compare_and_fusion
  14.0 1.3 select_reduce_fusion
  15.5 1.9 fusion.8
  17.6 33.1 %all-gather = f32[1024,2,1]{1,2,0:T(1,128)S(1)} all-gather(f32[64,2,1]{1,2,0:T(1,128)S(1)} %copy.76), channel_id=2, replica_groups=mesh['page'=16,'blk'=32] {'page'}, dimensions={0}, use_global_device_ids=true | all-gather | bytes 8704 | tf_op jit(solution)/shard_map/all_gather | solution.py:12
  50.9 25.1 %all-gather.1 = f32[1024,2,1]{1,2,0:T(1,128)S(1)} all-gather(f32[64,2,1]{1,2,0:T(1,128)S(1)} %copy.78), channel_id=3, replica_groups=mesh['page'=16,'blk'=32] {'page'}, dimensions={0}, use_global_device_ids=true | all-gather | bytes 8704 | tf_op jit(solution)/shard_map/all_gather | solution.py:12
  76.7 8.9 %all-gather.5.cloned.1.call-done = f32[1024,2,1,128]{3,0,1,2:T(8,128)} async-done(((f32[64,2,1,128]{3,0,1,2:T(8,128)}), f32[1024,2,1,128]{3,0,1,2:T(8,128)}) %all-gather.5.cloned.1.call-update) | async-done | bytes 1048592 | tf_op jit(solution)/shard_map/all_gather | solution.py:12
  85.6 0.8 slice.52
  86.5 1.3 slice.55
  87.7 10.6 %while.14 = (s32[]{:T(128)}, f32[64,2,1]{0,1,2:T(2,128)S(1)}, f32[64,2,1]{0,1,2:T(2,128)S(1)}, f32[64,2,1,128]{3,2,1,0:T(1,128)S(1)}, f32[15,64,2,1]{1,2,3,0:T(2...) while((s32[]{:T(128)}, f32[64,2,1]{0,1,2:T(2,128)S(1)}, ...), condition=%wide.region_7.8_spmd, body=%wide.region_6.7_spmd.sunk | while | flops 50050 | bytes 468577 | solution.py:15
  88.1 0.4 multiply_add_fusion.2
  90.9 0.4 multiply_add_fusion.2
  98.7 0.6 fusion.44
  99.4 1.8 copy-done.1
  101.3 1.9 dynamic_update_slice.15
  103.3 147.2 %all-reduce.5.cloned.1.call-done = f32[128,7168]{1,0:T(8,128)} async-done(((f32[128,7168]{1,0:T(8,128)}), f32[128,7168]{1,0:T(8,128)}) %all-reduce.5.cloned.1.call-update) | async-done | bytes 3670032 | tf_op jit(solution)/shard_map/psum | solution.py:137
  250.5 2.5 fusion.42
  253.1 0.8 multiply_reduce_fusion
  253.9 1.0 copy-done.2
  254.9 1.1 convolution_convert_fusion
  256.1 126.2 %all-reduce.7.cloned.1.call-done = bf16[128,896]{1,0:T(8,128)(2,1)} async-done(((bf16[128,896]{1,0:T(8,128)(2,1)}), bf16[128,896]{1,0:T(8,128)(2,1)}) %all-reduce.7.cloned.1.call-update) | async-done | bytes 229392 | tf_op jit(solution)/shard_map/psum | solution.py:152
  382.3 2.0 fusion.18
  384.4 1.3 dynamic-slice
  386.3 137.0 %all-reduce.9.cloned.1.call-done = f32[128,448]{1,0:T(8,128)} async-done(((f32[128,448]{1,0:T(8,128)}), f32[128,448]{1,0:T(8,128)}) %all-reduce.9.cloned.1.call-update) | async-done | bytes 229392
  523.3 1.1 multiply_reduce_fusion.1
  524.6 105.0 %psum.23 = f32[64,2]{1,0:T(8,128)S(1)} all-reduce(f32[64,2]{1,0:T(8,128)S(1)} %reshape.251), channel_id=1, replica_groups=mesh['page'=16,'blk'=32] {'page','blk'}, use_global_device_ids=true, to_apply=%region_14.15 | all-reduce | flops 128 | bytes 1024 | tf_op jit(solution)/shard_map/psum | solution.py:164
  629.6 0.6 copy.92
  630.3 0.7 copy.91
  (192 shorter events, 12.6 us)
Async XLA Ops:
  7.2 91.5 %copy-start = (bf16[128,7168]{1,0:T(8,128)(2,1)S(1)}, bf16[128,7168]{1,0:T(8,128)(2,1)}, u32[]{:S(2)}) copy-start(bf16[128,7168]{1,0:T(8,128)(2,1)} %param.27) | copy-start | bytes 5505028
  7.2 78.4 %all-gather.5.cloned.1.call-start = ((), (), s32[]{:S(2)}) async-start(), calls=%async_computation.2 | async-start | bytes 1114112 | tf_op jit(solution)/shard_map/all_gather | solution.py:12
  12.7 63.9 %copy-start.5 = (bf16[64,2,224]{2,1,0:T(2,128)(2,1)S(1)}, bf16[64,2,224]{2,1,0:T(2,128)(2,1)}, u32[]{:S(2)}) copy-start(bf16[64,2,224]{2,1,0:T(2,128)(2,1)} %param.26) | copy-start | bytes 172036
  17.4 233.1 %all-reduce.5.cloned.1.call-start = ((), (), s32[]{:S(2)}) async-start(), calls=%async_computation | async-start | bytes 7340032 | tf_op jit(solution)/shard_map/psum | solution.py:137
  98.7 4.6 copy-start.6
  98.7 4.6 copy-start.8
  98.7 4.6 copy-start.9
  99.3 1.8 copy-start.1
  103.2 279.1 %all-reduce.7.cloned.1.call-start = ((), (), s32[]{:S(2)}) async-start(), calls=%async_computation.1 | async-start | bytes 458752 | tf_op jit(solution)/shard_map/psum | solution.py:152
  253.0 1.9 copy-start.2
  253.1 1.9 copy-start.4
  253.1 3.0 copy-start.7
  253.1 129.2 %copy-start.3 = (bf16[896,448]{0,1:T(8,128)(2,1)S(1)}, bf16[896,448]{0,1:T(8,128)(2,1)}, u32[]{:S(2)}) copy-start(bf16[896,448]{0,1:T(8,128)(2,1)} %param.33) | copy-start | bytes 2408452
  253.1 131.3 %copy-start.10 = (bf16[14]{0:T(256)(128)(2,1)S(1)}, bf16[14]{0:T(256)(128)(2,1)}, u32[]{:S(2)}) copy-start(bf16[14]{0:T(256)(128)(2,1)} %param.34) | copy-start | bytes 88
  253.1 131.3 %copy-start.11 = (bf16[14]{0:T(256)(128)(2,1)S(1)}, bf16[14]{0:T(256)(128)(2,1)}, u32[]{:S(2)}) copy-start(bf16[14]{0:T(256)(128)(2,1)} %param.35) | copy-start | bytes 88
  256.0 267.3 %all-reduce.9.cloned.1.call-start = ((), (), s32[]{:S(2)}) async-start(), calls=%async_computation.3 | async-start | bytes 524288
Sparse Core Ops, SparseCore 0:
  17.6 67.9 all-gather.4
  103.3 147.1 all-reduce.4
  256.2 126.0 all-reduce.6
  385.7 137.5 all-reduce.8
where the time goes:
time: 638 us; the launch traced here: 637 us
  waiting for transfers between devices  419 us (66%)
  blocking collectives  163 us (26%)
  local copies, waits for them, and re-layouts  16.8 us (3%)
  between operations  14.8 us (2%)
  other arithmetic  13.4 us (2%)
  matrix products  9.27 us (1%)
    psum x1, waiting for transfers between devices, body(): summed = lax.psum(contrib, 'blk')  147 us
    unnamed x5, waiting for transfers between devices  137 us
    psum x1, waiting for transfers between devices, body(): hidden_sum = lax.psum(up_part, 'page').astype(jnp.float32)  126 us
    psum x1, blocking collectives, body(): row_score = lax.psum(score_part, ('page', 'blk'))  105 us
    all_gather x2, blocking collectives, combined_all(): pieces = jax.tree.map(lambda part: lax.all_gather(part, axis), value)  58.2 us
  transfers between devices with their start and end apart: 4, of which 4 were waited for; matrix products, arithmetic and copies ran while one was open for 0% of the time, Pallas kernels for 0%

commit v1 on v0

v1 whole, which is shorter than its diff:
```python
import math

import jax
import jax.numpy as jnp
from jax import lax
from jax.sharding import PartitionSpec as P

NEGATIVE = -1e30


def exchange(x, axis):
    return lax.all_to_all(x, axis, 0, 0, tiled=True)


def softmax_part(scores, visible):
    masked = jnp.where(visible, scores, NEGATIVE)
    highest = jnp.max(masked, axis=-1)
    weights = jnp.where(visible, jnp.exp(scores - highest[..., None]), 0.0)
    return (highest, jnp.sum(weights, axis=-1), weights.astype(jnp.bfloat16))


def ordered_sum(stack):
    total = stack[0]
    for j in range(1, stack.shape[0]):
        total = total + stack[j]
    return total


def body(
    queries,
    prompt_kv,
    tail_kv,
    page_table,
    prompt_len,
    tail_len,
    sample_prompt,
    stream_in,
    w_out,
    b_out,
    ln_gain,
    ln_bias,
    w_up,
    b_up,
    w_down,
    b_down,
    w_score,
):
    samples, new_count, heads_dev, head_dim = queries.shape
    slots_dev, page_len = (prompt_kv.shape[0], prompt_kv.shape[1])
    own_count, tail_max = (tail_kv.shape[0], tail_kv.shape[1])
    prompts, pages_max = page_table.shape
    n_page = samples // own_count
    page_pos = lax.axis_index("page")
    blk_pos = lax.axis_index("blk")
    inv_sqrt = 1.0 / math.sqrt(head_dim)
    width = w_out.shape[1]
    rows_own = own_count * new_count

    entries = page_table.reshape(-1)
    slot_ids = page_pos * slots_dev + jnp.arange(slots_dev, dtype=jnp.int32)
    matched = (entries[:, None] == slot_ids[None, :]).astype(jnp.int32)
    owner_index = jnp.sum(matched * jnp.arange(entries.shape[0], dtype=jnp.int32)[:, None], axis=0)
    slot_prompt = owner_index // pages_max
    slot_page = owner_index % pages_max
    prompt_pick = (slot_prompt[:, None] == jnp.arange(prompts, dtype=jnp.int32)[None, :]).astype(
        jnp.int32
    )
    slot_limit = jnp.sum(prompt_pick * prompt_len[None, :], axis=1)
    key_pos = slot_page[:, None] * page_len + jnp.arange(page_len, dtype=jnp.int32)[None, :]
    key_live = (key_pos < slot_limit[:, None]).reshape(-1)
    key_prompt = jnp.repeat(slot_prompt, page_len)
    prompt_visible = ((sample_prompt[:, None] == key_prompt[None, :]) & key_live[None, :])[
        :, None, None, :
    ]

    cache_rows = prompt_kv.reshape(slots_dev * page_len, heads_dev, 2 * head_dim)
    prompt_scores = (
        jnp.einsum(
            "snhd,khd->snhk",
            queries,
            cache_rows[:, :, :head_dim],
            preferred_element_type=jnp.float32,
        )
        * inv_sqrt
    )
    high_p, sum_p, weights_p = softmax_part(prompt_scores, prompt_visible)
    mixed_p = jnp.einsum(
        "snhk,khd->snhd", weights_p, cache_rows[:, :, head_dim:], preferred_element_type=jnp.float32
    )

    first_row = page_pos * own_count
    own_queries = lax.dynamic_slice_in_dim(queries, first_row, own_count, 0)
    own_lengths = lax.dynamic_slice_in_dim(tail_len, first_row, own_count, 0)
    tail_scores = (
        jnp.einsum(
            "snhd,sthd->snht",
            own_queries,
            tail_kv[..., :head_dim],
            preferred_element_type=jnp.float32,
        )
        * inv_sqrt
    )
    reach_pos = own_lengths[:, None] + jnp.arange(new_count, dtype=jnp.int32)[None, :]
    tail_visible = (
        jnp.arange(tail_max, dtype=jnp.int32)[None, None, None, :] <= reach_pos[:, :, None, None]
    )
    high_t, sum_t, weights_t = softmax_part(tail_scores, tail_visible)
    mixed_t = jnp.einsum(
        "snht,sthd->snhd", weights_t, tail_kv[..., head_dim:], preferred_element_type=jnp.float32
    )

    packed = jnp.concatenate([mixed_p, high_p[..., None], sum_p[..., None]], axis=-1)
    packed = packed.reshape(n_page, rows_own * heads_dev, head_dim + 2)
    got = exchange(packed, "page")
    high_all = got[..., head_dim]
    sum_all = got[..., head_dim + 1]
    mixed_all = got[..., :head_dim]
    high_t = high_t.reshape(rows_own * heads_dev)
    sum_t = sum_t.reshape(rows_own * heads_dev)
    mixed_t = mixed_t.reshape(rows_own * heads_dev, head_dim)
    highest = jnp.maximum(jnp.max(high_all, axis=0), high_t)
    scale_all = jnp.exp(high_all - highest[None, :])
    scale_t = jnp.exp(high_t - highest)
    weight_sum = ordered_sum(sum_all * scale_all) + sum_t * scale_t
    weighted = ordered_sum(mixed_all * scale_all[..., None]) + mixed_t * scale_t[..., None]
    attention = (
        (weighted / weight_sum[..., None])
        .astype(jnp.bfloat16)
        .reshape(rows_own, heads_dev * head_dim)
    )

    contrib = jnp.dot(attention, w_out, preferred_element_type=jnp.float32)
    slice_width = stream_in.shape[2]
    column = blk_pos * slice_width
    own_stream = (
        lax.dynamic_slice_in_dim(stream_in, first_row, own_count, 0)
        .reshape(rows_own, slice_width)
        .astype(jnp.float32)
    )
    contrib = lax.dynamic_update_slice_in_dim(
        contrib, lax.dynamic_slice_in_dim(contrib, column, slice_width, 1) + own_stream, column, 1
    )
    n_blk = width // slice_width
    pieces = contrib.reshape(rows_own, n_blk, slice_width).transpose(1, 0, 2)
    summed = ordered_sum(exchange(pieces, "blk"))
    own_bias = lax.dynamic_slice_in_dim(b_out, column, slice_width, 0).astype(jnp.float32)
    res_piece = (summed + own_bias).astype(jnp.bfloat16).astype(jnp.float32)
    gathered = exchange(jnp.broadcast_to(res_piece[None], (n_blk,) + res_piece.shape), "blk")
    residual_f = gathered.transpose(1, 0, 2).reshape(rows_own, width)

    row_mean = jnp.mean(residual_f, axis=-1, keepdims=True)
    centred = residual_f - row_mean
    inverse_std = lax.rsqrt(jnp.mean(centred * centred, axis=-1, keepdims=True) + 1e-05)
    scaled = centred * inverse_std

    feature_count = ln_gain.shape[0]
    piece_width = b_down.shape[0]
    scaled3 = scaled.reshape(rows_own, n_page, feature_count)
    res3 = lax.dynamic_slice_in_dim(
        residual_f.reshape(rows_own, n_page, feature_count), blk_pos * piece_width, piece_width, 2
    )
    outgoing = jnp.concatenate([scaled3, res3], axis=-1).transpose(1, 0, 2)
    incoming = exchange(outgoing, "page").reshape(samples * new_count, feature_count + piece_width)
    normed = (
        incoming[:, :feature_count] * ln_gain.astype(jnp.float32) + ln_bias.astype(jnp.float32)
    ).astype(jnp.bfloat16)
    residual_piece = incoming[:, feature_count:]

    up_part = jnp.dot(normed, w_up, preferred_element_type=jnp.float32).astype(jnp.bfloat16)
    up_rows = exchange(up_part.astype(jnp.float32).reshape(n_page, rows_own, -1), "page")
    hidden_rows = jnp.maximum(ordered_sum(up_rows) + b_up.astype(jnp.float32), 0.0)
    hidden_rows = hidden_rows.astype(jnp.bfloat16).astype(jnp.float32)
    hidden = exchange(
        jnp.broadcast_to(hidden_rows[None], (n_page,) + hidden_rows.shape), "page"
    ).reshape(samples * new_count, -1)

    projected = jnp.dot(hidden.astype(jnp.bfloat16), w_down, preferred_element_type=jnp.float32)
    proj_pieces = projected.reshape(samples * new_count, n_blk, piece_width).transpose(1, 0, 2)
    out_share = ordered_sum(exchange(proj_pieces, "blk"))
    output = (out_share + residual_piece + b_down.astype(jnp.float32)).astype(jnp.bfloat16)

    score_part = jnp.sum(output.astype(jnp.float32) * w_score.astype(jnp.float32), axis=-1)
    score_part = score_part.reshape(1, samples * new_count)
    blk_sum = ordered_sum(
        exchange(jnp.broadcast_to(score_part[None], (n_blk,) + score_part.shape), "blk")
    )
    row_score = ordered_sum(
        exchange(jnp.broadcast_to(blk_sum[None], (n_page,) + blk_sum.shape), "page")
    )
    return (output.reshape(samples, new_count, piece_width), row_score.reshape(samples, new_count))


def solution(mesh):
    placed = (
        P(None, None, "blk", None),
        P("page", None, "blk", None),
        P("page", None, "blk", None),
        P(),
        P(),
        P(),
        P(),
        P(None, None, "blk"),
        P("blk", None),
        P(),
        P("page"),
        P("page"),
        P("page", "blk"),
        P("blk"),
        P("blk", "page"),
        P(("page", "blk")),
        P(("page", "blk")),
    )
    return jax.shard_map(
        body,
        mesh=mesh,
        in_specs=placed,
        out_specs=(P(None, None, ("page", "blk")), P()),
        check_vma=False,
    )
```

time: 638 us -> 197 us (0.31)
  waiting for transfers between devices: 419 us -> 92.1 us
  blocking collectives: 163 us -> 10.5 us
  starting transfers between devices: 0.16 us -> 70 us
  between operations: 14.8 us -> 0.99 us
  other arithmetic: 13.4 us -> 6.19 us
    psum x2 -> x0, waiting for transfers between devices: 273 us -> none  [the longest x1 147 us: body(): summed = lax.psum(contrib, 'blk')]
    unnamed x5 -> x0, waiting for transfers between devices: 137 us -> none
    psum x1 -> x0, blocking collectives: 105 us -> none  [body(): row_score = lax.psum(score_part, ('page', 'blk'))]
    all_to_all x0 -> x8, waiting for transfers between devices: none -> 92.1 us  [exchange(): return lax.all_to_all(x, axis, 0, 0, tiled=True)]
    all_to_all x0 -> x8, starting transfers between devices: none -> 70 us  [exchange(): return lax.all_to_all(x, axis, 0, 0, tiled=True)]
    all_gather x2 -> x0, blocking collectives: 58.2 us -> none  [combined_all(): pieces = jax.tree.map(lambda part: lax.all_gather(part, axis), value)]
    all_to_all x0 -> x1, blocking collectives: none -> 10.5 us  [exchange(): return lax.all_to_all(x, axis, 0, 0, tiled=True)]
    all_gather x1 -> x0, waiting for transfers between devices: 8.86 us -> none  [combined_all(): pieces = jax.tree.map(lambda part: lax.all_gather(part, axis), value)]
  transfers between devices with their start and end apart: 4 -> 8, of which waited for: 4 -> 8; matrix products, arithmetic and copies ran while one was open for 0% -> 3% of each run, Pallas kernels for 0% -> 0%
where the time goes in v1:
time: 197 us; the launch traced here: 196 us
  waiting for transfers between devices  92.1 us (47%)
  starting transfers between devices  70 us (36%)
  local copies, waits for them, and re-layouts  10.5 us (5%)
  blocking collectives  10.5 us (5%)
  other arithmetic  6.19 us (3%)
  matrix products  5.57 us (3%)
    all_to_all x8, waiting for transfers between devices, exchange(): return lax.all_to_all(x, axis, 0, 0, tiled=True)  92.1 us
    all_to_all x8, starting transfers between devices, exchange(): return lax.all_to_all(x, axis, 0, 0, tiled=True)  70 us
    all_to_all x1, blocking collectives, exchange(): return lax.all_to_all(x, axis, 0, 0, tiled=True)  10.5 us
  transfers between devices with their start and end apart: 8, of which 8 were waited for; matrix products, arithmetic and copies ran while one was open for 3% of the time, Pallas kernels for 0%

profile of v1, /device:TPU:1, one launch (start us, length us, event | category | flops | bytes accessed | tf_op | source)
XLA Modules:
  0.0 195.9 jit_solution(8441189200442126085)
XLA Ops:
  0.7 0.9 eq.50
  1.8 0.7 select_reduce_fusion.3
  2.8 0.8 compare_and_fusion
  3.6 1.3 select_reduce_fusion
  5.2 1.3 convolution_bitcast_fusion.1
  6.8 0.7 pad_maximum_fusion
  7.6 15.7 %all-to-all-start = ((f32[16,8,130]{2,1,0:T(8,128)}), f32[16,8,130]{2,1,0:T(8,128)S(1)}, u32[]{:S(2)}, u32[]{:S(2)}) async-start(f32[16,8,130]{2,1,0:T(8,128)} %pad_maximum_fusion), calls=%async_computation | async-start | bytes 262144 | tf_op jit(solution)/shard_map/all_to_all | solution.py:12
  23.5 0.9 select_reduce_fusion.2
  25.7 9.6 %all-to-all-done = f32[16,8,130]{2,1,0:T(8,128)S(1)} async-done(((f32[16,8,130]{2,1,0:T(8,128)}), f32[16,8,130]{2,1,0:T(8,128)S(1)}, u32[]{:S(2)}, u32[]{:S(2)}) %all-to-all-start) | async-done | bytes 66592 | tf_op jit(solution)/shard_map/all_to_all | solution.py:12
  37.2 0.8 copy.344
  38.1 10.7 %all-to-all-start.1 = ((f32[32,8,224]{2,1,0:T(8,128)}), f32[32,8,224]{2,1,0:T(8,128)S(1)}, u32[]{:S(2)}, u32[]{:S(2)}) async-start(f32[32,8,224]{2,1,0:T(8,128)} %bitcast.219), calls=%async_computation.1 | async-start | bytes 524288 | tf_op jit(solution)/shard_map/all_to_all | solution.py:12
  48.8 0.8 dynamic-slice_convert_fusion.1
  49.5 8.1 %all-to-all-done.1 = f32[32,8,224]{2,1,0:T(8,128)S(1)} async-done(((f32[32,8,224]{2,1,0:T(8,128)}), f32[32,8,224]{2,1,0:T(8,128)S(1)}, u32[]{:S(2)}, u32[]{:S(2)}) %all-to-all-start.1) | async-done | bytes 229408 | tf_op jit(solution)/shard_map/all_to_all | solution.py:12
  57.7 0.7 broadcast_in_dim.55
  58.4 3.8 %all-to-all-start.2 = ((f32[32,8,224]{2,1,0:T(8,128)}), f32[32,8,224]{2,1,0:T(8,128)S(1)}, u32[]{:S(2)}, u32[]{:S(2)}) async-start(f32[32,8,224]{2,1,0:T(8,128)} %broadcast_in_dim.55), calls=%async_computation.2 | async-start | bytes 524288 | tf_op jit(solution)/shard_map/all_to_all | solution.py:12
  62.2 9.0 %all-to-all-done.2 = f32[32,8,224]{2,1,0:T(8,128)S(1)} async-done(((f32[32,8,224]{2,1,0:T(8,128)}), f32[32,8,224]{2,1,0:T(8,128)S(1)}, u32[]{:S(2)}, u32[]{:S(2)}) %all-to-all-start.2) | async-done | bytes 229408 | tf_op jit(solution)/shard_map/all_to_all | solution.py:12
  72.2 0.8 copy.259
  73.0 3.6 %all-to-all-start.3 = ((f32[16,8,462]{2,1,0:T(8,128)}), f32[16,8,462]{2,1,0:T(8,128)S(1)}, u32[]{:S(2)}, u32[]{:S(2)}) async-start(f32[16,8,462]{2,1,0:T(8,128)} %copy.259), calls=%async_computation.3 | async-start | bytes 524288 | tf_op jit(solution)/shard_map/all_to_all | solution.py:12
  76.6 14.1 %all-to-all-done.3 = f32[16,8,462]{2,1,0:T(8,128)S(1)} async-done(((f32[16,8,462]{2,1,0:T(8,128)}), f32[16,8,462]{2,1,0:T(8,128)S(1)}, u32[]{:S(2)}, u32[]{:S(2)}) %all-to-all-start.3) | async-done | bytes 236576 | tf_op jit(solution)/shard_map/all_to_all | solution.py:12
  90.7 1.1 fusion.2
  91.8 10.1 %all-to-all-start.4 = ((f32[16,8,896]{2,1,0:T(8,128)}), f32[16,8,896]{2,1,0:T(8,128)S(1)}, u32[]{:S(2)}, u32[]{:S(2)}) async-start(f32[16,8,896]{2,1,0:T(8,128)} %fusion.2), calls=%async_computation.4 | async-start | bytes 917504 | tf_op jit(solution)/shard_map/all_to_all | solution.py:12
  101.9 20.7 %all-to-all-done.4 = f32[16,8,896]{2,1,0:T(8,128)S(1)} async-done(((f32[16,8,896]{2,1,0:T(8,128)}), f32[16,8,896]{2,1,0:T(8,128)S(1)}, u32[]{:S(2)}, u32[]{:S(2)}) %all-to-all-start.4) | async-done | bytes 458784 | tf_op jit(solution)/shard_map/all_to_all | solution.py:12
  123.4 11.9 %all-to-all-start.5 = ((bf16[16,8,896]{2,1,0:T(8,128)(2,1)}), bf16[16,8,896]{2,1,0:T(8,128)(2,1)S(1)}, u32[]{:S(2)}, u32[]{:S(2)}) async-start(bf16[16,8,896]{2,1,0:T(8,128)(2,1)} %broadcast_in_dim.104), calls=%async_computation.5 | async-start | bytes 458752 | tf_op jit(solution)/shard_map/all_to_all | solution.py:12
  135.3 1.3 dot_general.44
  136.6 11.4 %all-to-all-done.5 = bf16[16,8,896]{2,1,0:T(8,128)(2,1)S(1)} async-done(((bf16[16,8,896]{2,1,0:T(8,128)(2,1)}), bf16[16,8,896]{2,1,0:T(8,128)(2,1)S(1)}, u32[]{:S(2)}, u32[]{:S(2)}) %all-to-all-start.5) | async-done | bytes 229408 | tf_op jit(solution)/shard_map/all_to_all | solution.py:12
  148.4 0.8 copy.261
  149.2 9.2 %all-to-all-start.6 = ((f32[32,128,14]{1,2,0:T(8,128)}), f32[32,128,14]{1,2,0:T(8,128)S(1)}, u32[]{:S(2)}, u32[]{:S(2)}) async-start(f32[32,128,14]{1,2,0:T(8,128)} %copy.261), calls=%async_computation.6 | async-start | bytes 524288 | tf_op jit(solution)/shard_map/all_to_all | solution.py:12
  158.7 8.7 %all-to-all-done.6 = f32[32,128,14]{1,2,0:T(8,128)S(1)} async-done(((f32[32,128,14]{1,2,0:T(8,128)}), f32[32,128,14]{1,2,0:T(8,128)S(1)}, u32[]{:S(2)}, u32[]{:S(2)}) %all-to-all-start.6) | async-done | bytes 229408 | tf_op jit(solution)/shard_map/all_to_all | solution.py:12
  167.6 10.5 %all_to_all.45 = f32[32,1,128]{2,1,0:T(1,128)S(1)} all-to-all(f32[32,1,128]{2,1,0:T(1,128)S(1)} %broadcast_in_dim.105), channel_id=1, replica_groups=mesh['page'=16,'blk'=32] {'blk'}, dimensions={0} | all-to-all | bytes 32768 | tf_op jit(solution)/shard_map/all_to_all | solution.py:12
  178.7 5.1 %all-to-all-start.8 = ((f32[16,1,128]{2,1,0:T(1,128)}), f32[16,1,128]{2,1,0:T(1,128)S(1)}, u32[]{:S(2)}, u32[]{:S(2)}) async-start(f32[16,1,128]{2,1,0:T(1,128)} %broadcast_in_dim.107), calls=%async_computation.8 | async-start | bytes 16384 | tf_op jit(solution)/shard_map/all_to_all | solution.py:12
  183.9 0.7 copy.281
  184.6 10.5 %all-to-all-done.8 = f32[16,1,128]{2,1,0:T(1,128)S(1)} async-done(((f32[16,1,128]{2,1,0:T(1,128)}), f32[16,1,128]{2,1,0:T(1,128)S(1)}, u32[]{:S(2)}, u32[]{:S(2)}) %all-to-all-start.8) | async-done | bytes 8224 | tf_op jit(solution)/shard_map/all_to_all | solution.py:12
  (83 shorter events, 8.5 us)
Async XLA Ops:
  0.6 35.6 %copy-start = (bf16[128,7168]{1,0:T(8,128)(2,1)S(1)}, bf16[128,7168]{1,0:T(8,128)(2,1)}, u32[]{:S(2)}) copy-start(bf16[128,7168]{1,0:T(8,128)(2,1)} %param.25) | copy-start | bytes 5505028
  2.8 20.5 %copy-start.6 = (s32[64]{0:T(128)S(1)}, s32[64]{0:T(128)}, u32[]{:S(2)}) copy-start(s32[64]{0:T(128)} %param.22) | copy-start | bytes 772
  2.8 20.7 %copy-start.5 = (bf16[4,256,1,256]{3,1,2,0:T(8,128)(2,1)S(1)}, bf16[4,256,1,256]{3,1,2,0:T(8,128)(2,1)}, u32[]{:S(2)}) copy-start(bf16[4,256,1,256]{3,1,2,0:T(8,128)(2,1)} %param.19) | copy-start | bytes 1572868
  7.6 27.7 %all-to-all-start = ((f32[16,8,130]{2,1,0:T(8,128)}), f32[16,8,130]{2,1,0:T(8,128)S(1)}, u32[]{:S(2)}, u32[]{:S(2)}) async-start(f32[16,8,130]{2,1,0:T(8,128)} %pad_maximum_fusion), calls=%async_computation | async-start | bytes 262144 | tf_op jit(solution)/shard_map/all_to_all | solution.py:12
  38.1 19.6 %all-to-all-start.1 = ((f32[32,8,224]{2,1,0:T(8,128)}), f32[32,8,224]{2,1,0:T(8,128)S(1)}, u32[]{:S(2)}, u32[]{:S(2)}) async-start(f32[32,8,224]{2,1,0:T(8,128)} %bitcast.219), calls=%async_computation.1 | async-start | bytes 524288 | tf_op jit(solution)/shard_map/all_to_all | solution.py:12
  58.4 12.8 %all-to-all-start.2 = ((f32[32,8,224]{2,1,0:T(8,128)}), f32[32,8,224]{2,1,0:T(8,128)S(1)}, u32[]{:S(2)}, u32[]{:S(2)}) async-start(f32[32,8,224]{2,1,0:T(8,128)} %broadcast_in_dim.55), calls=%async_computation.2 | async-start | bytes 524288 | tf_op jit(solution)/shard_map/all_to_all | solution.py:12
  71.4 5.2 %copy-start.3 = (bf16[448]{0:T(512)(128)(2,1)S(1)}, bf16[448]{0:T(512)(128)(2,1)}, u32[]{:S(2)}) copy-start(bf16[448]{0:T(512)(128)(2,1)} %param.27) | copy-start | bytes 2692
  71.4 5.2 %copy-start.4 = (bf16[448]{0:T(512)(128)(2,1)S(1)}, bf16[448]{0:T(512)(128)(2,1)}, u32[]{:S(2)}) copy-start(bf16[448]{0:T(512)(128)(2,1)} %param.28) | copy-start | bytes 2692
  71.4 19.3 %copy-start.1 = (bf16[448,896]{1,0:T(8,128)(2,1)S(1)}, bf16[448,896]{1,0:T(8,128)(2,1)}, u32[]{:S(2)}) copy-start(bf16[448,896]{1,0:T(8,128)(2,1)} %param.29) | copy-start | bytes 2408452
  72.2 29.8 %copy-start.2 = (bf16[896]{0:T(1024)(128)(2,1)S(1)}, bf16[896]{0:T(1024)(128)(2,1)}, u32[]{:S(2)}) copy-start(bf16[896]{0:T(1024)(128)(2,1)} %param.30) | copy-start | bytes 5380
  73.0 17.7 %all-to-all-start.3 = ((f32[16,8,462]{2,1,0:T(8,128)}), f32[16,8,462]{2,1,0:T(8,128)S(1)}, u32[]{:S(2)}, u32[]{:S(2)}) async-start(f32[16,8,462]{2,1,0:T(8,128)} %copy.259), calls=%async_computation.3 | async-start | bytes 524288 | tf_op jit(solution)/shard_map/all_to_all | solution.py:12
  91.8 30.8 %all-to-all-start.4 = ((f32[16,8,896]{2,1,0:T(8,128)}), f32[16,8,896]{2,1,0:T(8,128)S(1)}, u32[]{:S(2)}, u32[]{:S(2)}) async-start(f32[16,8,896]{2,1,0:T(8,128)} %fusion.2), calls=%async_computation.4 | async-start | bytes 917504 | tf_op jit(solution)/shard_map/all_to_all | solution.py:12
  123.4 24.6 %all-to-all-start.5 = ((bf16[16,8,896]{2,1,0:T(8,128)(2,1)}), bf16[16,8,896]{2,1,0:T(8,128)(2,1)S(1)}, u32[]{:S(2)}, u32[]{:S(2)}) async-start(bf16[16,8,896]{2,1,0:T(8,128)(2,1)} %broadcast_in_dim.104), calls=%async_computation.5 | async-start | bytes 458752 | tf_op jit(solution)/shard_map/all_to_all | solution.py:12
  135.2 23.2 %copy-start.7 = (bf16[14]{0:T(256)(128)(2,1)S(1)}, bf16[14]{0:T(256)(128)(2,1)}, u32[]{:S(2)}) copy-start(bf16[14]{0:T(256)(128)(2,1)} %param.32) | copy-start | bytes 88
  135.3 23.2 %copy-start.8 = (bf16[14]{0:T(256)(128)(2,1)S(1)}, bf16[14]{0:T(256)(128)(2,1)}, u32[]{:S(2)}) copy-start(bf16[14]{0:T(256)(128)(2,1)} %param.33) | copy-start | bytes 88
  149.2 18.1 %all-to-all-start.6 = ((f32[32,128,14]{1,2,0:T(8,128)}), f32[32,128,14]{1,2,0:T(8,128)S(1)}, u32[]{:S(2)}, u32[]{:S(2)}) async-start(f32[32,128,14]{1,2,0:T(8,128)} %copy.261), calls=%async_computation.6 | async-start | bytes 524288 | tf_op jit(solution)/shard_map/all_to_all | solution.py:12
  178.7 16.4 %all-to-all-start.8 = ((f32[16,1,128]{2,1,0:T(1,128)}), f32[16,1,128]{2,1,0:T(1,128)S(1)}, u32[]{:S(2)}, u32[]{:S(2)}) async-start(f32[16,1,128]{2,1,0:T(1,128)} %broadcast_in_dim.107), calls=%async_computation.8 | async-start | bytes 16384 | tf_op jit(solution)/shard_map/all_to_all | solution.py:12

commit v2 on v1

--- a/solution.py
+++ b/solution.py
@@ -3,13 +3,78 @@
 import jax
 import jax.numpy as jnp
 from jax import lax
+from jax.experimental import pallas as pl
+from jax.experimental.pallas import tpu as pltpu
 from jax.sharding import PartitionSpec as P
 
 NEGATIVE = -1e30
-
-
-def exchange(x, axis):
-    return lax.all_to_all(x, axis, 0, 0, tiled=True)
+AXES = ("page", "blk")
+MESH_ID = pl.DeviceIdType.MESH
+
+
+def exchange_kernel(axis, n, mode, x_ref, o_ref, buf, send_sem, recv_sem):
+    me = lax.axis_index(axis)
+    coords = [lax.axis_index(name) for name in AXES]
+
+    def device(j):
+        return tuple(j if name == axis else c for name, c in zip(AXES, coords))
+
+    if mode == "gather":
+        buf[me] = x_ref[...]
+    else:
+        buf[me] = x_ref[me]
+    barrier = pltpu.get_barrier_semaphore()
+    for k in range(1, n):
+        peer = lax.rem(me + k, n)
+        pl.semaphore_signal(barrier, inc=1, device_id=device(peer), device_id_type=MESH_ID)
+    pl.semaphore_wait(barrier, n - 1)
+    copies = []
+    for k in range(1, n):
+        peer = lax.rem(me + k, n)
+        source = x_ref if mode == "gather" else x_ref.at[peer]
+        copy = pltpu.make_async_remote_copy(
+            src_ref=source,
+            dst_ref=buf.at[me],
+            send_sem=send_sem.at[k],
+            recv_sem=recv_sem.at[k],
+            device_id=device(peer),
+            device_id_type=MESH_ID,
+        )
+        copy.start()
+        copies.append(copy)
+    for copy in copies:
+        copy.wait()
+    if mode == "sum":
+        total = buf[0]
+        for j in range(1, n):
+            total = total + buf[j]
+        o_ref[...] = total
+    else:
+        o_ref[...] = buf[...]
+
+
+CALL_IDS = {}
+
+
+def exchange(x, axis, mode="swap"):
+    n = lax.axis_size(axis)
+    x = x.astype(jnp.float32)
+    chunk = x.shape if mode == "gather" else x.shape[1:]
+    out_shape = chunk if mode == "sum" else (n,) + tuple(chunk)
+    cid = len(CALL_IDS)
+    CALL_IDS[cid] = axis
+    return pl.pallas_call(
+        lambda *refs: exchange_kernel(axis, n, mode, *refs),
+        out_shape=jax.ShapeDtypeStruct(out_shape, jnp.float32),
+        in_specs=[pl.BlockSpec(memory_space=pltpu.VMEM)],
+        out_specs=pl.BlockSpec(memory_space=pltpu.VMEM),
+        scratch_shapes=[
+            pltpu.VMEM((n,) + tuple(chunk), jnp.float32),
+            pltpu.SemaphoreType.DMA((n,)),
+            pltpu.SemaphoreType.DMA((n,)),
+        ],
+        compiler_params=pltpu.CompilerParams(collective_id=cid, has_side_effects=True),
+    )(x)
 
 
 def softmax_part(scores, visible):
@@ -45,6 +110,7 @@
     b_down,
     w_score,
 ):
+    CALL_IDS.clear()
     samples, new_count, heads_dev, head_dim = queries.shape
     slots_dev, page_len = (prompt_kv.shape[0], prompt_kv.shape[1])
     own_count, tail_max = (tail_kv.shape[0], tail_kv.shape[1])
@@ -142,10 +208,10 @@
     )
     n_blk = width // slice_width
     pieces = contrib.reshape(rows_own, n_blk, slice_width).transpose(1, 0, 2)
-    summed = ordered_sum(exchange(pieces, "blk"))
+    summed = exchange(pieces, "blk", "sum")
     own_bias = lax.dynamic_slice_in_dim(b_out, column, slice_width, 0).astype(jnp.float32)
     res_piece = (summed + own_bias).astype(jnp.bfloat16).astype(jnp.float32)
-    gathered = exchange(jnp.broadcast_to(res_piece[None], (n_blk,) + res_piece.shape), "blk")
+    gathered = exchange(res_piece, "blk", "gather")
     residual_f = gathered.transpose(1, 0, 2).reshape(rows_own, width)
 
     row_mean = jnp.mean(residual_f, axis=-1, keepdims=True)
@@ -167,26 +233,20 @@
     residual_piece = incoming[:, feature_count:]
 
     up_part = jnp.dot(normed, w_up, preferred_element_type=jnp.float32).astype(jnp.bfloat16)
-    up_rows = exchange(up_part.astype(jnp.float32).reshape(n_page, rows_own, -1), "page")
-    hidden_rows = jnp.maximum(ordered_sum(up_rows) + b_up.astype(jnp.float32), 0.0)
+    up_rows = exchange(up_part.astype(jnp.float32).reshape(n_page, rows_own, -1), "page", "sum")
+    hidden_rows = jnp.maximum(up_rows + b_up.astype(jnp.float32), 0.0)
     hidden_rows = hidden_rows.astype(jnp.bfloat16).astype(jnp.float32)
-    hidden = exchange(
-        jnp.broadcast_to(hidden_rows[None], (n_page,) + hidden_rows.shape), "page"
-    ).reshape(samples * new_count, -1)
+    hidden = exchange(hidden_rows, "page", "gather").reshape(samples * new_count, -1)
 
     projected = jnp.dot(hidden.astype(jnp.bfloat16), w_down, preferred_element_type=jnp.float32)
     proj_pieces = projected.reshape(samples * new_count, n_blk, piece_width).transpose(1, 0, 2)
-    out_share = ordered_sum(exchange(proj_pieces, "blk"))
+    out_share = exchange(proj_pieces, "blk", "sum")
     output = (out_share + residual_piece + b_down.astype(jnp.float32)).astype(jnp.bfloat16)
 
     score_part = jnp.sum(output.astype(jnp.float32) * w_score.astype(jnp.float32), axis=-1)
     score_part = score_part.reshape(1, samples * new_count)
-    blk_sum = ordered_sum(
-        exchange(jnp.broadcast_to(score_part[None], (n_blk,) + score_part.shape), "blk")
-    )
-    row_score = ordered_sum(
-        exchange(jnp.broadcast_to(blk_sum[None], (n_page,) + blk_sum.shape), "page")
-    )
+    blk_sum = ordered_sum(exchange(score_part, "blk", "gather"))
+    row_score = ordered_sum(exchange(blk_sum, "page", "gather"))
     return (output.reshape(samples, new_count, piece_width), row_score.reshape(samples, new_count))
 
 

time: 197 us -> 238 us (1.21)
  Pallas kernels: 0 us -> 202 us
  waiting for transfers between devices: 92.1 us -> 0 us
  starting transfers between devices: 70 us -> 0 us
  other arithmetic: 6.19 us -> 17.5 us
  blocking collectives: 10.5 us -> 0 us
    pallas_call x0 -> x9, Pallas kernels: none -> 202 us  [exchange(): pl.pallas_call(lambda *refs: exchange_kernel(axis, n, mode, *refs), out_s...]
    all_to_all x8 -> x0, waiting for transfers between devices: 92.1 us -> none  [exchange(): return lax.all_to_all(x, axis, 0, 0, tiled=True)]
    all_to_all x8 -> x0, starting transfers between devices: 70 us -> none  [exchange(): return lax.all_to_all(x, axis, 0, 0, tiled=True)]
    all_to_all x1 -> x0, blocking collectives: 10.5 us -> none  [exchange(): return lax.all_to_all(x, axis, 0, 0, tiled=True)]
    convert_element_type x1 -> x3, other arithmetic: 0.01 us -> 2.65 us  [the longest x1 1.36 us: body(): hidden_rows = hidden_rows.astype(jnp.bfloat16).astype(jnp.float32)]
  transfers between devices with their start and end apart: 8 -> 0, of which waited for: 8 -> 0; matrix products, arithmetic and copies ran while one was open for 3% -> 0% of each run, Pallas kernels for 0% -> 0%
where the time goes in v2:
time: 238 us; the launch traced here: 236 us
  Pallas kernels  202 us (85%)
  other arithmetic  17.5 us (7%)
  local copies, waits for them, and re-layouts  9.72 us (4%)
  matrix products  6.56 us (3%)
    pallas_call x9, Pallas kernels, exchange(): pl.pallas_call(lambda *refs: exchange_kernel(axis, n, mode, *refs), out_s...  202 us

profile of v2, /device:TPU:1, one launch (start us, length us, event | category | flops | bytes accessed | tf_op | source)
XLA Modules:
  0.0 236.3 jit_solution(5392855721277871697)
XLA Ops:
  0.7 0.9 eq.50
  1.8 0.7 select_reduce_fusion.3
  2.8 0.8 compare_and_fusion
  3.6 1.3 select_reduce_fusion
  4.9 1.3 convolution_bitcast_fusion
  7.6 22.7 %shard_map.176 = f32[16,8,130]{2,1,0:T(8,128)} custom-call(f32[16,8,130]{2,1,0:T(8,128)} %pad_maximum_fusion.refs_0_), custom_call_target="tpu_custom_call" | custom-call | tf_op jit(solution)/shard_map/pallas_call | solution.py:66
  30.3 1.1 fusion.45
  31.6 0.9 select_reduce_fusion.2
  33.4 0.9 subtract_exponential_fusion
  34.5 0.9 slice_multiply_fusion.1
  37.4 0.8 copy.125
  38.2 15.8 %shard_map.177 = f32[8,224]{1,0:T(8,128)} custom-call(f32[32,8,224]{2,1,0:T(8,128)} %bitcast.164), custom_call_target="tpu_custom_call" | custom-call | tf_op jit(solution)/shard_map/pallas_call | solution.py:66
  54.0 0.8 dynamic-slice_convert_fusion.1
  54.8 1.3 fusion.25.refs_0_
  56.1 12.2 %shard_map.178 = f32[32,8,224]{2,1,0:T(8,128)} custom-call(f32[8,224]{1,0:T(8,128)} %fusion.25.refs_0_), custom_call_target="tpu_custom_call" | custom-call | tf_op jit(solution)/shard_map/pallas_call | solution.py:66
  68.3 1.1 copy.107
  69.5 1.1 reduce_sum.67
  70.7 1.2 multiply_reduce_fusion
  72.2 0.8 maximum_bitcast_fusion.refs_0_
  72.9 23.8 %shard_map.179 = f32[16,8,462]{2,1,0:T(8,128)} custom-call(f32[16,8,462]{2,1,0:T(8,128)} %maximum_bitcast_fusion.refs_0_), custom_call_target="tpu_custom_call" | custom-call | tf_op jit(solution)/shard_map/pallas_call | solution.py:66
  96.8 2.0 fusion.2.refs_0_
  98.9 29.6 %shard_map.180 = f32[8,896]{1,0:T(8,128)} custom-call(f32[16,8,896]{2,1,0:T(8,128)} %fusion.2.refs_0_), custom_call_target="tpu_custom_call" | custom-call | tf_op jit(solution)/shard_map/pallas_call | solution.py:66
  128.4 1.4 fusion.24.refs_0_
  129.8 27.9 %shard_map.181 = f32[16,8,896]{2,1,0:T(8,128)} custom-call(f32[8,896]{1,0:T(8,128)} %fusion.24.refs_0_), custom_call_target="tpu_custom_call" | custom-call | tf_op jit(solution)/shard_map/pallas_call | solution.py:66
  157.7 1.4 dot_general.44
  159.5 2.0 copy.111
  161.5 46.0 %shard_map.182 = f32[128,14]{1,0:T(8,128)} custom-call(f32[32,128,14]{2,1,0:T(8,128)} %bitcast.160), custom_call_target="tpu_custom_call" | custom-call | tf_op jit(solution)/shard_map/pallas_call | solution.py:66
  207.6 1.6 multiply_reduce_fusion.1
  209.1 9.5 %shard_map.183 = f32[32,1,128]{2,1,0:T(1,128)} custom-call(f32[1,128]{1,0:T(1,128)} %bitcast.170), custom_call_target="tpu_custom_call" | custom-call | tf_op jit(solution)/shard_map/pallas_call | solution.py:66
  218.7 1.3 bitcast_add_fusion.refs_0_
  220.0 14.1 %shard_map.184 = f32[16,1,128]{2,1,0:T(1,128)} custom-call(f32[1,128]{1,0:T(1,128)} %bitcast_add_fusion.refs_0_), custom_call_target="tpu_custom_call" | custom-call | tf_op jit(solution)/shard_map/pallas_call | solution.py:66
  234.1 0.8 add_reduce_fusion.1
  (67 shorter events, 7.3 us)
Async XLA Ops:
  0.6 35.1 %copy-start = (bf16[128,7168]{1,0:T(8,128)(2,1)S(1)}, bf16[128,7168]{1,0:T(8,128)(2,1)}, u32[]{:S(2)}) copy-start(bf16[128,7168]{1,0:T(8,128)(2,1)} %param.25) | copy-start | bytes 5505028
  3.6 27.9 %copy-start.7 = (s32[64]{0:T(128)S(1)}, s32[64]{0:T(128)}, u32[]{:S(2)}) copy-start(s32[64]{0:T(128)} %param.22) | copy-start | bytes 772
  3.6 28.0 %copy-start.6 = (bf16[4,256,1,256]{3,1,2,0:T(8,128)(2,1)S(1)}, bf16[4,256,1,256]{3,1,2,0:T(8,128)(2,1)}, u32[]{:S(2)}) copy-start(bf16[4,256,1,256]{3,1,2,0:T(8,128)(2,1)} %param.19) | copy-start | bytes 1572868
  68.3 28.5 %copy-start.4 = (bf16[448]{0:T(512)(128)(2,1)S(1)}, bf16[448]{0:T(512)(128)(2,1)}, u32[]{:S(2)}) copy-start(bf16[448]{0:T(512)(128)(2,1)} %param.27) | copy-start | bytes 2692
  68.3 28.5 %copy-start.5 = (bf16[448]{0:T(512)(128)(2,1)S(1)}, bf16[448]{0:T(512)(128)(2,1)}, u32[]{:S(2)}) copy-start(bf16[448]{0:T(512)(128)(2,1)} %param.28) | copy-start | bytes 2692
  68.3 28.5 %copy-start.2 = (bf16[448,896]{1,0:T(8,128)(2,1)S(1)}, bf16[448,896]{1,0:T(8,128)(2,1)}, u32[]{:S(2)}) copy-start(bf16[448,896]{1,0:T(8,128)(2,1)} %param.29) | copy-start | bytes 2408452
  72.1 56.4 %copy-start.3 = (bf16[896]{0:T(1024)(128)(2,1)S(1)}, bf16[896]{0:T(1024)(128)(2,1)}, u32[]{:S(2)}) copy-start(bf16[896]{0:T(1024)(128)(2,1)} %param.30) | copy-start | bytes 5380
  157.7 1.4 copy-start.1
  159.5 48.0 %copy-start.8 = (bf16[14]{0:T(256)(128)(2,1)S(1)}, bf16[14]{0:T(256)(128)(2,1)}, u32[]{:S(2)}) copy-start(bf16[14]{0:T(256)(128)(2,1)} %param.32) | copy-start | bytes 88
  159.5 48.0 %copy-start.9 = (bf16[14]{0:T(256)(128)(2,1)S(1)}, bf16[14]{0:T(256)(128)(2,1)}, u32[]{:S(2)}) copy-start(bf16[14]{0:T(256)(128)(2,1)} %param.33) | copy-start | bytes 88

commit v3 on v1

--- a/solution.py
+++ b/solution.py
@@ -3,13 +3,156 @@
 import jax
 import jax.numpy as jnp
 from jax import lax
+from jax.experimental import pallas as pl
+from jax.experimental.pallas import tpu as pltpu
 from jax.sharding import PartitionSpec as P
 
 NEGATIVE = -1e30
+AXES = ("page", "blk")
+MESH_ID = pl.DeviceIdType.MESH
+
+
+def device_on(axis, j):
+    return tuple(j if name == axis else lax.axis_index(name) for name in AXES)
+
+
+def enter(sizes):
+    barrier = pltpu.get_barrier_semaphore()
+    total = 0
+    for axis, n in sizes:
+        me = lax.axis_index(axis)
+        for k in range(1, n):
+            peer = lax.rem(me + k, n)
+            pl.semaphore_signal(barrier, inc=1, device_id=device_on(axis, peer), device_id_type=MESH_ID)
+        total += n - 1
+    pl.semaphore_wait(barrier, total)
+
+
+def send_round(axis, n, source, buf, send_sem, recv_sem):
+    me = lax.axis_index(axis)
+    copies = []
+    for k in range(1, n):
+        peer = lax.rem(me + k, n)
+        copy = pltpu.make_async_remote_copy(
+            src_ref=source(peer),
+            dst_ref=buf.at[me],
+            send_sem=send_sem.at[k],
+            recv_sem=recv_sem.at[k],
+            device_id=device_on(axis, peer),
+            device_id_type=MESH_ID,
+        )
+        copy.start()
+        copies.append(copy)
+    for copy in copies:
+        copy.wait()
+
+
+def slot_sum(buf, n):
+    total = buf[0].astype(jnp.float32)
+    for j in range(1, n):
+        total = total + buf[j].astype(jnp.float32)
+    return total
+
+
+def exchange_kernel(axis, n, x_ref, o_ref, buf, send_sem, recv_sem):
+    me = lax.axis_index(axis)
+    buf[me] = x_ref[me]
+    enter([(axis, n)])
+    send_round(axis, n, lambda peer: x_ref.at[peer], buf, send_sem, recv_sem)
+    o_ref[...] = buf[...]
+
+
+def sum_gather_kernel(axis, n, finish, x_ref, extra_ref, o_ref, buf, gat, sems):
+    me = lax.axis_index(axis)
+    buf[me] = x_ref[me]
+    enter([(axis, n)])
+    send_round(axis, n, lambda peer: x_ref.at[peer], buf, sems.at[0], sems.at[1])
+    gat[me] = finish(slot_sum(buf, n), extra_ref[...]).astype(gat.dtype)
+    send_round(axis, n, lambda peer: gat.at[me], gat, sems.at[2], sems.at[3])
+    o_ref[...] = gat[...]
+
+
+def output_kernel(n_blk, n_page, x_ref, res_ref, bias_ref, score_w_ref, out_ref, score_ref,
+                  buf, blk_buf, page_buf, sems):
+    me_blk = lax.axis_index("blk")
+    me_page = lax.axis_index("page")
+    buf[me_blk] = x_ref[me_blk]
+    enter([("blk", n_blk), ("page", n_page)])
+    send_round("blk", n_blk, lambda peer: x_ref.at[peer], buf, sems.at[0], sems.at[1])
+    output = (slot_sum(buf, n_blk) + res_ref[...] + bias_ref[...]).astype(jnp.bfloat16)
+    out_ref[...] = output
+    blk_buf[me_blk] = jnp.sum(output.astype(jnp.float32) * score_w_ref[...], axis=0, keepdims=True)
+    send_round("blk", n_blk, lambda peer: blk_buf.at[me_blk], blk_buf, sems.at[2], sems.at[3])
+    page_buf[me_page] = slot_sum(blk_buf, n_blk)
+    send_round("page", n_page, lambda peer: page_buf.at[me_page], page_buf, sems.at[4], sems.at[5])
+    score_ref[...] = slot_sum(page_buf, n_page)
+
+
+CALL_IDS = {}
+
+
+def next_id(axis):
+    cid = len(CALL_IDS)
+    CALL_IDS[cid] = axis
+    return cid
+
+
+def vmem_specs(count):
+    return [pl.BlockSpec(memory_space=pltpu.VMEM)] * count
 
 
 def exchange(x, axis):
-    return lax.all_to_all(x, axis, 0, 0, tiled=True)
+    n = lax.axis_size(axis)
+    return pl.pallas_call(
+        lambda *refs: exchange_kernel(axis, n, *refs),
+        out_shape=jax.ShapeDtypeStruct(x.shape, x.dtype),
+        in_specs=vmem_specs(1),
+        out_specs=vmem_specs(1)[0],
+        scratch_shapes=[
+            pltpu.VMEM(x.shape, x.dtype),
+            pltpu.SemaphoreType.DMA((n,)),
+            pltpu.SemaphoreType.DMA((n,)),
+        ],
+        compiler_params=pltpu.CompilerParams(collective_id=next_id(axis), has_side_effects=True),
+    )(x)
+
+
+def sum_gather(x, extra, axis, finish, out_dtype):
+    n = lax.axis_size(axis)
+    return pl.pallas_call(
+        lambda *refs: sum_gather_kernel(axis, n, finish, *refs),
+        out_shape=jax.ShapeDtypeStruct(x.shape, out_dtype),
+        in_specs=vmem_specs(2),
+        out_specs=vmem_specs(1)[0],
+        scratch_shapes=[
+            pltpu.VMEM(x.shape, x.dtype),
+            pltpu.VMEM(x.shape, out_dtype),
+            pltpu.SemaphoreType.DMA((4, n)),
+        ],
+        compiler_params=pltpu.CompilerParams(collective_id=next_id(axis), has_side_effects=True),
+    )(x, extra)
+
+
+def output_and_score(x, res, bias, score_w):
+    n_blk = lax.axis_size("blk")
+    n_page = lax.axis_size("page")
+    lanes = x.shape[2]
+    return pl.pallas_call(
+        lambda *refs: output_kernel(n_blk, n_page, *refs),
+        out_shape=(
+            jax.ShapeDtypeStruct(x.shape[1:], jnp.bfloat16),
+            jax.ShapeDtypeStruct((1, lanes), jnp.float32),
+        ),
+        in_specs=vmem_specs(4),
+        out_specs=tuple(vmem_specs(2)),
+        scratch_shapes=[
+            pltpu.VMEM(x.shape, jnp.float32),
+            pltpu.VMEM((n_blk, 1, lanes), jnp.float32),
+            pltpu.VMEM((n_page, 1, lanes), jnp.float32),
+            pltpu.SemaphoreType.DMA((6, max(n_blk, n_page))),
+        ],
+        compiler_params=pltpu.CompilerParams(collective_id=next_id("both"), has_side_effects=True),
+    )(x, res, bias, score_w)
 
 
 def softmax_part(scores, visible):
@@ -45,6 +188,7 @@
     b_down,
     w_score,
 ):
+    CALL_IDS.clear()
     samples, new_count, heads_dev, head_dim = queries.shape
     slots_dev, page_len = (prompt_kv.shape[0], prompt_kv.shape[1])
     own_count, tail_max = (tail_kv.shape[0], tail_kv.shape[1])
@@ -142,10 +286,14 @@
     )
     n_blk = width // slice_width
     pieces = contrib.reshape(rows_own, n_blk, slice_width).transpose(1, 0, 2)
-    summed = ordered_sum(exchange(pieces, "blk"))
     own_bias = lax.dynamic_slice_in_dim(b_out, column, slice_width, 0).astype(jnp.float32)
-    res_piece = (summed + own_bias).astype(jnp.bfloat16).astype(jnp.float32)
-    gathered = exchange(jnp.broadcast_to(res_piece[None], (n_blk,) + res_piece.shape), "blk")
+    gathered = sum_gather(
+        pieces,
+        own_bias.reshape(1, slice_width),
+        "blk",
+        lambda total, bias: (total + bias).astype(jnp.bfloat16),
+        jnp.float32,
+    )
     residual_f = gathered.transpose(1, 0, 2).reshape(rows_own, width)
 
     row_mean = jnp.mean(residual_f, axis=-1, keepdims=True)
@@ -167,26 +315,27 @@
     residual_piece = incoming[:, feature_count:]
 
     up_part = jnp.dot(normed, w_up, preferred_element_type=jnp.float32).astype(jnp.bfloat16)
-    up_rows = exchange(up_part.astype(jnp.float32).reshape(n_page, rows_own, -1), "page")
-    hidden_rows = jnp.maximum(ordered_sum(up_rows) + b_up.astype(jnp.float32), 0.0)
-    hidden_rows = hidden_rows.astype(jnp.bfloat16).astype(jnp.float32)
-    hidden = exchange(
-        jnp.broadcast_to(hidden_rows[None], (n_page,) + hidden_rows.shape), "page"
-    ).reshape(samples * new_count, -1)
-
-    projected = jnp.dot(hidden.astype(jnp.bfloat16), w_down, preferred_element_type=jnp.float32)
-    proj_pieces = projected.reshape(samples * new_count, n_blk, piece_width).transpose(1, 0, 2)
-    out_share = ordered_sum(exchange(proj_pieces, "blk"))
-    output = (out_share + residual_piece + b_down.astype(jnp.float32)).astype(jnp.bfloat16)
-
-    score_part = jnp.sum(output.astype(jnp.float32) * w_score.astype(jnp.float32), axis=-1)
-    score_part = score_part.reshape(1, samples * new_count)
-    blk_sum = ordered_sum(
-        exchange(jnp.broadcast_to(score_part[None], (n_blk,) + score_part.shape), "blk")
-    )
-    row_score = ordered_sum(
-        exchange(jnp.broadcast_to(blk_sum[None], (n_page,) + blk_sum.shape), "page")
-    )
+    ff_dev = up_part.shape[1]
+    lane_rows = rows_own * ff_dev // feature_count
+    up_chunks = up_part.reshape(n_page, lane_rows, feature_count)
+    bias_rows = jnp.tile(b_up.astype(jnp.float32).reshape(-1, feature_count), (lane_rows * feature_count // ff_dev, 1))
+    hidden = sum_gather(
+        up_chunks,
+        bias_rows,
+        "page",
+        lambda total, bias: jnp.maximum(total + bias, 0.0),
+        jnp.bfloat16,
+    ).reshape(samples * new_count, ff_dev)
+
+    projected_t = jnp.einsum("rf,fk->kr", hidden, w_down, preferred_element_type=jnp.float32)
+    proj_pieces = projected_t.reshape(n_blk, piece_width, samples * new_count)
+    output_t, row_score = output_and_score(
+        proj_pieces,
+        residual_piece.T,
+        b_down.astype(jnp.float32).reshape(piece_width, 1),
+        w_score.astype(jnp.float32).reshape(piece_width, 1),
+    )
+    output = output_t.T
     return (output.reshape(samples, new_count, piece_width), row_score.reshape(samples, new_count))
 
 

time: 197 us -> 172 us (0.87)
  Pallas kernels: 0 us -> 136 us
  waiting for transfers between devices: 92.1 us -> 0 us
  starting transfers between devices: 70 us -> 0 us
  blocking collectives: 10.5 us -> 0 us
  other arithmetic: 6.19 us -> 13 us
  local copies, waits for them, and re-layouts: 10.5 us -> 14.1 us
    pallas_call x0 -> x5, Pallas kernels: none -> 136 us  [the longest x2 61.9 us: sum_gather(): pl.pallas_call(lambda *refs: sum_gather_kernel(axis, n, finish, *refs), o...]
    all_to_all x8 -> x0, waiting for transfers between devices: 92.1 us -> none  [exchange(): return lax.all_to_all(x, axis, 0, 0, tiled=True)]
    all_to_all x8 -> x0, starting transfers between devices: 70 us -> none  [exchange(): return lax.all_to_all(x, axis, 0, 0, tiled=True)]
    all_to_all x1 -> x0, blocking collectives: 10.5 us -> none  [exchange(): return lax.all_to_all(x, axis, 0, 0, tiled=True)]
    reshape x0 -> x6, local copies, waits for them, and re-layouts: none -> 4.29 us  [the longest x1 1.18 us: body(): hidden = sum_gather(up_chunks, bias_rows, 'page', lambda total, bias: jnp...]
    broadcast_in_dim x4 -> x0, local copies, waits for them, and re-layouts: 2.02 us -> none  [the longest x1 0.71 us: body(): jnp.broadcast_to(res_piece[None], (n_blk,) + res_piece.shape)]
  transfers between devices with their start and end apart: 8 -> 0, of which waited for: 8 -> 0; matrix products, arithmetic and copies ran while one was open for 3% -> 0% of each run, Pallas kernels for 0% -> 0%
where the time goes in v3:
time: 172 us; the launch traced here: 171 us
  Pallas kernels  136 us (79%)
  local copies, waits for them, and re-layouts  14.1 us (8%)
  other arithmetic  13 us (8%)
  matrix products  6.92 us (4%)
    pallas_call x2, Pallas kernels, sum_gather(): pl.pallas_call(lambda *refs: sum_gather_kernel(axis, n, finish, *refs), o...  61.9 us
    pallas_call x2, Pallas kernels, exchange(): pl.pallas_call(lambda *refs: exchange_kernel(axis, n, *refs), out_shape=j...  46.5 us
    pallas_call x1, Pallas kernels, output_and_score(): pl.pallas_call(lambda *refs: output_kernel(n_blk, n_page, *refs), out_sha...  27.2 us

profile of v3, /device:TPU:1, one launch (start us, length us, event | category | flops | bytes accessed | tf_op | source)
XLA Modules:
  0.0 170.7 jit_solution(5361388095208283835)
XLA Ops:
  0.7 0.9 eq.50
  1.8 0.7 select_reduce_fusion.3
  2.8 0.8 compare_and_fusion
  3.6 1.3 select_reduce_fusion
  4.9 1.3 convolution_bitcast_fusion.1
  6.9 0.7 pad_maximum_fusion.refs_0_
  7.6 22.7 %shard_map.176 = f32[16,8,130]{2,1,0:T(8,128)} custom-call(f32[16,8,130]{2,1,0:T(8,128)} %pad_maximum_fusion.refs_0_), custom_call_target="tpu_custom_call" | custom-call | tf_op jit(solution)/shard_map/pallas_call | solution.py:106
  30.3 1.1 fusion.34
  31.6 0.9 select_reduce_fusion.2
  33.4 0.9 subtract_exponential_fusion
  34.5 0.9 slice_multiply_fusion.1
  36.1 0.7 dynamic-slice_convert_fusion
  37.4 0.8 copy.133
  38.2 1.3 dynamic-slice_convert_fusion.1
  39.5 23.5 %shard_map.177 = f32[32,8,224]{2,1,0:T(8,128)} custom-call(f32[32,8,224]{2,1,0:T(8,128)} %bitcast.103, f32[1,224]{1,0:T(1,128)} %bitcast.109), custom_call_target="tpu_custom_call" | custom-call | tf_op jit(solution)/shard_map/pallas_call | solution.py:122
  63.1 1.1 copy.114
  64.3 1.1 reduce_sum.58
  65.4 1.2 multiply_reduce_fusion
  66.9 0.8 maximum_bitcast_fusion.refs_0_
  67.7 23.8 %shard_map.178 = f32[16,8,462]{2,1,0:T(8,128)} custom-call(f32[16,8,462]{2,1,0:T(8,128)} %maximum_bitcast_fusion.refs_0_), custom_call_target="tpu_custom_call" | custom-call | tf_op jit(solution)/shard_map/pallas_call | solution.py:106
  91.6 1.3 convolution_convert_fusion
  92.8 0.9 reshape.424.refs_0_
  94.5 38.4 %shard_map.179 = bf16[16,16,448]{2,1,0:T(8,128)(2,1)} custom-call(bf16[16,16,448]{2,1,0:T(8,128)(2,1)} %reshape.424.refs_0_, f32[16,448]{1,0:T(8,128)} %tile.15.refs_1_), custom_call_target="tpu_custom_call" | custom-call | tf_op jit(solution)/shard_map/pallas_call | solution.py:122
  132.9 1.2 reshape.425
  134.1 1.5 convolution_bitcast_fusion
  135.6 0.7 reshape.426.refs_0_
  136.3 0.9 slice.185
  138.6 0.7 copy.119.refs_3_
  139.3 27.2 %shard_map.180 = (bf16[14,128]{1,0:T(8,128)(2,1)}, f32[1,128]{1,0:T(1,128)}) custom-call(f32[32,14,128]{2,1,0:T(8,128)} %reshape.426.refs_0_, f32[14,128]{1,0:T(8,128)} %bitcast.106, f32[14,1]{1,0:T(8,128)} %copy.118.refs_2_, f32[14,1]{1,0:T(8,128)} %copy.119.refs_3_), custom_call_target="tpu_custom_call" | custom-call | tf_op jit(solution)/shard_map/pallas_call | solution.py:140
  166.6 0.8 copy.120
  167.4 0.7 copy.121
  168.6 1.3 reduce.13
  (66 shorter events, 7.4 us)
Async XLA Ops:
  0.6 35.1 %copy-start = (bf16[128,7168]{1,0:T(8,128)(2,1)S(1)}, bf16[128,7168]{1,0:T(8,128)(2,1)}, u32[]{:S(2)}) copy-start(bf16[128,7168]{1,0:T(8,128)(2,1)} %param.25) | copy-start | bytes 5505028
  3.6 27.9 %copy-start.6 = (s32[64]{0:T(128)S(1)}, s32[64]{0:T(128)}, u32[]{:S(2)}) copy-start(s32[64]{0:T(128)} %param.22) | copy-start | bytes 772
  3.6 28.0 %copy-start.5 = (bf16[4,256,1,256]{3,1,2,0:T(8,128)(2,1)S(1)}, bf16[4,256,1,256]{3,1,2,0:T(8,128)(2,1)}, u32[]{:S(2)}) copy-start(bf16[4,256,1,256]{3,1,2,0:T(8,128)(2,1)} %param.19) | copy-start | bytes 1572868
  63.0 28.5 %copy-start.3 = (bf16[448]{0:T(512)(128)(2,1)S(1)}, bf16[448]{0:T(512)(128)(2,1)}, u32[]{:S(2)}) copy-start(bf16[448]{0:T(512)(128)(2,1)} %param.27) | copy-start | bytes 2692
  63.0 28.5 %copy-start.4 = (bf16[448]{0:T(512)(128)(2,1)S(1)}, bf16[448]{0:T(512)(128)(2,1)}, u32[]{:S(2)}) copy-start(bf16[448]{0:T(512)(128)(2,1)} %param.28) | copy-start | bytes 2692
  63.1 28.5 %copy-start.1 = (bf16[448,896]{1,0:T(8,128)(2,1)S(1)}, bf16[448,896]{1,0:T(8,128)(2,1)}, u32[]{:S(2)}) copy-start(bf16[448,896]{1,0:T(8,128)(2,1)} %param.29) | copy-start | bytes 2408452
  66.6 27.1 %copy-start.2 = (bf16[896]{0:T(1024)(128)(2,1)S(1)}, bf16[896]{0:T(1024)(128)(2,1)}, u32[]{:S(2)}) copy-start(bf16[896]{0:T(1024)(128)(2,1)} %param.30) | copy-start | bytes 5380
  92.8 45.1 %copy-start.7 = (bf16[14]{0:T(256)(128)(2,1)S(1)}, bf16[14]{0:T(256)(128)(2,1)}, u32[]{:S(2)}) copy-start(bf16[14]{0:T(256)(128)(2,1)} %param.32) | copy-start | bytes 88
  92.8 45.8 %copy-start.8 = (bf16[14]{0:T(256)(128)(2,1)S(1)}, bf16[14]{0:T(256)(128)(2,1)}, u32[]{:S(2)}) copy-start(bf16[14]{0:T(256)(128)(2,1)} %param.33) | copy-start | bytes 88

commit v4 on v3

--- a/solution.py
+++ b/solution.py
@@ -88,6 +88,40 @@
     score_ref[...] = slot_sum(page_buf, n_page)
 
 
+def attention_out_kernel(n_page, n_blk, heads, part_ref, tail_ref, w_ref, stream_ref, bias_ref,
+                         o_ref, recv, contrib, red, gat, sems):
+    me_page = lax.axis_index("page")
+    me_blk = lax.axis_index("blk")
+    recv[me_page] = part_ref[me_page]
+    enter([("page", n_page), ("blk", n_blk)])
+    send_round("page", n_page, lambda peer: part_ref.at[peer], recv, sems.at[0], sems.at[1])
+    hd = w_ref.shape[1] // heads
+    tail = tail_ref[...]
+    highest = tail[:, hd:2 * hd]
+    for j in range(n_page):
+        highest = jnp.maximum(highest, recv[j][:, hd:2 * hd])
+    scale = jnp.exp(tail[:, hd:2 * hd] - highest)
+    weight_sum = tail[:, 2 * hd:] * scale
+    weighted = tail[:, :hd] * scale
+    for j in range(n_page):
+        part = recv[j]
+        scale = jnp.exp(part[:, hd:2 * hd] - highest)
+        weight_sum = weight_sum + part[:, 2 * hd:] * scale
+        weighted = weighted + part[:, :hd] * scale
+    attention = (weighted / weight_sum).astype(jnp.bfloat16)
+    rows = attention.shape[0] // heads
+    if heads > 1:
+        attention = jnp.concatenate([attention[h * rows:(h + 1) * rows] for h in range(heads)], axis=1)
+    for j in range(n_blk):
+        contrib[j] = jnp.dot(attention, w_ref[j], preferred_element_type=jnp.float32)
+    red[me_blk] = contrib[me_blk] + stream_ref[...]
+    send_round("blk", n_blk, lambda peer: contrib.at[peer], red, sems.at[2], sems.at[3])
+    total = slot_sum(red, n_blk) + bias_ref[...]
+    gat[me_blk] = total.astype(jnp.bfloat16).astype(jnp.float32)
+    send_round("blk", n_blk, lambda peer: gat.at[me_blk], gat, sems.at[4], sems.at[5])
+    o_ref[...] = gat[...]
+
+
 CALL_IDS = {}
 
 
@@ -131,6 +165,27 @@
         ],
         compiler_params=pltpu.CompilerParams(collective_id=next_id(axis), has_side_effects=True),
     )(x, extra)
+
+
+def attention_out(part, tail, w_chunks, stream, bias):
+    n_page = lax.axis_size("page")
+    n_blk = lax.axis_size("blk")
+    heads = w_chunks.shape[1] // (part.shape[2] // 3)
+    chunk = (stream.shape[0], w_chunks.shape[2])
+    return pl.pallas_call(
+        lambda *refs: attention_out_kernel(n_page, n_blk, heads, *refs),
+        out_shape=jax.ShapeDtypeStruct((n_blk,) + chunk, jnp.float32),
+        in_specs=vmem_specs(5),
+        out_specs=vmem_specs(1)[0],
+        scratch_shapes=[
+            pltpu.VMEM(part.shape, jnp.float32),
+            pltpu.VMEM((n_blk,) + chunk, jnp.float32),
+            pltpu.VMEM((n_blk,) + chunk, jnp.float32),
+            pltpu.VMEM((n_blk,) + chunk, jnp.float32),
+            pltpu.SemaphoreType.DMA((6, max(n_blk, n_page))),
+        ],
+        compiler_params=pltpu.CompilerParams(collective_id=next_id("both"), has_side_effects=True),
+    )(part, tail, w_chunks, stream, bias)
 
 
 def output_and_score(x, res, bias, score_w):
@@ -253,46 +308,29 @@
         "snht,sthd->snhd", weights_t, tail_kv[..., head_dim:], preferred_element_type=jnp.float32
     )
 
-    packed = jnp.concatenate([mixed_p, high_p[..., None], sum_p[..., None]], axis=-1)
-    packed = packed.reshape(n_page, rows_own * heads_dev, head_dim + 2)
-    got = exchange(packed, "page")
-    high_all = got[..., head_dim]
-    sum_all = got[..., head_dim + 1]
-    mixed_all = got[..., :head_dim]
-    high_t = high_t.reshape(rows_own * heads_dev)
-    sum_t = sum_t.reshape(rows_own * heads_dev)
-    mixed_t = mixed_t.reshape(rows_own * heads_dev, head_dim)
-    highest = jnp.maximum(jnp.max(high_all, axis=0), high_t)
-    scale_all = jnp.exp(high_all - highest[None, :])
-    scale_t = jnp.exp(high_t - highest)
-    weight_sum = ordered_sum(sum_all * scale_all) + sum_t * scale_t
-    weighted = ordered_sum(mixed_all * scale_all[..., None]) + mixed_t * scale_t[..., None]
-    attention = (
-        (weighted / weight_sum[..., None])
-        .astype(jnp.bfloat16)
-        .reshape(rows_own, heads_dev * head_dim)
-    )
-
-    contrib = jnp.dot(attention, w_out, preferred_element_type=jnp.float32)
+    def pack(mixed, high, total):
+        lanes = mixed.shape[-1]
+        parts = [mixed, jnp.broadcast_to(high[..., None], mixed.shape), jnp.broadcast_to(total[..., None], mixed.shape)]
+        whole = jnp.concatenate(parts, axis=-1)
+        whole = whole.reshape(-1, own_count, new_count, heads_dev, 3 * lanes).transpose(0, 3, 1, 2, 4)
+        return whole.reshape(-1, heads_dev * rows_own, 3 * lanes)
+
     slice_width = stream_in.shape[2]
     column = blk_pos * slice_width
+    n_blk = width // slice_width
     own_stream = (
         lax.dynamic_slice_in_dim(stream_in, first_row, own_count, 0)
         .reshape(rows_own, slice_width)
         .astype(jnp.float32)
     )
-    contrib = lax.dynamic_update_slice_in_dim(
-        contrib, lax.dynamic_slice_in_dim(contrib, column, slice_width, 1) + own_stream, column, 1
-    )
-    n_blk = width // slice_width
-    pieces = contrib.reshape(rows_own, n_blk, slice_width).transpose(1, 0, 2)
     own_bias = lax.dynamic_slice_in_dim(b_out, column, slice_width, 0).astype(jnp.float32)
-    gathered = sum_gather(
-        pieces,
+    w_chunks = w_out.reshape(heads_dev * head_dim, n_blk, slice_width).transpose(1, 0, 2)
+    gathered = attention_out(
+        pack(mixed_p, high_p, sum_p),
+        pack(mixed_t, high_t, sum_t)[0],
+        w_chunks,
+        own_stream,
         own_bias.reshape(1, slice_width),
-        "blk",
-        lambda total, bias: (total + bias).astype(jnp.bfloat16),
-        jnp.float32,
     )
     residual_f = gathered.transpose(1, 0, 2).reshape(rows_own, width)
 

time: 172 us -> 171 us (level)
  local copies, waits for them, and re-layouts: 14.1 us -> 20.5 us
  other arithmetic: 13 us -> 8.96 us
    pallas_call x0 -> x1, Pallas kernels: none -> 46.2 us  [attention_out(): pl.pallas_call(lambda *refs: attention_out_kernel(n_page, n_blk, heads, *...]
    pallas_call x2 -> x1, Pallas kernels: 61.9 us -> 34.8 us  [sum_gather(): pl.pallas_call(lambda *refs: sum_gather_kernel(axis, n, finish, *refs), o...]
    pallas_call x2 -> x1, Pallas kernels: 46.5 us -> 23.9 us  [exchange(): pl.pallas_call(lambda *refs: exchange_kernel(axis, n, *refs), out_shape=j...]
    unnamed x21 -> x22, local copies, waits for them, and re-layouts: 2.08 us -> 5.36 us
    pallas_call x1, Pallas kernels: 27.2 us -> 29.6 us  [output_and_score(): pl.pallas_call(lambda *refs: output_kernel(n_blk, n_page, *refs), out_sha...]
    reshape x4 -> x1, local copies, waits for them, and re-layouts: 1.2 us -> 3.09 us  [body(): w_out.reshape(heads_dev * head_dim, n_blk, slice_width).transpose(1, 0, 2)]
where the time goes in v4:
time: 171 us; the launch traced here: 170 us
  Pallas kernels  135 us (79%)
  local copies, waits for them, and re-layouts  20.5 us (12%)
  other arithmetic  8.96 us (5%)
  matrix products  5.39 us (3%)
    pallas_call x1, Pallas kernels, attention_out(): pl.pallas_call(lambda *refs: attention_out_kernel(n_page, n_blk, heads, *...  46.2 us
    pallas_call x1, Pallas kernels, sum_gather(): pl.pallas_call(lambda *refs: sum_gather_kernel(axis, n, finish, *refs), o...  34.8 us
    pallas_call x1, Pallas kernels, output_and_score(): pl.pallas_call(lambda *refs: output_kernel(n_blk, n_page, *refs), out_sha...  29.6 us
    pallas_call x1, Pallas kernels, exchange(): pl.pallas_call(lambda *refs: exchange_kernel(axis, n, *refs), out_shape=j...  23.9 us
    unnamed x22, local copies, waits for them, and re-layouts  5.36 us

profile of v4, /device:TPU:1, one launch (start us, length us, event | category | flops | bytes accessed | tf_op | source)
XLA Modules:
  0.0 170.4 jit_solution(1694235797142367986)
XLA Ops:
  0.6 0.8 eq.50
  1.8 0.7 select_reduce_fusion.3
  2.7 0.8 compare_and_fusion
  3.5 1.3 select_reduce_fusion
  5.3 1.3 convolution_bitcast_fusion.1
  6.7 0.8 reshape_transpose_reshape.3.refs_0_
  7.7 0.9 select_reduce_fusion.2
  9.8 3.3 %copy.47 = bf16[128,7168]{0,1:T(8,128)(2,1)S(1)} copy(bf16[128,7168]{1,0:T(8,128)(2,1)} %param.25) | data formatting | bytes 3670016 | tf_op args[8]
  13.1 3.1 %copy.48 = bf16[128,32,224]{2,0,1:T(8,128)(2,1)} copy(bf16[128,32,224]{0,2,1:T(8,128)(2,1)S(1)} %bitcast.82) | data formatting | bytes 3670016 | tf_op jit(solution)/shard_map/reshape | solution.py:327
  16.2 0.7 dynamic-slice_convert_fusion
  17.5 1.3 dynamic-slice_convert_fusion.1
  18.8 46.2 %shard_map.176 = f32[32,8,224]{2,1,0:T(8,128)} custom-call(f32[16,8,384]{2,1,0:T(8,128)} %reshape_transpose_reshape.3.refs_0_, f32[8,384]{1,0:T(8,128)} %squeeze_reshape_transpose_reshape.3.refs_1_, bf16[32,128,224]{2,1,0:T(8,128)(2,1)} %bitcast.81, f32[8,224]{1,0:T(8,128)} %reshape.296.refs_3_, f32[1,224]{1,0:T(1,128)} %bitcast.88), custom_call_target="tpu_custom_call" | custom-call | tf_op jit(solution)/shard_map/pallas_call | solution.py:175
  65.0 1.1 reduce_sum.58
  66.2 1.2 multiply_reduce_fusion
  67.4 1.0 copy.49
  68.8 0.8 maximum_bitcast_fusion.refs_0_
  69.6 23.9 %shard_map.177 = f32[16,8,462]{2,1,0:T(8,128)} custom-call(f32[16,8,462]{2,1,0:T(8,128)} %maximum_bitcast_fusion.refs_0_), custom_call_target="tpu_custom_call" | custom-call | tf_op jit(solution)/shard_map/pallas_call | solution.py:140
  93.6 1.3 convolution_convert_fusion
  94.9 0.9 reshape.287.refs_0_
  95.9 0.6 tile.15.refs_1_
  96.5 34.8 %shard_map.178 = bf16[16,16,448]{2,1,0:T(8,128)(2,1)} custom-call(bf16[16,16,448]{2,1,0:T(8,128)(2,1)} %reshape.287.refs_0_, f32[16,448]{1,0:T(8,128)} %tile.15.refs_1_), custom_call_target="tpu_custom_call" | custom-call | tf_op jit(solution)/shard_map/pallas_call | solution.py:156
  131.4 1.2 reshape.288
  133.0 0.7 reshape.289.refs_0_
  133.7 0.9 slice.29
  134.6 0.7 copy.58
  135.3 0.7 copy.53.refs_2_
  136.0 0.7 copy.54.refs_3_
  136.7 29.6 %shard_map.179 = (bf16[14,128]{1,0:T(8,128)(2,1)}, f32[1,128]{1,0:T(1,128)}) custom-call(f32[32,14,128]{2,1,0:T(8,128)} %reshape.289.refs_0_, f32[14,128]{1,0:T(8,128)} %bitcast.87, f32[14,1]{1,0:T(8,128)} %copy.53.refs_2_, f32[14,1]{1,0:T(8,128)} %copy.54.refs_3_), custom_call_target="tpu_custom_call" | custom-call | tf_op jit(solution)/shard_map/pallas_call | solution.py:195
  166.3 0.8 copy.55
  167.1 0.7 copy.56
  168.3 1.3 reduce.10
  169.7 0.6 copy.57
  (53 shorter events, 4.6 us)
Async XLA Ops:
  0.6 93.0 %copy-start = (bf16[448,896]{1,0:T(8,128)(2,1)S(1)}, bf16[448,896]{1,0:T(8,128)(2,1)}, u32[]{:S(2)}) copy-start(bf16[448,896]{1,0:T(8,128)(2,1)} %param.29) | copy-start | bytes 2408452
  3.5 4.0 %copy-start.6 = (s32[64]{0:T(128)S(1)}, s32[64]{0:T(128)}, u32[]{:S(2)}) copy-start(s32[64]{0:T(128)} %param.22) | copy-start | bytes 772
  3.5 4.2 %copy-start.5 = (bf16[4,256,1,256]{3,1,2,0:T(8,128)(2,1)S(1)}, bf16[4,256,1,256]{3,1,2,0:T(8,128)(2,1)}, u32[]{:S(2)}) copy-start(bf16[4,256,1,256]{3,1,2,0:T(8,128)(2,1)} %param.19) | copy-start | bytes 1572868
  65.0 28.5 %copy-start.3 = (bf16[448]{0:T(512)(128)(2,1)S(1)}, bf16[448]{0:T(512)(128)(2,1)}, u32[]{:S(2)}) copy-start(bf16[448]{0:T(512)(128)(2,1)} %param.28) | copy-start | bytes 2692
  65.0 28.5 %copy-start.4 = (bf16[448]{0:T(512)(128)(2,1)S(1)}, bf16[448]{0:T(512)(128)(2,1)}, u32[]{:S(2)}) copy-start(bf16[448]{0:T(512)(128)(2,1)} %param.27) | copy-start | bytes 2692
  68.6 27.2 %copy-start.2 = (bf16[896]{0:T(1024)(128)(2,1)S(1)}, bf16[896]{0:T(1024)(128)(2,1)}, u32[]{:S(2)}) copy-start(bf16[896]{0:T(1024)(128)(2,1)} %param.30) | copy-start | bytes 5380
  69.6 62.9 %copy-start.1 = (bf16[896,448]{0,1:T(8,128)(2,1)S(1)}, bf16[896,448]{0,1:T(8,128)(2,1)}, u32[]{:S(2)}) copy-start(bf16[896,448]{0,1:T(8,128)(2,1)} %param.31) | copy-start | bytes 2408452
  94.9 40.4 %copy-start.7 = (bf16[14]{0:T(256)(128)(2,1)S(1)}, bf16[14]{0:T(256)(128)(2,1)}, u32[]{:S(2)}) copy-start(bf16[14]{0:T(256)(128)(2,1)} %param.32) | copy-start | bytes 88
  94.9 41.1 %copy-start.8 = (bf16[14]{0:T(256)(128)(2,1)S(1)}, bf16[14]{0:T(256)(128)(2,1)}, u32[]{:S(2)}) copy-start(bf16[14]{0:T(256)(128)(2,1)} %param.33) | copy-start | bytes 88

commit v5 on v4

--- a/solution.py
+++ b/solution.py
@@ -89,13 +89,13 @@
 
 
 def attention_out_kernel(n_page, n_blk, heads, part_ref, tail_ref, w_ref, stream_ref, bias_ref,
-                         o_ref, recv, contrib, red, gat, sems):
+                         res_ref, scaled_ref, recv, full, red, gat, sems):
     me_page = lax.axis_index("page")
     me_blk = lax.axis_index("blk")
     recv[me_page] = part_ref[me_page]
     enter([("page", n_page), ("blk", n_blk)])
     send_round("page", n_page, lambda peer: part_ref.at[peer], recv, sems.at[0], sems.at[1])
-    hd = w_ref.shape[1] // heads
+    hd = w_ref.shape[0] // heads
     tail = tail_ref[...]
     highest = tail[:, hd:2 * hd]
     for j in range(n_page):
@@ -112,15 +112,92 @@
     rows = attention.shape[0] // heads
     if heads > 1:
         attention = jnp.concatenate([attention[h * rows:(h + 1) * rows] for h in range(heads)], axis=1)
-    for j in range(n_blk):
-        contrib[j] = jnp.dot(attention, w_ref[j], preferred_element_type=jnp.float32)
-    red[me_blk] = contrib[me_blk] + stream_ref[...]
-    send_round("blk", n_blk, lambda peer: contrib.at[peer], red, sems.at[2], sems.at[3])
-    total = slot_sum(red, n_blk) + bias_ref[...]
-    gat[me_blk] = total.astype(jnp.bfloat16).astype(jnp.float32)
-    send_round("blk", n_blk, lambda peer: gat.at[me_blk], gat, sems.at[4], sems.at[5])
-    o_ref[...] = gat[...]
-
+    full[...] = jnp.dot(attention, w_ref[...], preferred_element_type=jnp.float32) + stream_ref[...]
+    lanes = red.shape[2]
+    n_chunk = gat.shape[0]
+
+    def own(ref):
+        return ref[:, pl.ds(pl.multiple_of(me_blk * lanes, lanes), lanes)]
+
+    def scatter_copy(t):
+        return pltpu.make_async_remote_copy(
+            src_ref=full.at[:, pl.ds(t * lanes, lanes)],
+            dst_ref=red.at[me_blk],
+            send_sem=sems.at[2, t],
+            recv_sem=sems.at[3, me_blk],
+            device_id=device_on("blk", t),
+            device_id_type=MESH_ID,
+        )
+
+    def scatter_arrival(s):
+        return pltpu.make_async_remote_copy(
+            src_ref=full.at[:, pl.ds(0, lanes)],
+            dst_ref=red.at[s],
+            send_sem=sems.at[2, 0],
+            recv_sem=sems.at[3, s],
+            device_id=device_on("blk", s),
+            device_id_type=MESH_ID,
+        )
+
+    def gather_copy(k):
+        return pltpu.make_async_remote_copy(
+            src_ref=gat.at[me_blk],
+            dst_ref=gat.at[me_blk],
+            send_sem=sems.at[4, k],
+            recv_sem=sems.at[5, me_blk],
+            device_id=device_on("blk", lax.rem(me_blk + k, n_blk)),
+            device_id_type=MESH_ID,
+        )
+
+    def gather_arrival(s):
+        return pltpu.make_async_remote_copy(
+            src_ref=gat.at[s],
+            dst_ref=gat.at[s],
+            send_sem=sems.at[4, 0],
+            recv_sem=sems.at[5, s],
+            device_id=device_on("blk", s),
+            device_id_type=MESH_ID,
+        )
+
+    for t in range(n_chunk):
+        @pl.when(me_blk != t)
+        def _():
+            scatter_copy(t).start()
+
+    @pl.when(me_blk < n_chunk)
+    def _():
+        red[me_blk] = own(full)
+        for s in range(n_blk):
+            @pl.when(me_blk != s)
+            def _():
+                scatter_arrival(s).wait_recv()
+        total = slot_sum(red, n_blk) + own(bias_ref)
+        gat[me_blk] = total.astype(jnp.bfloat16).astype(jnp.float32)
+        for k in range(1, n_blk):
+            gather_copy(k).start()
+
+    for t in range(n_chunk):
+        @pl.when(me_blk != t)
+        def _():
+            scatter_copy(t).wait_send()
+
+    @pl.when(me_blk < n_chunk)
+    def _():
+        for k in range(1, n_blk):
+            gather_copy(k).wait_send()
+
+    for s in range(n_chunk):
+        @pl.when(me_blk != s)
+        def _():
+            gather_arrival(s).wait_recv()
+
+    for t in range(n_chunk):
+        res_ref[:, t * lanes:(t + 1) * lanes] = gat[t]
+    residual = res_ref[...]
+    row_mean = jnp.mean(residual, axis=-1, keepdims=True)
+    centred = residual - row_mean
+    inverse_std = lax.rsqrt(jnp.mean(centred * centred, axis=-1, keepdims=True) + 1e-05)
+    scaled_ref[...] = centred * inverse_std
 
 CALL_IDS = {}
 
@@ -167,25 +244,31 @@
     )(x, extra)
 
 
-def attention_out(part, tail, w_chunks, stream, bias):
+def attention_out(part, tail, w_out, stream, bias):
     n_page = lax.axis_size("page")
     n_blk = lax.axis_size("blk")
-    heads = w_chunks.shape[1] // (part.shape[2] // 3)
-    chunk = (stream.shape[0], w_chunks.shape[2])
+    rows, width = stream.shape
+    heads = w_out.shape[0] // (part.shape[2] // 3)
+    lanes = 128 * (-(-width // (128 * n_blk)))
+    n_chunk = width // lanes
+    assert n_chunk * lanes == width
     return pl.pallas_call(
         lambda *refs: attention_out_kernel(n_page, n_blk, heads, *refs),
-        out_shape=jax.ShapeDtypeStruct((n_blk,) + chunk, jnp.float32),
+        out_shape=(
+            jax.ShapeDtypeStruct((rows, width), jnp.float32),
+            jax.ShapeDtypeStruct((rows, width), jnp.float32),
+        ),
         in_specs=vmem_specs(5),
-        out_specs=vmem_specs(1)[0],
+        out_specs=tuple(vmem_specs(2)),
         scratch_shapes=[
             pltpu.VMEM(part.shape, jnp.float32),
-            pltpu.VMEM((n_blk,) + chunk, jnp.float32),
-            pltpu.VMEM((n_blk,) + chunk, jnp.float32),
-            pltpu.VMEM((n_blk,) + chunk, jnp.float32),
+            pltpu.VMEM((rows, width), jnp.float32),
+            pltpu.VMEM((n_blk, rows, lanes), jnp.float32),
+            pltpu.VMEM((n_chunk, rows, lanes), jnp.float32),
             pltpu.SemaphoreType.DMA((6, max(n_blk, n_page))),
         ],
         compiler_params=pltpu.CompilerParams(collective_id=next_id("both"), has_side_effects=True),
-    )(part, tail, w_chunks, stream, bias)
+    )(part, tail, w_out, stream, bias)
 
 
 def output_and_score(x, res, bias, score_w):
@@ -323,21 +406,16 @@
         .reshape(rows_own, slice_width)
         .astype(jnp.float32)
     )
-    own_bias = lax.dynamic_slice_in_dim(b_out, column, slice_width, 0).astype(jnp.float32)
-    w_chunks = w_out.reshape(heads_dev * head_dim, n_blk, slice_width).transpose(1, 0, 2)
-    gathered = attention_out(
+    stream_full = lax.dynamic_update_slice_in_dim(
+        jnp.zeros((rows_own, width), jnp.float32), own_stream, column, 1
+    )
+    residual_f, scaled = attention_out(
         pack(mixed_p, high_p, sum_p),
         pack(mixed_t, high_t, sum_t)[0],
-        w_chunks,
-        own_stream,
-        own_bias.reshape(1, slice_width),
-    )
-    residual_f = gathered.transpose(1, 0, 2).reshape(rows_own, width)
-
-    row_mean = jnp.mean(residual_f, axis=-1, keepdims=True)
-    centred = residual_f - row_mean
-    inverse_std = lax.rsqrt(jnp.mean(centred * centred, axis=-1, keepdims=True) + 1e-05)
-    scaled = centred * inverse_std
+        w_out,
+        stream_full,
+        b_out.astype(jnp.float32).reshape(1, width),
+    )
 
     feature_count = ln_gain.shape[0]
     piece_width = b_down.shape[0]

time: 171 us -> 164 us (0.959)
  local copies, waits for them, and re-layouts: 20.5 us -> 15.8 us
  other arithmetic: 8.96 us -> 5.76 us
    unnamed x22, local copies, waits for them, and re-layouts: 5.36 us -> 2.14 us
    reduce_sum x2 -> x0, other arithmetic: 2.34 us -> none  [the longest x1 1.2 us: body(): jnp.mean(centred * centred, axis=-1, keepdims=True) + 1e-05]
where the time goes in v5:
time: 164 us; the launch traced here: 163 us
  Pallas kernels  134 us (82%)
  local copies, waits for them, and re-layouts  15.8 us (10%)
  matrix products  6.56 us (4%)
  other arithmetic  5.76 us (4%)
    pallas_call x1, Pallas kernels, attention_out(): pl.pallas_call(lambda *refs: attention_out_kernel(n_page, n_blk, heads, *...  46.2 us
    pallas_call x1, Pallas kernels, sum_gather(): pl.pallas_call(lambda *refs: sum_gather_kernel(axis, n, finish, *refs), o...  35.2 us
    pallas_call x1, Pallas kernels, output_and_score(): pl.pallas_call(lambda *refs: output_kernel(n_blk, n_page, *refs), out_sha...  28.6 us
    pallas_call x1, Pallas kernels, exchange(): pl.pallas_call(lambda *refs: exchange_kernel(axis, n, *refs), out_shape=j...  23.9 us

profile of v5, /device:TPU:1, one launch (start us, length us, event | category | flops | bytes accessed | tf_op | source)
XLA Modules:
  0.0 162.9 jit_solution(5812135447135075575)
XLA Ops:
  0.7 0.8 dynamic_slice.12
  1.5 1.2 select_reduce_fusion.2
  2.7 1.2 convolution_bitcast_fusion.2
  4.2 0.6 squeeze_reshape_transpose_reshape.3.refs_1_
  4.9 0.8 eq.50
  5.8 0.7 select_reduce_fusion.3
  6.9 0.8 compare_and_fusion
  7.7 1.3 select_reduce_fusion
  8.9 1.3 convolution_bitcast_fusion.1
  10.8 0.8 reshape_transpose_reshape.3.refs_0_
  11.6 0.7 dynamic-slice_convert_fusion
  12.7 0.6 reshape.268
  13.4 46.2 %shard_map.176 = (f32[8,7168]{1,0:T(8,128)}, f32[8,7168]{1,0:T(8,128)}) custom-call(f32[16,8,384]{2,1,0:T(8,128)} %reshape_transpose_reshape.3.refs_0_, f32[8,384]{1,0:T(8,128)} %squeeze_reshape_transpose_reshape.3.refs_1_, bf16[128,7168]{1,0:T(8,128)(2,1)} %refs_2_.1, f32[8,7168]{1,0:T(8,128)} %copy-done.1, f32[1,7168]{1,0:T(1,128)} %bitcast.80), custom_call_target="tpu_custom_call" | custom-call | tf_op jit(solution)/shard_map/pallas_call | solution.py:255
  59.6 1.1 reshape.255
  60.9 1.1 reshape.256
  62.1 0.8 maximum_bitcast_fusion.refs_0_
  62.8 23.9 %shard_map.177 = f32[16,8,462]{2,1,0:T(8,128)} custom-call(f32[16,8,462]{2,1,0:T(8,128)} %maximum_bitcast_fusion.refs_0_), custom_call_target="tpu_custom_call" | custom-call | tf_op jit(solution)/shard_map/pallas_call | solution.py:217
  86.8 1.3 convolution_convert_fusion
  88.1 0.9 reshape.258.refs_0_
  89.1 0.6 tile.15.refs_1_
  89.7 35.2 %shard_map.178 = bf16[16,16,448]{2,1,0:T(8,128)(2,1)} custom-call(bf16[16,16,448]{2,1,0:T(8,128)(2,1)} %reshape.258.refs_0_, f32[16,448]{1,0:T(8,128)} %tile.15.refs_1_), custom_call_target="tpu_custom_call" | custom-call | tf_op jit(solution)/shard_map/pallas_call | solution.py:233
  124.9 1.2 reshape.259
  126.5 0.7 reshape.260.refs_0_
  127.2 0.9 slice.29
  128.1 0.7 copy.53
  128.8 0.7 copy.47.refs_2_
  129.5 0.7 copy.48.refs_3_
  130.2 28.6 %shard_map.179 = (bf16[14,128]{1,0:T(8,128)(2,1)}, f32[1,128]{1,0:T(1,128)}) custom-call(f32[32,14,128]{2,1,0:T(8,128)} %reshape.260.refs_0_, f32[14,128]{1,0:T(8,128)} %bitcast.81, f32[14,1]{1,0:T(8,128)} %copy.47.refs_2_, f32[14,1]{1,0:T(8,128)} %copy.48.refs_3_), custom_call_target="tpu_custom_call" | custom-call | tf_op jit(solution)/shard_map/pallas_call | solution.py:278
  158.8 0.8 copy.49
  159.6 0.7 copy.50
  160.8 1.3 reduce.7
  162.2 0.6 copy.51
  (50 shorter events, 3.4 us)
Async XLA Ops:
  0.6 86.1 %copy-start = (bf16[448,896]{1,0:T(8,128)(2,1)S(1)}, bf16[448,896]{1,0:T(8,128)(2,1)}, u32[]{:S(2)}) copy-start(bf16[448,896]{1,0:T(8,128)(2,1)} %param.29) | copy-start | bytes 2408452
  8.9 3.8 %copy-start.3 = (bf16[7168]{0:T(1024)(128)(2,1)S(1)}, bf16[7168]{0:T(1024)(128)(2,1)}, u32[]{:S(2)}) copy-start(bf16[7168]{0:T(1024)(128)(2,1)} %param.26) | copy-start | bytes 43012
  12.7 0.7 copy-start.1
  59.6 27.1 %copy-start.5 = (bf16[448]{0:T(512)(128)(2,1)S(1)}, bf16[448]{0:T(512)(128)(2,1)}, u32[]{:S(2)}) copy-start(bf16[448]{0:T(512)(128)(2,1)} %param.27) | copy-start | bytes 2692
  59.6 27.1 %copy-start.6 = (bf16[448]{0:T(512)(128)(2,1)S(1)}, bf16[448]{0:T(512)(128)(2,1)}, u32[]{:S(2)}) copy-start(bf16[448]{0:T(512)(128)(2,1)} %param.28) | copy-start | bytes 2692
  60.8 28.1 %copy-start.4 = (bf16[896]{0:T(1024)(128)(2,1)S(1)}, bf16[896]{0:T(1024)(128)(2,1)}, u32[]{:S(2)}) copy-start(bf16[896]{0:T(1024)(128)(2,1)} %param.30) | copy-start | bytes 5380
  62.8 63.2 %copy-start.2 = (bf16[896,448]{0,1:T(8,128)(2,1)S(1)}, bf16[896,448]{0,1:T(8,128)(2,1)}, u32[]{:S(2)}) copy-start(bf16[896,448]{0,1:T(8,128)(2,1)} %param.31) | copy-start | bytes 2408452
  88.0 40.8 %copy-start.7 = (bf16[14]{0:T(256)(128)(2,1)S(1)}, bf16[14]{0:T(256)(128)(2,1)}, u32[]{:S(2)}) copy-start(bf16[14]{0:T(256)(128)(2,1)} %param.32) | copy-start | bytes 88
  88.0 41.4 %copy-start.8 = (bf16[14]{0:T(256)(128)(2,1)S(1)}, bf16[14]{0:T(256)(128)(2,1)}, u32[]{:S(2)}) copy-start(bf16[14]{0:T(256)(128)(2,1)} %param.33) | copy-start | bytes 88

commit v6 on v5

--- a/solution.py
+++ b/solution.py
@@ -199,6 +199,103 @@
     inverse_std = lax.rsqrt(jnp.mean(centred * centred, axis=-1, keepdims=True) + 1e-05)
     scaled_ref[...] = centred * inverse_std
 
+def up_kernel(n_page, x_ref, gain_ref, bias_ref, w_ref, b_up_ref, recv_out_ref, hid_out_ref,
+              recv, up_s, red, hid_ref, sems):
+    me = lax.axis_index("page")
+    recv[me] = x_ref[me]
+    enter([("page", n_page)])
+    send_round("page", n_page, lambda peer: x_ref.at[peer], recv, sems.at[0], sems.at[1])
+    recv_out_ref[...] = recv[...]
+    features = gain_ref.shape[1]
+    rows = recv.shape[1]
+    scaled = jnp.concatenate([recv[j][:, :features] for j in range(n_page)], axis=0)
+    normed = (scaled * gain_ref[...] + bias_ref[...]).astype(jnp.bfloat16)
+    up_s[...] = jnp.dot(normed, w_ref[...], preferred_element_type=jnp.float32).astype(jnp.bfloat16)
+    block = red.shape[1]
+    n_recv = up_s.shape[0] // block
+
+    def rows_of(k):
+        return pl.ds(k * block, block)
+
+    def scatter_copy(k):
+        return pltpu.make_async_remote_copy(
+            src_ref=up_s.at[rows_of(k)],
+            dst_ref=red.at[me],
+            send_sem=sems.at[2, k],
+            recv_sem=sems.at[3, me],
+            device_id=device_on("page", 2 * k),
+            device_id_type=MESH_ID,
+        )
+
+    def scatter_arrival(s):
+        return pltpu.make_async_remote_copy(
+            src_ref=up_s.at[rows_of(0)],
+            dst_ref=red.at[s],
+            send_sem=sems.at[2, 0],
+            recv_sem=sems.at[3, s],
+            device_id=device_on("page", s),
+            device_id_type=MESH_ID,
+        )
+
+    def gather_copy(k, mine):
+        return pltpu.make_async_remote_copy(
+            src_ref=hid_ref.at[rows_of(mine)],
+            dst_ref=hid_ref.at[rows_of(mine)],
+            send_sem=sems.at[4, k],
+            recv_sem=sems.at[5, mine],
+            device_id=device_on("page", lax.rem(me + k, n_page)),
+            device_id_type=MESH_ID,
+        )
+
+    def gather_arrival(k):
+        return pltpu.make_async_remote_copy(
+            src_ref=hid_ref.at[rows_of(k)],
+            dst_ref=hid_ref.at[rows_of(k)],
+            send_sem=sems.at[4, 0],
+            recv_sem=sems.at[5, k],
+            device_id=device_on("page", 2 * k),
+            device_id_type=MESH_ID,
+        )
+
+    for k in range(n_recv):
+        @pl.when(me != 2 * k)
+        def _():
+            scatter_copy(k).start()
+
+    mine = me // 2
+
+    @pl.when(me % 2 == 0)
+    def _():
+        red[me] = up_s[pl.ds(pl.multiple_of(mine * block, block), block)]
+        for s in range(n_page):
+            @pl.when(me != s)
+            def _():
+                scatter_arrival(s).wait_recv()
+        total = slot_sum(red, n_page) + b_up_ref[...]
+        hid_ref[pl.ds(pl.multiple_of(mine * block, block), block)] = jnp.maximum(total, 0.0).astype(
+            jnp.bfloat16
+        )
+        for k in range(1, n_page):
+            gather_copy(k, mine).start()
+
+    for k in range(n_recv):
+        @pl.when(me != 2 * k)
+        def _():
+            scatter_copy(k).wait_send()
+
+    @pl.when(me % 2 == 0)
+    def _():
+        for k in range(1, n_page):
+            gather_copy(k, mine).wait_send()
+
+    for k in range(n_recv):
+        @pl.when(me != 2 * k)
+        def _():
+            gather_arrival(k).wait_recv()
+
+    hid_out_ref[...] = hid_ref[...]
+
+
 CALL_IDS = {}
 
 
@@ -269,6 +366,30 @@
         ],
         compiler_params=pltpu.CompilerParams(collective_id=next_id("both"), has_side_effects=True),
     )(part, tail, w_out, stream, bias)
+
+
+def up_project(outgoing, gain, bias, w_up, b_up):
+    n_page = lax.axis_size("page")
+    rows = outgoing.shape[0] * outgoing.shape[1]
+    ff = w_up.shape[1]
+    block = 2 * rows // n_page
+    return pl.pallas_call(
+        lambda *refs: up_kernel(n_page, *refs),
+        out_shape=(
+            jax.ShapeDtypeStruct(outgoing.shape, jnp.float32),
+            jax.ShapeDtypeStruct((rows, ff), jnp.bfloat16),
+        ),
+        in_specs=vmem_specs(5),
+        out_specs=tuple(vmem_specs(2)),
+        scratch_shapes=[
+            pltpu.VMEM(outgoing.shape, jnp.float32),
+            pltpu.VMEM((rows, ff), jnp.bfloat16),
+            pltpu.VMEM((n_page, block, ff), jnp.bfloat16),
+            pltpu.VMEM((rows, ff), jnp.bfloat16),
+            pltpu.SemaphoreType.DMA((6, n_page)),
+        ],
+        compiler_params=pltpu.CompilerParams(collective_id=next_id("page"), has_side_effects=True),
+    )(outgoing, gain, bias, w_up, b_up)
 
 
 def output_and_score(x, res, bias, score_w):
@@ -424,24 +545,14 @@
         residual_f.reshape(rows_own, n_page, feature_count), blk_pos * piece_width, piece_width, 2
     )
     outgoing = jnp.concatenate([scaled3, res3], axis=-1).transpose(1, 0, 2)
-    incoming = exchange(outgoing, "page").reshape(samples * new_count, feature_count + piece_width)
-    normed = (
-        incoming[:, :feature_count] * ln_gain.astype(jnp.float32) + ln_bias.astype(jnp.float32)
-    ).astype(jnp.bfloat16)
-    residual_piece = incoming[:, feature_count:]
-
-    up_part = jnp.dot(normed, w_up, preferred_element_type=jnp.float32).astype(jnp.bfloat16)
-    ff_dev = up_part.shape[1]
-    lane_rows = rows_own * ff_dev // feature_count
-    up_chunks = up_part.reshape(n_page, lane_rows, feature_count)
-    bias_rows = jnp.tile(b_up.astype(jnp.float32).reshape(-1, feature_count), (lane_rows * feature_count // ff_dev, 1))
-    hidden = sum_gather(
-        up_chunks,
-        bias_rows,
-        "page",
-        lambda total, bias: jnp.maximum(total + bias, 0.0),
-        jnp.bfloat16,
-    ).reshape(samples * new_count, ff_dev)
+    incoming, hidden = up_project(
+        outgoing,
+        ln_gain.astype(jnp.float32).reshape(1, feature_count),
+        ln_bias.astype(jnp.float32).reshape(1, feature_count),
+        w_up,
+        b_up.astype(jnp.float32).reshape(1, -1),
+    )
+    residual_piece = incoming.reshape(samples * new_count, feature_count + piece_width)[:, feature_count:]
 
     projected_t = jnp.einsum("rf,fk->kr", hidden, w_down, preferred_element_type=jnp.float32)
     proj_pieces = projected_t.reshape(n_blk, piece_width, samples * new_count)

time: 164 us -> 159 us (0.970)
  Pallas kernels: 134 us -> 131 us
  local copies, waits for them, and re-layouts: 15.8 us -> 13.6 us
    pallas_call x2 -> x1, Pallas kernels: 59 us -> 52.7 us  [up_project(): pl.pallas_call(lambda *refs: up_kernel(n_page, *refs), out_shape=(jax.Sha...]
    pallas_call x1, Pallas kernels: 28.6 us -> 31.5 us  [output_and_score(): pl.pallas_call(lambda *refs: output_kernel(n_blk, n_page, *refs), out_sha...]
where the time goes in v6:
time: 159 us; the launch traced here: 158 us
  Pallas kernels  131 us (82%)
  local copies, waits for them, and re-layouts  13.6 us (9%)
  other arithmetic  6.95 us (4%)
  matrix products  6.25 us (4%)
    pallas_call x1, Pallas kernels, up_project(): pl.pallas_call(lambda *refs: up_kernel(n_page, *refs), out_shape=(jax.Sha...  52.7 us
    pallas_call x1, Pallas kernels, attention_out(): pl.pallas_call(lambda *refs: attention_out_kernel(n_page, n_blk, heads, *...  46.3 us
    pallas_call x1, Pallas kernels, output_and_score(): pl.pallas_call(lambda *refs: output_kernel(n_blk, n_page, *refs), out_sha...  31.5 us

profile of v6, /device:TPU:1, one launch (start us, length us, event | category | flops | bytes accessed | tf_op | source)
XLA Modules:
  0.0 158.2 jit_solution(1627735964726398847)
XLA Ops:
  0.7 0.8 dynamic_slice.12
  1.5 1.2 select_reduce_fusion.2
  2.7 1.2 convolution_bitcast_fusion.2
  4.2 0.6 squeeze_reshape_transpose_reshape.3.refs_1_
  4.9 0.8 eq.50
  5.8 0.7 select_reduce_fusion.3
  6.9 0.8 compare_and_fusion
  7.7 1.3 select_reduce_fusion
  8.9 1.3 convolution_bitcast_fusion.1
  10.8 0.8 reshape_transpose_reshape.3.refs_0_
  11.6 0.7 dynamic-slice_convert_fusion
  12.7 0.6 reshape.274
  13.4 46.3 %shard_map.176 = (f32[8,7168]{1,0:T(8,128)}, f32[8,7168]{1,0:T(8,128)}) custom-call(f32[16,8,384]{2,1,0:T(8,128)} %reshape_transpose_reshape.3.refs_0_, f32[8,384]{1,0:T(8,128)} %squeeze_reshape_transpose_reshape.3.refs_1_, bf16[128,7168]{1,0:T(8,128)(2,1)} %refs_2_.1, f32[8,7168]{1,0:T(8,128)} %copy-done.1, f32[1,7168]{1,0:T(1,128)} %bitcast.79), custom_call_target="tpu_custom_call" | custom-call | tf_op jit(solution)/shard_map/pallas_call | solution.py:352
  59.7 1.1 reshape.257
  61.0 1.1 reshape.258
  62.2 0.8 maximum_bitcast_fusion.refs_0_
  63.0 0.6 reshape.281.refs_4_
  63.5 0.6 reshape.276
  64.1 0.6 reshape.278
  64.7 52.7 %shard_map.177 = (f32[16,8,462]{2,1,0:T(8,128)}, bf16[128,896]{1,0:T(8,128)(2,1)}) custom-call(f32[16,8,462]{2,1,0:T(8,128)} %maximum_bitcast_fusion.refs_0_, f32[1,448]{1,0:T(1,128)} %bitcast.82, f32[1,448]{1,0:T(1,128)} %bitcast.83, bf16[448,896]{1,0:T(8,128)(2,1)} %refs_3_.1, f32[1,896]{1,0:T(1,128)} %reshape.281.refs_4_), custom_call_target="tpu_custom_call" | custom-call | tf_op jit(solution)/shard_map/pallas_call | solution.py:376
  117.4 1.3 convolution_bitcast_fusion
  118.8 0.7 reshape.265.refs_0_
  119.5 0.9 slice.24
  120.4 0.7 copy.53
  121.1 0.7 copy.47.refs_2_
  121.8 0.7 copy.48.refs_3_
  122.5 31.5 %shard_map.178 = (bf16[14,128]{1,0:T(8,128)(2,1)}, f32[1,128]{1,0:T(1,128)}) custom-call(f32[32,14,128]{2,1,0:T(8,128)} %reshape.265.refs_0_, f32[14,128]{1,0:T(8,128)} %bitcast.80, f32[14,1]{1,0:T(8,128)} %copy.47.refs_2_, f32[14,1]{1,0:T(8,128)} %copy.48.refs_3_), custom_call_target="tpu_custom_call" | custom-call | tf_op jit(solution)/shard_map/pallas_call | solution.py:399
  154.0 0.8 copy.49
  154.8 0.7 copy.50
  155.5 0.5 broadcast.173
  156.1 1.3 reduce.7
  157.5 0.6 copy.51
  (42 shorter events, 2.4 us)
Async XLA Ops:
  0.6 116.8 %copy-start = (bf16[896,448]{0,1:T(8,128)(2,1)S(1)}, bf16[896,448]{0,1:T(8,128)(2,1)}, u32[]{:S(2)}) copy-start(bf16[896,448]{0,1:T(8,128)(2,1)} %param.31) | copy-start | bytes 2408452
  8.9 3.8 %copy-start.2 = (bf16[7168]{0:T(1024)(128)(2,1)S(1)}, bf16[7168]{0:T(1024)(128)(2,1)}, u32[]{:S(2)}) copy-start(bf16[7168]{0:T(1024)(128)(2,1)} %param.26) | copy-start | bytes 43012
  12.7 0.7 copy-start.1
  13.4 49.6 %copy-start.3 = (bf16[896]{0:T(1024)(128)(2,1)S(1)}, bf16[896]{0:T(1024)(128)(2,1)}, u32[]{:S(2)}) copy-start(bf16[896]{0:T(1024)(128)(2,1)} %param.30) | copy-start | bytes 5380
  13.4 50.1 %copy-start.4 = (bf16[448]{0:T(512)(128)(2,1)S(1)}, bf16[448]{0:T(512)(128)(2,1)}, u32[]{:S(2)}) copy-start(bf16[448]{0:T(512)(128)(2,1)} %param.27) | copy-start | bytes 2692
  13.4 50.7 %copy-start.5 = (bf16[448]{0:T(512)(128)(2,1)S(1)}, bf16[448]{0:T(512)(128)(2,1)}, u32[]{:S(2)}) copy-start(bf16[448]{0:T(512)(128)(2,1)} %param.28) | copy-start | bytes 2692
  62.1 59.0 %copy-start.6 = (bf16[14]{0:T(256)(128)(2,1)S(1)}, bf16[14]{0:T(256)(128)(2,1)}, u32[]{:S(2)}) copy-start(bf16[14]{0:T(256)(128)(2,1)} %param.32) | copy-start | bytes 88
  62.2 59.6 %copy-start.7 = (bf16[14]{0:T(256)(128)(2,1)S(1)}, bf16[14]{0:T(256)(128)(2,1)}, u32[]{:S(2)}) copy-start(bf16[14]{0:T(256)(128)(2,1)} %param.33) | copy-start | bytes 88

commit v7 on v6

--- a/solution.py
+++ b/solution.py
@@ -72,16 +72,15 @@
     o_ref[...] = gat[...]
 
 
-def output_kernel(n_blk, n_page, x_ref, res_ref, bias_ref, score_w_ref, out_ref, score_ref,
-                  buf, blk_buf, page_buf, sems):
+def output_phase(n_blk, n_page, x_ref, res_t, bias, score_w, out_ref, score_ref,
+                 buf, blk_buf, page_buf, sems):
     me_blk = lax.axis_index("blk")
     me_page = lax.axis_index("page")
     buf[me_blk] = x_ref[me_blk]
-    enter([("blk", n_blk), ("page", n_page)])
     send_round("blk", n_blk, lambda peer: x_ref.at[peer], buf, sems.at[0], sems.at[1])
-    output = (slot_sum(buf, n_blk) + res_ref[...] + bias_ref[...]).astype(jnp.bfloat16)
+    output = (slot_sum(buf, n_blk) + res_t + bias).astype(jnp.bfloat16)
     out_ref[...] = output
-    blk_buf[me_blk] = jnp.sum(output.astype(jnp.float32) * score_w_ref[...], axis=0, keepdims=True)
+    blk_buf[me_blk] = jnp.sum(output.astype(jnp.float32) * score_w, axis=0, keepdims=True)
     send_round("blk", n_blk, lambda peer: blk_buf.at[me_blk], blk_buf, sems.at[2], sems.at[3])
     page_buf[me_page] = slot_sum(blk_buf, n_blk)
     send_round("page", n_page, lambda peer: page_buf.at[me_page], page_buf, sems.at[4], sems.at[5])
@@ -199,16 +198,16 @@
     inverse_std = lax.rsqrt(jnp.mean(centred * centred, axis=-1, keepdims=True) + 1e-05)
     scaled_ref[...] = centred * inverse_std
 
-def up_kernel(n_page, x_ref, gain_ref, bias_ref, w_ref, b_up_ref, recv_out_ref, hid_out_ref,
-              recv, up_s, red, hid_ref, sems):
+def mlp_kernel(n_page, n_blk, x_ref, gain_ref, bias_ref, w_ref, b_up_ref, pick_ref, w_down_ref,
+               b_down_ref, score_w_ref, out_ref, score_ref,
+               recv, up_s, red, hid_ref, pieces, out_buf, blk_buf, page_buf, sems):
     me = lax.axis_index("page")
     recv[me] = x_ref[me]
-    enter([("page", n_page)])
+    enter([("page", n_page), ("blk", n_blk)])
     send_round("page", n_page, lambda peer: x_ref.at[peer], recv, sems.at[0], sems.at[1])
-    recv_out_ref[...] = recv[...]
     features = gain_ref.shape[1]
-    rows = recv.shape[1]
-    scaled = jnp.concatenate([recv[j][:, :features] for j in range(n_page)], axis=0)
+    arrived = jnp.concatenate([recv[j] for j in range(n_page)], axis=0)
+    scaled = arrived[:, :features]
     normed = (scaled * gain_ref[...] + bias_ref[...]).astype(jnp.bfloat16)
     up_s[...] = jnp.dot(normed, w_ref[...], preferred_element_type=jnp.float32).astype(jnp.bfloat16)
     block = red.shape[1]
@@ -293,7 +292,18 @@
         def _():
             gather_arrival(k).wait_recv()
 
-    hid_out_ref[...] = hid_ref[...]
+    projected_t = lax.dot_general(
+        w_down_ref[...], hid_ref[...], (((0,), (1,)), ((), ())), preferred_element_type=jnp.float32
+    )
+    width = pieces.shape[1]
+    for j in range(n_blk):
+        pieces[j] = projected_t[j * width:(j + 1) * width]
+    res_t = lax.dot_general(
+        pick_ref[...], arrived, (((1,), (1,)), ((), ())),
+        precision=lax.Precision.HIGHEST, preferred_element_type=jnp.float32,
+    )
+    output_phase(n_blk, n_page, pieces, res_t, b_down_ref[...], score_w_ref[...], out_ref, score_ref,
+                 out_buf, blk_buf, page_buf, sems.at[6:12])
 
 
 CALL_IDS = {}
@@ -368,28 +378,34 @@
     )(part, tail, w_out, stream, bias)
 
 
-def up_project(outgoing, gain, bias, w_up, b_up):
+def mlp(outgoing, gain, bias, w_up, b_up, pick, w_down, b_down, score_w):
     n_page = lax.axis_size("page")
+    n_blk = lax.axis_size("blk")
     rows = outgoing.shape[0] * outgoing.shape[1]
     ff = w_up.shape[1]
     block = 2 * rows // n_page
+    width = b_down.shape[0]
     return pl.pallas_call(
-        lambda *refs: up_kernel(n_page, *refs),
+        lambda *refs: mlp_kernel(n_page, n_blk, *refs),
         out_shape=(
-            jax.ShapeDtypeStruct(outgoing.shape, jnp.float32),
-            jax.ShapeDtypeStruct((rows, ff), jnp.bfloat16),
+            jax.ShapeDtypeStruct((width, rows), jnp.bfloat16),
+            jax.ShapeDtypeStruct((1, rows), jnp.float32),
         ),
-        in_specs=vmem_specs(5),
+        in_specs=vmem_specs(9),
         out_specs=tuple(vmem_specs(2)),
         scratch_shapes=[
             pltpu.VMEM(outgoing.shape, jnp.float32),
             pltpu.VMEM((rows, ff), jnp.bfloat16),
             pltpu.VMEM((n_page, block, ff), jnp.bfloat16),
             pltpu.VMEM((rows, ff), jnp.bfloat16),
-            pltpu.SemaphoreType.DMA((6, n_page)),
+            pltpu.VMEM((n_blk, width, rows), jnp.float32),
+            pltpu.VMEM((n_blk, width, rows), jnp.float32),
+            pltpu.VMEM((n_blk, 1, rows), jnp.float32),
+            pltpu.VMEM((n_page, 1, rows), jnp.float32),
+            pltpu.SemaphoreType.DMA((12, max(n_page, n_blk))),
         ],
-        compiler_params=pltpu.CompilerParams(collective_id=next_id("page"), has_side_effects=True),
-    )(outgoing, gain, bias, w_up, b_up)
+        compiler_params=pltpu.CompilerParams(collective_id=next_id("both"), has_side_effects=True),
+    )(outgoing, gain, bias, w_up, b_up, pick, w_down, b_down, score_w)
 
 
 def output_and_score(x, res, bias, score_w):
@@ -545,20 +561,19 @@
         residual_f.reshape(rows_own, n_page, feature_count), blk_pos * piece_width, piece_width, 2
     )
     outgoing = jnp.concatenate([scaled3, res3], axis=-1).transpose(1, 0, 2)
-    incoming, hidden = up_project(
+    lanes_in = feature_count + piece_width
+    pick = (
+        jnp.arange(lanes_in, dtype=jnp.int32)[None, :]
+        == feature_count + jnp.arange(piece_width, dtype=jnp.int32)[:, None]
+    ).astype(jnp.float32)
+    output_t, row_score = mlp(
         outgoing,
         ln_gain.astype(jnp.float32).reshape(1, feature_count),
         ln_bias.astype(jnp.float32).reshape(1, feature_count),
         w_up,
         b_up.astype(jnp.float32).reshape(1, -1),
-    )
-    residual_piece = incoming.reshape(samples * new_count, feature_count + piece_width)[:, feature_count:]
-
-    projected_t = jnp.einsum("rf,fk->kr", hidden, w_down, preferred_element_type=jnp.float32)
-    proj_pieces = projected_t.reshape(n_blk, piece_width, samples * new_count)
-    output_t, row_score = output_and_score(
-        proj_pieces,
-        residual_piece.T,
+        pick,
+        w_down,
         b_down.astype(jnp.float32).reshape(piece_width, 1),
         w_score.astype(jnp.float32).reshape(piece_width, 1),
     )

time: 159 us -> 149 us (0.937)
  Pallas kernels: 131 us -> 122 us
    pallas_call x2 -> x1, Pallas kernels: 84.3 us -> 76.1 us  [mlp(): pl.pallas_call(lambda *refs: mlp_kernel(n_page, n_blk, *refs), out_shape=...]
where the time goes in v7:
time: 149 us
  Pallas kernels  122 us (82%)
  local copies, waits for them, and re-layouts  12.7 us (9%)
  other arithmetic  7.65 us (5%)
  matrix products  4.89 us (3%)
    pallas_call x1, Pallas kernels, mlp(): pl.pallas_call(lambda *refs: mlp_kernel(n_page, n_blk, *refs), out_shape=...  76.1 us
    pallas_call x1, Pallas kernels, attention_out(): pl.pallas_call(lambda *refs: attention_out_kernel(n_page, n_blk, heads, *...  46.3 us

profile of v7, /device:TPU:1, one launch (start us, length us, event | category | flops | bytes accessed | tf_op | source)
XLA Modules:
  0.0 148.5 jit_solution(12801674496084365834)
XLA Ops:
  0.7 0.7 dynamic_slice.12
  1.5 1.2 select_reduce_fusion.2
  2.7 1.2 convolution_bitcast_fusion.1
  4.2 0.6 squeeze_reshape_transpose_reshape.3.refs_1_
  4.8 0.8 eq.63
  5.5 0.2 select_reduce_fusion.1
  5.7 0.7 select_reduce_fusion.3
  6.8 0.8 compare_and_fusion
  7.6 1.3 select_reduce_fusion
  8.8 1.3 convolution_bitcast_fusion
  10.1 0.3 fusion.2
  10.7 0.8 reshape_transpose_reshape.3.refs_0_
  11.5 0.7 dynamic-slice_convert_fusion
  12.3 0.3 dynamic_update_slice.3.refs_3_
  12.6 0.6 reshape.271
  13.3 46.3 %shard_map.176 = (f32[8,7168]{1,0:T(8,128)}, f32[8,7168]{1,0:T(8,128)}) custom-call(f32[16,8,384]{2,1,0:T(8,128)} %reshape_transpose_reshape.3.refs_0_, f32[8,384]{1,0:T(8,128)} %squeeze_reshape_transpose_reshape.3.refs_1_, bf16[128,7168]{1,0:T(8,128)(2,1)} %refs_2_.1, f32[8,7168]{1,0:T(8,128)} %copy-done.1, f32[1,7168]{1,0:T(1,128)} %bitcast.74), custom_call_target="tpu_custom_call" | custom-call | tf_op jit(solution)/shard_map/pallas_call | solution.py:362
  59.6 1.1 reshape.256
  60.9 1.1 reshape.257
  62.1 0.8 maximum_bitcast_fusion.refs_0_
  62.9 1.5 %copy.46.refs_6_ = bf16[896,448]{1,0:T(8,128)(2,1)} copy(bf16[896,448]{0,1:T(8,128)(2,1)S(1)} %copy-done.2) | data formatting | bytes 1605632 | tf_op args[14]
  64.4 0.7 fusion.10.refs_5_
  65.1 0.7 copy.47.refs_7_
  65.8 0.7 copy.48.refs_8_
  66.5 0.6 reshape.278.refs_4_
  67.1 0.6 reshape.273
  67.7 0.6 reshape.275
  68.3 76.1 %shard_map.177 = (bf16[14,128]{1,0:T(8,128)(2,1)}, f32[1,128]{1,0:T(1,128)}) custom-call(f32[16,8,462]{2,1,0:T(8,128)} %maximum_bitcast_fusion.refs_0_, f32[1,448]{1,0:T(1,128)} %bitcast.75, f32[1,448]{1,0:T(1,128)} %bitcast.76, bf16[448,896]{1,0:T(8,128)(2,1)} %refs_3_.1, f32[1,896]{1,0:T(1,128)} %reshape.278.refs_4_, f32[14,462]{1,0:T(8,128)} %fusion.10.refs_5_, ...), custom_call_target="tpu_custom_call" | custom-call | tf_op jit(solution)/shard_map/pallas_call | solution.py:388
  144.4 0.8 copy.49
  145.2 0.7 copy.50
  145.9 0.5 broadcast.183
  146.4 1.3 reduce.7
  147.9 0.6 copy.51
  (42 shorter events, 1.6 us)
Async XLA Ops:
  0.6 0.8 copy-start
  8.8 3.8 %copy-start.3 = (bf16[7168]{0:T(1024)(128)(2,1)S(1)}, bf16[7168]{0:T(1024)(128)(2,1)}, u32[]{:S(2)}) copy-start(bf16[7168]{0:T(1024)(128)(2,1)} %param.26) | copy-start | bytes 43012
  12.6 0.7 copy-start.1
  13.3 49.6 %copy-start.2 = (bf16[896,448]{0,1:T(8,128)(2,1)S(1)}, bf16[896,448]{0,1:T(8,128)(2,1)}, u32[]{:S(2)}) copy-start(bf16[896,448]{0,1:T(8,128)(2,1)} %param.31) | copy-start | bytes 2408452
  60.7 4.4 %copy-start.7 = (bf16[14]{0:T(256)(128)(2,1)S(1)}, bf16[14]{0:T(256)(128)(2,1)}, u32[]{:S(2)}) copy-start(bf16[14]{0:T(256)(128)(2,1)} %param.32) | copy-start | bytes 88
  60.7 5.1 %copy-start.8 = (bf16[14]{0:T(256)(128)(2,1)S(1)}, bf16[14]{0:T(256)(128)(2,1)}, u32[]{:S(2)}) copy-start(bf16[14]{0:T(256)(128)(2,1)} %param.33) | copy-start | bytes 88
  60.7 5.8 %copy-start.4 = (bf16[896]{0:T(1024)(128)(2,1)S(1)}, bf16[896]{0:T(1024)(128)(2,1)}, u32[]{:S(2)}) copy-start(bf16[896]{0:T(1024)(128)(2,1)} %param.30) | copy-start | bytes 5380
  60.7 6.3 %copy-start.5 = (bf16[448]{0:T(512)(128)(2,1)S(1)}, bf16[448]{0:T(512)(128)(2,1)}, u32[]{:S(2)}) copy-start(bf16[448]{0:T(512)(128)(2,1)} %param.27) | copy-start | bytes 2692
  60.8 6.9 %copy-start.6 = (bf16[448]{0:T(512)(128)(2,1)S(1)}, bf16[448]{0:T(512)(128)(2,1)}, u32[]{:S(2)}) copy-start(bf16[448]{0:T(512)(128)(2,1)} %param.28) | copy-start | bytes 2692

commit v8 on v7

--- a/solution.py
+++ b/solution.py
@@ -16,7 +16,7 @@
     return tuple(j if name == axis else lax.axis_index(name) for name in AXES)
 
 
-def enter(sizes):
+def greet(sizes):
     barrier = pltpu.get_barrier_semaphore()
     total = 0
     for axis, n in sizes:
@@ -25,7 +25,11 @@
             peer = lax.rem(me + k, n)
             pl.semaphore_signal(barrier, inc=1, device_id=device_on(axis, peer), device_id_type=MESH_ID)
         total += n - 1
-    pl.semaphore_wait(barrier, total)
+    return total
+
+
+def enter(sizes):
+    pl.semaphore_wait(pltpu.get_barrier_semaphore(), greet(sizes))
 
 
 def send_round(axis, n, source, buf, send_sem, recv_sem):
@@ -87,15 +91,60 @@
     score_ref[...] = slot_sum(page_buf, n_page)
 
 
-def attention_out_kernel(n_page, n_blk, heads, part_ref, tail_ref, w_ref, stream_ref, bias_ref,
-                         res_ref, scaled_ref, recv, full, red, gat, sems):
+def softmax_rows(scores, visible):
+    highest = jnp.max(jnp.where(visible, scores, NEGATIVE), axis=1, keepdims=True)
+    weights = jnp.where(visible, jnp.exp(scores - highest), 0.0)
+    return highest, jnp.sum(weights, axis=1, keepdims=True), weights.astype(jnp.bfloat16)
+
+
+def attention_out_kernel(n_page, n_blk, heads, q_ref, kv_ref, tkv_ref, row_code_ref, key_code_ref,
+                         t_lo_ref, t_hi_ref, w_ref, stream_ref, bias_ref,
+                         res_ref, scaled_ref, part_ref, recv, full, red, gat, sems):
     me_page = lax.axis_index("page")
     me_blk = lax.axis_index("blk")
+    expected = greet([("page", n_page), ("blk", n_blk)])
+    hd = kv_ref.shape[1] // (2 * heads)
+    own_rows = t_lo_ref.shape[0]
+    inv_sqrt = 1.0 / math.sqrt(hd)
+    visible = row_code_ref[...] == key_code_ref[...]
+    position = lax.broadcasted_iota(jnp.int32, (1, tkv_ref.shape[0]), 1)
+    tail_visible = (position >= t_lo_ref[...]) & (position <= t_hi_ref[...])
+    own_block = pl.ds(pl.multiple_of(me_page * own_rows, own_rows), own_rows)
+    contract = (((1,), (1,)), ((), ()))
+    tail_parts = []
+    for h in range(heads):
+        keys = kv_ref[:, 2 * h * hd:(2 * h + 1) * hd]
+        values = kv_ref[:, (2 * h + 1) * hd:(2 * h + 2) * hd]
+        query = q_ref[:, h * hd:(h + 1) * hd]
+        scores = lax.dot_general(query, keys, contract, preferred_element_type=jnp.float32) * inv_sqrt
+        high, total, weights = softmax_rows(scores, visible)
+        mixed = jnp.dot(weights, values, preferred_element_type=jnp.float32)
+        for j in range(n_page):
+            rows = slice(j * own_rows, (j + 1) * own_rows)
+            part_ref[j, h * own_rows:(h + 1) * own_rows, :] = jnp.concatenate(
+                [
+                    mixed[rows],
+                    jnp.broadcast_to(high[rows], (own_rows, hd)),
+                    jnp.broadcast_to(total[rows], (own_rows, hd)),
+                ],
+                axis=1,
+            )
+        keys = tkv_ref[:, 2 * h * hd:(2 * h + 1) * hd]
+        values = tkv_ref[:, (2 * h + 1) * hd:(2 * h + 2) * hd]
+        query = q_ref[own_block, h * hd:(h + 1) * hd]
+        scores = lax.dot_general(query, keys, contract, preferred_element_type=jnp.float32) * inv_sqrt
+        high, total, weights = softmax_rows(scores, tail_visible)
+        mixed = jnp.dot(weights, values, preferred_element_type=jnp.float32)
+        tail_parts.append(
+            jnp.concatenate(
+                [mixed, jnp.broadcast_to(high, (own_rows, hd)), jnp.broadcast_to(total, (own_rows, hd))],
+                axis=1,
+            )
+        )
+    tail = jnp.concatenate(tail_parts, axis=0) if heads > 1 else tail_parts[0]
+    pl.semaphore_wait(pltpu.get_barrier_semaphore(), expected)
     recv[me_page] = part_ref[me_page]
-    enter([("page", n_page), ("blk", n_blk)])
     send_round("page", n_page, lambda peer: part_ref.at[peer], recv, sems.at[0], sems.at[1])
-    hd = w_ref.shape[0] // heads
-    tail = tail_ref[...]
     highest = tail[:, hd:2 * hd]
     for j in range(n_page):
         highest = jnp.maximum(highest, recv[j][:, hd:2 * hd])
@@ -351,31 +400,33 @@
     )(x, extra)
 
 
-def attention_out(part, tail, w_out, stream, bias):
+def attention_out(queries, kv, tkv, row_code, key_code, t_lo, t_hi, w_out, stream, bias, head_dim):
     n_page = lax.axis_size("page")
     n_blk = lax.axis_size("blk")
     rows, width = stream.shape
-    heads = w_out.shape[0] // (part.shape[2] // 3)
+    heads = kv.shape[1] // (2 * head_dim)
     lanes = 128 * (-(-width // (128 * n_blk)))
     n_chunk = width // lanes
     assert n_chunk * lanes == width
+    part_shape = (n_page, heads * rows, 3 * head_dim)
     return pl.pallas_call(
         lambda *refs: attention_out_kernel(n_page, n_blk, heads, *refs),
         out_shape=(
             jax.ShapeDtypeStruct((rows, width), jnp.float32),
             jax.ShapeDtypeStruct((rows, width), jnp.float32),
         ),
-        in_specs=vmem_specs(5),
+        in_specs=vmem_specs(10),
         out_specs=tuple(vmem_specs(2)),
         scratch_shapes=[
-            pltpu.VMEM(part.shape, jnp.float32),
+            pltpu.VMEM(part_shape, jnp.float32),
+            pltpu.VMEM(part_shape, jnp.float32),
             pltpu.VMEM((rows, width), jnp.float32),
             pltpu.VMEM((n_blk, rows, lanes), jnp.float32),
             pltpu.VMEM((n_chunk, rows, lanes), jnp.float32),
             pltpu.SemaphoreType.DMA((6, max(n_blk, n_page))),
         ],
         compiler_params=pltpu.CompilerParams(collective_id=next_id("both"), has_side_effects=True),
-    )(part, tail, w_out, stream, bias)
+    )(queries, kv, tkv, row_code, key_code, t_lo, t_hi, w_out, stream, bias)
 
 
 def mlp(outgoing, gain, bias, w_up, b_up, pick, w_down, b_down, score_w):
@@ -428,13 +479,6 @@
         ],
         compiler_params=pltpu.CompilerParams(collective_id=next_id("both"), has_side_effects=True),
     )(x, res, bias, score_w)
-
-
-def softmax_part(scores, visible):
-    masked = jnp.where(visible, scores, NEGATIVE)
-    highest = jnp.max(masked, axis=-1)
-    weights = jnp.where(visible, jnp.exp(scores - highest[..., None]), 0.0)
-    return (highest, jnp.sum(weights, axis=-1), weights.astype(jnp.bfloat16))
 
 
 def ordered_sum(stack):
@@ -488,56 +532,17 @@
     key_pos = slot_page[:, None] * page_len + jnp.arange(page_len, dtype=jnp.int32)[None, :]
     key_live = (key_pos < slot_limit[:, None]).reshape(-1)
     key_prompt = jnp.repeat(slot_prompt, page_len)
-    prompt_visible = ((sample_prompt[:, None] == key_prompt[None, :]) & key_live[None, :])[
-        :, None, None, :
-    ]
-
-    cache_rows = prompt_kv.reshape(slots_dev * page_len, heads_dev, 2 * head_dim)
-    prompt_scores = (
-        jnp.einsum(
-            "snhd,khd->snhk",
-            queries,
-            cache_rows[:, :, :head_dim],
-            preferred_element_type=jnp.float32,
-        )
-        * inv_sqrt
-    )
-    high_p, sum_p, weights_p = softmax_part(prompt_scores, prompt_visible)
-    mixed_p = jnp.einsum(
-        "snhk,khd->snhd", weights_p, cache_rows[:, :, head_dim:], preferred_element_type=jnp.float32
-    )
+    key_code = jnp.where(key_live, key_prompt, -1).astype(jnp.int32).reshape(1, -1)
+    row_code = jnp.repeat(sample_prompt, new_count).astype(jnp.int32).reshape(-1, 1)
 
     first_row = page_pos * own_count
-    own_queries = lax.dynamic_slice_in_dim(queries, first_row, own_count, 0)
     own_lengths = lax.dynamic_slice_in_dim(tail_len, first_row, own_count, 0)
-    tail_scores = (
-        jnp.einsum(
-            "snhd,sthd->snht",
-            own_queries,
-            tail_kv[..., :head_dim],
-            preferred_element_type=jnp.float32,
-        )
-        * inv_sqrt
-    )
-    reach_pos = own_lengths[:, None] + jnp.arange(new_count, dtype=jnp.int32)[None, :]
-    tail_visible = (
-        jnp.arange(tail_max, dtype=jnp.int32)[None, None, None, :] <= reach_pos[:, :, None, None]
-    )
-    high_t, sum_t, weights_t = softmax_part(tail_scores, tail_visible)
-    mixed_t = jnp.einsum(
-        "snht,sthd->snhd", weights_t, tail_kv[..., head_dim:], preferred_element_type=jnp.float32
-    )
-
-    def pack(mixed, high, total):
-        lanes = mixed.shape[-1]
-        parts = [mixed, jnp.broadcast_to(high[..., None], mixed.shape), jnp.broadcast_to(total[..., None], mixed.shape)]
-        whole = jnp.concatenate(parts, axis=-1)
-        whole = whole.reshape(-1, own_count, new_count, heads_dev, 3 * lanes).transpose(0, 3, 1, 2, 4)
-        return whole.reshape(-1, heads_dev * rows_own, 3 * lanes)
+    local_row = jnp.arange(rows_own, dtype=jnp.int32)
+    t_lo = (local_row // new_count) * tail_max
+    t_hi = t_lo + jnp.repeat(own_lengths, new_count) + local_row % new_count
 
     slice_width = stream_in.shape[2]
     column = blk_pos * slice_width
-    n_blk = width // slice_width
     own_stream = (
         lax.dynamic_slice_in_dim(stream_in, first_row, own_count, 0)
         .reshape(rows_own, slice_width)
@@ -547,11 +552,17 @@
         jnp.zeros((rows_own, width), jnp.float32), own_stream, column, 1
     )
     residual_f, scaled = attention_out(
-        pack(mixed_p, high_p, sum_p),
-        pack(mixed_t, high_t, sum_t)[0],
+        queries.reshape(samples * new_count, heads_dev * head_dim),
+        prompt_kv.reshape(slots_dev * page_len, heads_dev * 2 * head_dim),
+        tail_kv.reshape(own_count * tail_max, heads_dev * 2 * head_dim),
+        row_code,
+        key_code,
+        t_lo.reshape(-1, 1),
+        t_hi.reshape(-1, 1),
         w_out,
         stream_full,
         b_out.astype(jnp.float32).reshape(1, width),
+        head_dim,
     )
 
     feature_count = ln_gain.shape[0]

time: 149 us -> 144 us (0.966)
  matrix products: 4.89 us -> 0 us
    dot_general x4 -> x0, matrix products: 4.89 us -> none  [the longest x1 1.27 us: body(): jnp.einsum('snhd,khd->snhk', queries, cache_rows[:, :, :head_dim], prefer...]
where the time goes in v8:
time: 144 us
  Pallas kernels  122 us (85%)
  local copies, waits for them, and re-layouts  12.9 us (9%)
  other arithmetic  7.6 us (5%)
    pallas_call x1, Pallas kernels, mlp(): pl.pallas_call(lambda *refs: mlp_kernel(n_page, n_blk, *refs), out_shape=...  76.1 us
    pallas_call x1, Pallas kernels, attention_out(): pl.pallas_call(lambda *refs: attention_out_kernel(n_page, n_blk, heads, *...  46.3 us
    unnamed x18, local copies, waits for them, and re-layouts  2.93 us

profile of v8, /device:TPU:1, one launch (start us, length us, event | category | flops | bytes accessed | tf_op | source)
XLA Modules:
  0.0 143.7 jit_solution(1236549502197304738)
XLA Ops:
  0.6 0.7 dynamic-slice_convert_fusion
  1.4 0.3 dynamic_update_slice.3.refs_8_
  1.7 0.8 dynamic_slice.9
  2.5 0.1 reshape.253
  2.6 0.6 fusion.8
  3.2 0.8 eq.24
  4.0 0.2 select_reduce_fusion
  4.2 0.7 select_reduce_fusion.1
  5.0 0.7 select_n.78.refs_4_
  5.7 0.7 broadcast_in_dim.12
  6.4 0.7 reshape_reshape.4.refs_3_
  7.1 1.3 reshape.241
  8.4 46.3 %shard_map.176 = (f32[8,7168]{1,0:T(8,128)}, f32[8,7168]{1,0:T(8,128)}) custom-call(bf16[128,128]{1,0:T(8,128)(2,1)} %bitcast.20, bf16[1024,256]{1,0:T(8,128)(2,1)} %bitcast.16, bf16[1024,256]{1,0:T(8,128)(2,1)} %bitcast.17, s32[128,1]{1,0:T(8,128)} %reshape_reshape.4.refs_3_, s32[1,1024]{1,0:T(1,128)} %select_n.78.refs_4_, ...), custom_call_target="tpu_custom_call" | custom-call | tf_op jit(solution)/shard_map/pallas_call | solution.py:412
  54.8 1.1 reshape.227
  56.0 0.1 constant_dynamic-slice_fusion
  56.1 1.1 reshape.226
  57.2 0.2 copy.39
  57.3 0.8 maximum_bitcast_fusion.refs_0_
  58.1 1.5 %copy.40.refs_6_ = bf16[896,448]{1,0:T(8,128)(2,1)} copy(bf16[896,448]{0,1:T(8,128)(2,1)S(1)} %copy-done.1) | data formatting | bytes 1605632 | tf_op args[14]
  59.6 0.7 fusion.refs_5_
  60.3 0.7 copy.41.refs_7_
  61.0 0.7 copy.42.refs_8_
  61.7 0.6 reshape.248.refs_4_
  62.3 0.6 reshape.243
  62.9 0.6 reshape.245
  63.5 76.1 %shard_map.177 = (bf16[14,128]{1,0:T(8,128)(2,1)}, f32[1,128]{1,0:T(1,128)}) custom-call(f32[16,8,462]{2,1,0:T(8,128)} %maximum_bitcast_fusion.refs_0_, f32[1,448]{1,0:T(1,128)} %bitcast.21, f32[1,448]{1,0:T(1,128)} %bitcast.22, bf16[448,896]{1,0:T(8,128)(2,1)} %refs_3_.1, f32[1,896]{1,0:T(1,128)} %reshape.248.refs_4_, f32[14,462]{1,0:T(8,128)} %fusion.refs_5_, ...), custom_call_target="tpu_custom_call" | custom-call | tf_op jit(solution)/shard_map/pallas_call | solution.py:439
  139.6 0.8 copy.43
  140.4 0.7 copy.44
  141.1 0.5 broadcast.234
  141.6 1.3 reduce.3
  142.9 0.1 reshape.239
  143.1 0.6 copy.45
  (24 shorter events, 0.3 us)
Async XLA Ops:
  1.7 6.7 %copy-start = (f32[8,7168]{1,0:T(8,128)}, f32[8,7168]{1,0:T(8,128)S(1)}, u32[]{:S(2)}) copy-start(f32[8,7168]{1,0:T(8,128)S(1)} %dynamic_update_slice.3.refs_8_) | copy-start | bytes 688132
  54.8 3.3 %copy-start.1 = (bf16[896,448]{0,1:T(8,128)(2,1)S(1)}, bf16[896,448]{0,1:T(8,128)(2,1)}, u32[]{:S(2)}) copy-start(bf16[896,448]{0,1:T(8,128)(2,1)} %param.31) | copy-start | bytes 2408452
  55.9 4.4 %copy-start.5 = (bf16[14]{0:T(256)(128)(2,1)S(1)}, bf16[14]{0:T(256)(128)(2,1)}, u32[]{:S(2)}) copy-start(bf16[14]{0:T(256)(128)(2,1)} %param.32) | copy-start | bytes 88
  55.9 5.1 %copy-start.6 = (bf16[14]{0:T(256)(128)(2,1)S(1)}, bf16[14]{0:T(256)(128)(2,1)}, u32[]{:S(2)}) copy-start(bf16[14]{0:T(256)(128)(2,1)} %param.33) | copy-start | bytes 88
  55.9 5.8 %copy-start.2 = (bf16[896]{0:T(1024)(128)(2,1)S(1)}, bf16[896]{0:T(1024)(128)(2,1)}, u32[]{:S(2)}) copy-start(bf16[896]{0:T(1024)(128)(2,1)} %param.30) | copy-start | bytes 5380
  55.9 6.3 %copy-start.3 = (bf16[448]{0:T(512)(128)(2,1)S(1)}, bf16[448]{0:T(512)(128)(2,1)}, u32[]{:S(2)}) copy-start(bf16[448]{0:T(512)(128)(2,1)} %param.27) | copy-start | bytes 2692
  56.0 6.9 %copy-start.4 = (bf16[448]{0:T(512)(128)(2,1)S(1)}, bf16[448]{0:T(512)(128)(2,1)}, u32[]{:S(2)}) copy-start(bf16[448]{0:T(512)(128)(2,1)} %param.28) | copy-start | bytes 2692

commit v9 on v8

--- a/solution.py
+++ b/solution.py
@@ -98,8 +98,8 @@
 
 
 def attention_out_kernel(n_page, n_blk, heads, q_ref, kv_ref, tkv_ref, row_code_ref, key_code_ref,
-                         t_lo_ref, t_hi_ref, w_ref, stream_ref, bias_ref,
-                         res_ref, scaled_ref, part_ref, recv, full, red, gat, sems):
+                         t_lo_ref, t_hi_ref, w_ref, stream_ref,
+                         res_ref, scaled_ref, part_ref, recv, full, res_s, red, gat, sems):
     me_page = lax.axis_index("page")
     me_blk = lax.axis_index("blk")
     expected = greet([("page", n_page), ("blk", n_blk)])
@@ -219,7 +219,7 @@
             @pl.when(me_blk != s)
             def _():
                 scatter_arrival(s).wait_recv()
-        total = slot_sum(red, n_blk) + own(bias_ref)
+        total = slot_sum(red, n_blk)
         gat[me_blk] = total.astype(jnp.bfloat16).astype(jnp.float32)
         for k in range(1, n_blk):
             gather_copy(k).start()
@@ -240,24 +240,47 @@
             gather_arrival(s).wait_recv()
 
     for t in range(n_chunk):
-        res_ref[:, t * lanes:(t + 1) * lanes] = gat[t]
-    residual = res_ref[...]
+        res_s[:, t * lanes:(t + 1) * lanes] = gat[t]
+    residual = res_s[...]
     row_mean = jnp.mean(residual, axis=-1, keepdims=True)
     centred = residual - row_mean
     inverse_std = lax.rsqrt(jnp.mean(centred * centred, axis=-1, keepdims=True) + 1e-05)
-    scaled_ref[...] = centred * inverse_std
-
-def mlp_kernel(n_page, n_blk, x_ref, gain_ref, bias_ref, w_ref, b_up_ref, pick_ref, w_down_ref,
-               b_down_ref, score_w_ref, out_ref, score_ref,
-               recv, up_s, red, hid_ref, pieces, out_buf, blk_buf, page_buf, sems):
+    scaled = centred * inverse_std
+    group = scaled_ref.shape[2]
+    for q in range(n_page):
+        scaled_ref[q] = scaled[:, q * group:(q + 1) * group]
+        res_ref[q] = residual[:, q * group:(q + 1) * group]
+
+def mlp_kernel(n_page, n_blk, x_ref, r_ref, vec_ref, w_ref, w_down_ref, col_ref, out_ref, score_ref,
+               recv, recv_r, up_s, red, hid_ref, pieces, out_buf, blk_buf, page_buf, sems):
     me = lax.axis_index("page")
     recv[me] = x_ref[me]
+    recv_r[me] = r_ref[me]
     enter([("page", n_page), ("blk", n_blk)])
-    send_round("page", n_page, lambda peer: x_ref.at[peer], recv, sems.at[0], sems.at[1])
-    features = gain_ref.shape[1]
-    arrived = jnp.concatenate([recv[j] for j in range(n_page)], axis=0)
-    scaled = arrived[:, :features]
-    normed = (scaled * gain_ref[...] + bias_ref[...]).astype(jnp.bfloat16)
+    copies = []
+    for k in range(1, n_page):
+        peer = lax.rem(me + k, n_page)
+        for src, dst, idx in ((x_ref, recv, 0), (r_ref, recv_r, 12)):
+            copy = pltpu.make_async_remote_copy(
+                src_ref=src.at[peer],
+                dst_ref=dst.at[me],
+                send_sem=sems.at[idx, k],
+                recv_sem=sems.at[idx + 1, k],
+                device_id=device_on("page", peer),
+                device_id_type=MESH_ID,
+            )
+            copy.start()
+            copies.append(copy)
+    for copy in copies:
+        copy.wait()
+    features = x_ref.shape[2]
+    pad = -(-features // 128) * 128
+    gain = vec_ref[:, 0:features]
+    bias = vec_ref[:, pad:pad + features]
+    b_up = vec_ref[:, 2 * pad:]
+    scaled = jnp.concatenate([recv[j] for j in range(n_page)], axis=0)
+    res_rows = jnp.concatenate([recv_r[j] for j in range(n_page)], axis=0)
+    normed = (scaled * gain + bias).astype(jnp.bfloat16)
     up_s[...] = jnp.dot(normed, w_ref[...], preferred_element_type=jnp.float32).astype(jnp.bfloat16)
     block = red.shape[1]
     n_recv = up_s.shape[0] // block
@@ -319,7 +342,7 @@
             @pl.when(me != s)
             def _():
                 scatter_arrival(s).wait_recv()
-        total = slot_sum(red, n_page) + b_up_ref[...]
+        total = slot_sum(red, n_page) + b_up
         hid_ref[pl.ds(pl.multiple_of(mine * block, block), block)] = jnp.maximum(total, 0.0).astype(
             jnp.bfloat16
         )
@@ -347,11 +370,15 @@
     width = pieces.shape[1]
     for j in range(n_blk):
         pieces[j] = projected_t[j * width:(j + 1) * width]
+    eye = (
+        lax.broadcasted_iota(jnp.int32, (width, width), 0) == lax.broadcasted_iota(jnp.int32, (width, width), 1)
+    ).astype(jnp.float32)
     res_t = lax.dot_general(
-        pick_ref[...], arrived, (((1,), (1,)), ((), ())),
+        eye, res_rows, (((1,), (1,)), ((), ())),
         precision=lax.Precision.HIGHEST, preferred_element_type=jnp.float32,
     )
-    output_phase(n_blk, n_page, pieces, res_t, b_down_ref[...], score_w_ref[...], out_ref, score_ref,
+    columns = col_ref[...]
+    output_phase(n_blk, n_page, pieces, res_t, columns[:, 0:1], columns[:, 1:2], out_ref, score_ref,
                  out_buf, blk_buf, page_buf, sems.at[6:12])
 
 
@@ -400,7 +427,7 @@
     )(x, extra)
 
 
-def attention_out(queries, kv, tkv, row_code, key_code, t_lo, t_hi, w_out, stream, bias, head_dim):
+def attention_out(queries, kv, tkv, row_code, key_code, t_lo, t_hi, w_out, stream, head_dim):
     n_page = lax.axis_size("page")
     n_blk = lax.axis_size("blk")
     rows, width = stream.shape
@@ -412,40 +439,42 @@
     return pl.pallas_call(
         lambda *refs: attention_out_kernel(n_page, n_blk, heads, *refs),
         out_shape=(
-            jax.ShapeDtypeStruct((rows, width), jnp.float32),
-            jax.ShapeDtypeStruct((rows, width), jnp.float32),
+            jax.ShapeDtypeStruct((n_page, rows, width // n_page), jnp.float32),
+            jax.ShapeDtypeStruct((n_page, rows, width // n_page), jnp.float32),
         ),
-        in_specs=vmem_specs(10),
+        in_specs=vmem_specs(9),
         out_specs=tuple(vmem_specs(2)),
         scratch_shapes=[
             pltpu.VMEM(part_shape, jnp.float32),
             pltpu.VMEM(part_shape, jnp.float32),
+            pltpu.VMEM((rows, width), jnp.float32),
             pltpu.VMEM((rows, width), jnp.float32),
             pltpu.VMEM((n_blk, rows, lanes), jnp.float32),
             pltpu.VMEM((n_chunk, rows, lanes), jnp.float32),
             pltpu.SemaphoreType.DMA((6, max(n_blk, n_page))),
         ],
         compiler_params=pltpu.CompilerParams(collective_id=next_id("both"), has_side_effects=True),
-    )(queries, kv, tkv, row_code, key_code, t_lo, t_hi, w_out, stream, bias)
-
-
-def mlp(outgoing, gain, bias, w_up, b_up, pick, w_down, b_down, score_w):
+    )(queries, kv, tkv, row_code, key_code, t_lo, t_hi, w_out, stream)
+
+
+def mlp(scaled, res_pieces, vectors, w_up, w_down, columns):
     n_page = lax.axis_size("page")
     n_blk = lax.axis_size("blk")
-    rows = outgoing.shape[0] * outgoing.shape[1]
+    rows = scaled.shape[0] * scaled.shape[1]
     ff = w_up.shape[1]
     block = 2 * rows // n_page
-    width = b_down.shape[0]
+    width = columns.shape[0]
     return pl.pallas_call(
         lambda *refs: mlp_kernel(n_page, n_blk, *refs),
         out_shape=(
             jax.ShapeDtypeStruct((width, rows), jnp.bfloat16),
             jax.ShapeDtypeStruct((1, rows), jnp.float32),
         ),
-        in_specs=vmem_specs(9),
+        in_specs=vmem_specs(6),
         out_specs=tuple(vmem_specs(2)),
         scratch_shapes=[
-            pltpu.VMEM(outgoing.shape, jnp.float32),
+            pltpu.VMEM(scaled.shape, jnp.float32),
+            pltpu.VMEM(res_pieces.shape, jnp.float32),
             pltpu.VMEM((rows, ff), jnp.bfloat16),
             pltpu.VMEM((n_page, block, ff), jnp.bfloat16),
             pltpu.VMEM((rows, ff), jnp.bfloat16),
@@ -453,10 +482,10 @@
             pltpu.VMEM((n_blk, width, rows), jnp.float32),
             pltpu.VMEM((n_blk, 1, rows), jnp.float32),
             pltpu.VMEM((n_page, 1, rows), jnp.float32),
-            pltpu.SemaphoreType.DMA((12, max(n_page, n_blk))),
+            pltpu.SemaphoreType.DMA((14, max(n_page, n_blk))),
         ],
         compiler_params=pltpu.CompilerParams(collective_id=next_id("both"), has_side_effects=True),
-    )(outgoing, gain, bias, w_up, b_up, pick, w_down, b_down, score_w)
+    )(scaled, res_pieces, vectors, w_up, w_down, columns)
 
 
 def output_and_score(x, res, bias, score_w):
@@ -548,10 +577,11 @@
         .reshape(rows_own, slice_width)
         .astype(jnp.float32)
     )
+    own_bias = lax.dynamic_slice_in_dim(b_out, column, slice_width, 0).astype(jnp.float32)
     stream_full = lax.dynamic_update_slice_in_dim(
-        jnp.zeros((rows_own, width), jnp.float32), own_stream, column, 1
-    )
-    residual_f, scaled = attention_out(
+        jnp.zeros((rows_own, width), jnp.float32), own_stream + own_bias, column, 1
+    )
+    residual16, scaled16 = attention_out(
         queries.reshape(samples * new_count, heads_dev * head_dim),
         prompt_kv.reshape(slots_dev * page_len, heads_dev * 2 * head_dim),
         tail_kv.reshape(own_count * tail_max, heads_dev * 2 * head_dim),
@@ -561,33 +591,22 @@
         t_hi.reshape(-1, 1),
         w_out,
         stream_full,
-        b_out.astype(jnp.float32).reshape(1, width),
         head_dim,
     )
 
     feature_count = ln_gain.shape[0]
     piece_width = b_down.shape[0]
-    scaled3 = scaled.reshape(rows_own, n_page, feature_count)
-    res3 = lax.dynamic_slice_in_dim(
-        residual_f.reshape(rows_own, n_page, feature_count), blk_pos * piece_width, piece_width, 2
-    )
-    outgoing = jnp.concatenate([scaled3, res3], axis=-1).transpose(1, 0, 2)
-    lanes_in = feature_count + piece_width
-    pick = (
-        jnp.arange(lanes_in, dtype=jnp.int32)[None, :]
-        == feature_count + jnp.arange(piece_width, dtype=jnp.int32)[:, None]
-    ).astype(jnp.float32)
-    output_t, row_score = mlp(
-        outgoing,
-        ln_gain.astype(jnp.float32).reshape(1, feature_count),
-        ln_bias.astype(jnp.float32).reshape(1, feature_count),
-        w_up,
-        b_up.astype(jnp.float32).reshape(1, -1),
-        pick,
-        w_down,
-        b_down.astype(jnp.float32).reshape(piece_width, 1),
-        w_score.astype(jnp.float32).reshape(piece_width, 1),
-    )
+    res_pieces = lax.dynamic_slice_in_dim(residual16, blk_pos * piece_width, piece_width, 2)
+    pad = -(-feature_count // 128) * 128
+    vectors = jnp.concatenate(
+        [
+            jnp.pad(ln_gain.astype(jnp.float32), (0, pad - feature_count)),
+            jnp.pad(ln_bias.astype(jnp.float32), (0, pad - feature_count)),
+            b_up.astype(jnp.float32),
+        ]
+    ).reshape(1, -1)
+    columns = jnp.stack([b_down.astype(jnp.float32), w_score.astype(jnp.float32)], axis=1)
+    output_t, row_score = mlp(scaled16, res_pieces, vectors, w_up, w_down, columns)
     output = output_t.T
     return (output.reshape(samples, new_count, piece_width), row_score.reshape(samples, new_count))
 

time: 144 us -> 143 us (level)
  Pallas kernels: 122 us -> 126 us
  other arithmetic: 7.6 us -> 4.43 us
  local copies, waits for them, and re-layouts: 12.9 us -> 11.4 us
    reshape x6 -> x1, local copies, waits for them, and re-layouts: 4.29 us -> 0.6 us  [body(): vectors = jnp.concatenate([jnp.pad(ln_gain.astype(jnp.float32), (0, pad -...]
    pallas_call x1, Pallas kernels: 76.1 us -> 79.7 us  [mlp(): pl.pallas_call(lambda *refs: mlp_kernel(n_page, n_blk, *refs), out_shape=...]
    reshape x5 -> x1, other arithmetic: 2.48 us -> 0.01 us  [body(): vectors = jnp.concatenate([jnp.pad(ln_gain.astype(jnp.float32), (0, pad -...]
    dynamic_slice x1, local copies, waits for them, and re-layouts: 0.09 us -> 1.63 us  [body(): lax.dynamic_slice_in_dim(residual16, blk_pos * piece_width, piece_width, 2)]
    unnamed x18 -> x17, local copies, waits for them, and re-layouts: 2.93 us -> 2.9 us
where the time goes in v9:
time: 143 us
  Pallas kernels  126 us (88%)
  local copies, waits for them, and re-layouts  11.4 us (8%)
  other arithmetic  4.43 us (3%)
    pallas_call x1, Pallas kernels, mlp(): pl.pallas_call(lambda *refs: mlp_kernel(n_page, n_blk, *refs), out_shape=...  79.7 us
    pallas_call x1, Pallas kernels, attention_out(): pl.pallas_call(lambda *refs: attention_out_kernel(n_page, n_blk, heads, *...  46.6 us
    unnamed x17, local copies, waits for them, and re-layouts  2.9 us

profile of v9, /device:TPU:1, one launch (start us, length us, event | category | flops | bytes accessed | tf_op | source)
XLA Modules:
  0.0 142.9 jit_solution(3869227062038498530)
XLA Ops:
  0.6 0.7 dynamic-slice_convert_fusion
  1.3 0.8 dynamic-slice_convert_fusion.1
  2.1 0.0 copy-start.1
  2.2 0.3 dynamic_update_slice.3.refs_8_
  2.5 0.8 dynamic_slice.12
  3.2 0.1 broadcast_in_dim.28
  3.3 0.1 reshape.196
  3.4 0.6 fusion.10
  4.0 0.8 eq.32
  4.8 0.2 select_reduce_fusion
  5.0 0.7 select_reduce_fusion.1
  5.7 0.1 fusion.4
  5.8 0.7 select_n.79.refs_4_
  6.5 0.7 broadcast_in_dim.12
  7.2 0.7 reshape_reshape.4.refs_3_
  7.9 0.0 copy-done
  7.9 0.0 copy-start.5
  7.9 0.0 copy-start.6
  7.9 46.6 %shard_map.176 = (f32[16,8,448]{2,1,0:T(8,128)}, f32[16,8,448]{2,1,0:T(8,128)}) custom-call(bf16[128,128]{1,0:T(8,128)(2,1)} %bitcast.10, bf16[1024,256]{1,0:T(8,128)(2,1)} %bitcast.7, bf16[1024,256]{1,0:T(8,128)(2,1)} %bitcast.8, s32[128,1]{1,0:T(8,128)} %reshape_reshape.4.refs_3_, s32[1,1024]{1,0:T(1,128)} %select_n.79.refs_4_, ...), custom_call_target="tpu_custom_call" | custom-call | tf_op jit(solution)/shard_map/pallas_call | solution.py:439
  54.6 1.6 %constant_dynamic-slice_fusion.refs_1_ = f32[16,8,14]{2,1,0:T(8,128)} fusion(f32[16,8,448]{2,1,0:T(8,128)} %get-tuple-element.7, s32[]{:T(128)S(6)} %select_n.84), kind=kLoop, calls=%fused_computation.37 | loop fusion | bytes 14340 | tf_op jit(solution)/shard_map/dynamic_slice | solution.py:599
  56.2 1.5 %copy.50.refs_4_ = bf16[896,448]{1,0:T(8,128)(2,1)} copy(bf16[896,448]{0,1:T(8,128)(2,1)S(1)} %copy-done.1) | data formatting | bytes 1605632 | tf_op args[14]
  57.7 0.0 copy-done.4
  57.8 0.6 reshape.195.refs_2_
  58.4 0.0 copy-done.6
  58.4 0.7 copy.51.refs_5_
  59.1 79.7 %shard_map.177 = (bf16[14,128]{1,0:T(8,128)(2,1)}, f32[1,128]{1,0:T(1,128)}) custom-call(f32[16,8,448]{2,1,0:T(8,128)} %get-tuple-element.6.refs_0_, f32[16,8,14]{2,1,0:T(8,128)} %constant_dynamic-slice_fusion.refs_1_, f32[1,1920]{1,0:T(1,128)} %reshape.195.refs_2_, bf16[448,896]{1,0:T(8,128)(2,1)} %refs_3_.1, bf16[896,448]{1,0:T(8,128)(2,1)} %copy.50.refs_4_, ...), custom_call_target="tpu_custom_call" | custom-call | tf_op jit(solution)/shard_map/pallas_call | solution.py:467
  138.8 0.8 copy.52
  139.6 0.7 copy.53
  140.3 0.5 broadcast.237
  140.8 1.3 reduce.3
  142.1 0.1 reshape.192
  142.3 0.6 copy.54
  (15 shorter events, 0.1 us)
Async XLA Ops:
  2.1 54.1 %copy-start.1 = (bf16[896,448]{0,1:T(8,128)(2,1)S(1)}, bf16[896,448]{0,1:T(8,128)(2,1)}, u32[]{:S(2)}) copy-start(bf16[896,448]{0,1:T(8,128)(2,1)} %param.31) | copy-start | bytes 2408452
  2.5 5.4 %copy-start = (f32[8,7168]{1,0:T(8,128)}, f32[8,7168]{1,0:T(8,128)S(1)}, u32[]{:S(2)}) copy-start(f32[8,7168]{1,0:T(8,128)S(1)} %dynamic_update_slice.3.refs_8_) | copy-start | bytes 688132
  7.9 49.8 %copy-start.2 = (bf16[896]{0:T(1024)(128)(2,1)S(1)}, bf16[896]{0:T(1024)(128)(2,1)}, u32[]{:S(2)}) copy-start(bf16[896]{0:T(1024)(128)(2,1)} %param.30) | copy-start | bytes 5380
  7.9 49.8 %copy-start.3 = (bf16[448]{0:T(512)(128)(2,1)S(1)}, bf16[448]{0:T(512)(128)(2,1)}, u32[]{:S(2)}) copy-start(bf16[448]{0:T(512)(128)(2,1)} %param.28) | copy-start | bytes 2692
  7.9 49.8 %copy-start.4 = (bf16[448]{0:T(512)(128)(2,1)S(1)}, bf16[448]{0:T(512)(128)(2,1)}, u32[]{:S(2)}) copy-start(bf16[448]{0:T(512)(128)(2,1)} %param.27) | copy-start | bytes 2692
  7.9 50.4 %copy-start.5 = (bf16[14]{0:T(256)(128)(2,1)S(1)}, bf16[14]{0:T(256)(128)(2,1)}, u32[]{:S(2)}) copy-start(bf16[14]{0:T(256)(128)(2,1)} %param.33) | copy-start | bytes 88
  7.9 50.4 %copy-start.6 = (bf16[14]{0:T(256)(128)(2,1)S(1)}, bf16[14]{0:T(256)(128)(2,1)}, u32[]{:S(2)}) copy-start(bf16[14]{0:T(256)(128)(2,1)} %param.32) | copy-start | bytes 88

commit v10 on v9

--- a/solution.py
+++ b/solution.py
@@ -111,6 +111,7 @@
     tail_visible = (position >= t_lo_ref[...]) & (position <= t_hi_ref[...])
     own_block = pl.ds(pl.multiple_of(me_page * own_rows, own_rows), own_rows)
     contract = (((1,), (1,)), ((), ()))
+    half = lax.broadcasted_iota(jnp.int32, (1, hd), 1) < hd // 2
     tail_parts = []
     for h in range(heads):
         keys = kv_ref[:, 2 * h * hd:(2 * h + 1) * hd]
@@ -119,42 +120,33 @@
         scores = lax.dot_general(query, keys, contract, preferred_element_type=jnp.float32) * inv_sqrt
         high, total, weights = softmax_rows(scores, visible)
         mixed = jnp.dot(weights, values, preferred_element_type=jnp.float32)
+        stats = jnp.where(half, jnp.broadcast_to(high, (high.shape[0], hd)), jnp.broadcast_to(total, (high.shape[0], hd)))
         for j in range(n_page):
             rows = slice(j * own_rows, (j + 1) * own_rows)
-            part_ref[j, h * own_rows:(h + 1) * own_rows, :] = jnp.concatenate(
-                [
-                    mixed[rows],
-                    jnp.broadcast_to(high[rows], (own_rows, hd)),
-                    jnp.broadcast_to(total[rows], (own_rows, hd)),
-                ],
-                axis=1,
-            )
+            part_ref[j, h * own_rows:(h + 1) * own_rows, :] = jnp.concatenate([mixed[rows], stats[rows]], axis=1)
         keys = tkv_ref[:, 2 * h * hd:(2 * h + 1) * hd]
         values = tkv_ref[:, (2 * h + 1) * hd:(2 * h + 2) * hd]
         query = q_ref[own_block, h * hd:(h + 1) * hd]
         scores = lax.dot_general(query, keys, contract, preferred_element_type=jnp.float32) * inv_sqrt
         high, total, weights = softmax_rows(scores, tail_visible)
         mixed = jnp.dot(weights, values, preferred_element_type=jnp.float32)
-        tail_parts.append(
-            jnp.concatenate(
-                [mixed, jnp.broadcast_to(high, (own_rows, hd)), jnp.broadcast_to(total, (own_rows, hd))],
-                axis=1,
-            )
-        )
-    tail = jnp.concatenate(tail_parts, axis=0) if heads > 1 else tail_parts[0]
+        tail_parts.append((mixed, high, total))
+    tail_mixed = jnp.concatenate([t[0] for t in tail_parts], axis=0)
+    tail_high = jnp.concatenate([t[1] for t in tail_parts], axis=0)
+    tail_total = jnp.concatenate([t[2] for t in tail_parts], axis=0)
     pl.semaphore_wait(pltpu.get_barrier_semaphore(), expected)
     recv[me_page] = part_ref[me_page]
     send_round("page", n_page, lambda peer: part_ref.at[peer], recv, sems.at[0], sems.at[1])
-    highest = tail[:, hd:2 * hd]
+    highest = tail_high
     for j in range(n_page):
-        highest = jnp.maximum(highest, recv[j][:, hd:2 * hd])
-    scale = jnp.exp(tail[:, hd:2 * hd] - highest)
-    weight_sum = tail[:, 2 * hd:] * scale
-    weighted = tail[:, :hd] * scale
+        highest = jnp.maximum(highest, recv[j][:, hd:hd + 1])
+    scale = jnp.exp(tail_high - highest)
+    weight_sum = tail_total * scale
+    weighted = tail_mixed * scale
     for j in range(n_page):
         part = recv[j]
-        scale = jnp.exp(part[:, hd:2 * hd] - highest)
-        weight_sum = weight_sum + part[:, 2 * hd:] * scale
+        scale = jnp.exp(part[:, hd:hd + 1] - highest)
+        weight_sum = weight_sum + part[:, hd + hd // 2:hd + hd // 2 + 1] * scale
         weighted = weighted + part[:, :hd] * scale
     attention = (weighted / weight_sum).astype(jnp.bfloat16)
     rows = attention.shape[0] // heads
@@ -251,35 +243,21 @@
         scaled_ref[q] = scaled[:, q * group:(q + 1) * group]
         res_ref[q] = residual[:, q * group:(q + 1) * group]
 
-def mlp_kernel(n_page, n_blk, x_ref, r_ref, vec_ref, w_ref, w_down_ref, col_ref, out_ref, score_ref,
-               recv, recv_r, up_s, red, hid_ref, pieces, out_buf, blk_buf, page_buf, sems):
+def mlp_kernel(n_page, n_blk, x_ref, vec_ref, w_ref, w_down_ref, col_ref, out_ref, score_ref,
+               recv, up_s, red, hid_ref, pieces, out_buf, blk_buf, page_buf, sems):
     me = lax.axis_index("page")
     recv[me] = x_ref[me]
-    recv_r[me] = r_ref[me]
     enter([("page", n_page), ("blk", n_blk)])
-    copies = []
-    for k in range(1, n_page):
-        peer = lax.rem(me + k, n_page)
-        for src, dst, idx in ((x_ref, recv, 0), (r_ref, recv_r, 12)):
-            copy = pltpu.make_async_remote_copy(
-                src_ref=src.at[peer],
-                dst_ref=dst.at[me],
-                send_sem=sems.at[idx, k],
-                recv_sem=sems.at[idx + 1, k],
-                device_id=device_on("page", peer),
-                device_id_type=MESH_ID,
-            )
-            copy.start()
-            copies.append(copy)
-    for copy in copies:
-        copy.wait()
-    features = x_ref.shape[2]
+    send_round("page", n_page, lambda peer: x_ref.at[peer], recv, sems.at[0], sems.at[1])
+    width = col_ref.shape[0]
+    lanes_in = x_ref.shape[2]
+    features = lanes_in - width
     pad = -(-features // 128) * 128
     gain = vec_ref[:, 0:features]
     bias = vec_ref[:, pad:pad + features]
     b_up = vec_ref[:, 2 * pad:]
-    scaled = jnp.concatenate([recv[j] for j in range(n_page)], axis=0)
-    res_rows = jnp.concatenate([recv_r[j] for j in range(n_page)], axis=0)
+    arrived = jnp.concatenate([recv[j] for j in range(n_page)], axis=0)
+    scaled = arrived[:, :features]
     normed = (scaled * gain + bias).astype(jnp.bfloat16)
     up_s[...] = jnp.dot(normed, w_ref[...], preferred_element_type=jnp.float32).astype(jnp.bfloat16)
     block = red.shape[1]
@@ -367,14 +345,14 @@
     projected_t = lax.dot_general(
         w_down_ref[...], hid_ref[...], (((0,), (1,)), ((), ())), preferred_element_type=jnp.float32
     )
-    width = pieces.shape[1]
     for j in range(n_blk):
         pieces[j] = projected_t[j * width:(j + 1) * width]
-    eye = (
-        lax.broadcasted_iota(jnp.int32, (width, width), 0) == lax.broadcasted_iota(jnp.int32, (width, width), 1)
+    pick = (
+        lax.broadcasted_iota(jnp.int32, (width, lanes_in), 1)
+        == lax.broadcasted_iota(jnp.int32, (width, lanes_in), 0) + features
     ).astype(jnp.float32)
     res_t = lax.dot_general(
-        eye, res_rows, (((1,), (1,)), ((), ())),
+        pick, arrived, (((1,), (1,)), ((), ())),
         precision=lax.Precision.HIGHEST, preferred_element_type=jnp.float32,
     )
     columns = col_ref[...]
@@ -435,7 +413,7 @@
     lanes = 128 * (-(-width // (128 * n_blk)))
     n_chunk = width // lanes
     assert n_chunk * lanes == width
-    part_shape = (n_page, heads * rows, 3 * head_dim)
+    part_shape = (n_page, heads * rows, 2 * head_dim)
     return pl.pallas_call(
         lambda *refs: attention_out_kernel(n_page, n_blk, heads, *refs),
         out_shape=(
@@ -457,10 +435,10 @@
     )(queries, kv, tkv, row_code, key_code, t_lo, t_hi, w_out, stream)
 
 
-def mlp(scaled, res_pieces, vectors, w_up, w_down, columns):
+def mlp(outgoing, vectors, w_up, w_down, columns):
     n_page = lax.axis_size("page")
     n_blk = lax.axis_size("blk")
-    rows = scaled.shape[0] * scaled.shape[1]
+    rows = outgoing.shape[0] * outgoing.shape[1]
     ff = w_up.shape[1]
     block = 2 * rows // n_page
     width = columns.shape[0]
@@ -470,11 +448,10 @@
             jax.ShapeDtypeStruct((width, rows), jnp.bfloat16),
             jax.ShapeDtypeStruct((1, rows), jnp.float32),
         ),
-        in_specs=vmem_specs(6),
+        in_specs=vmem_specs(5),
         out_specs=tuple(vmem_specs(2)),
         scratch_shapes=[
-            pltpu.VMEM(scaled.shape, jnp.float32),
-            pltpu.VMEM(res_pieces.shape, jnp.float32),
+            pltpu.VMEM(outgoing.shape, jnp.float32),
             pltpu.VMEM((rows, ff), jnp.bfloat16),
             pltpu.VMEM((n_page, block, ff), jnp.bfloat16),
             pltpu.VMEM((rows, ff), jnp.bfloat16),
@@ -482,10 +459,10 @@
             pltpu.VMEM((n_blk, width, rows), jnp.float32),
             pltpu.VMEM((n_blk, 1, rows), jnp.float32),
             pltpu.VMEM((n_page, 1, rows), jnp.float32),
-            pltpu.SemaphoreType.DMA((14, max(n_page, n_blk))),
+            pltpu.SemaphoreType.DMA((12, max(n_page, n_blk))),
         ],
         compiler_params=pltpu.CompilerParams(collective_id=next_id("both"), has_side_effects=True),
-    )(scaled, res_pieces, vectors, w_up, w_down, columns)
+    )(outgoing, vectors, w_up, w_down, columns)
 
 
 def output_and_score(x, res, bias, score_w):
@@ -606,7 +583,8 @@
         ]
     ).reshape(1, -1)
     columns = jnp.stack([b_down.astype(jnp.float32), w_score.astype(jnp.float32)], axis=1)
-    output_t, row_score = mlp(scaled16, res_pieces, vectors, w_up, w_down, columns)
+    outgoing = jnp.concatenate([scaled16, res_pieces], axis=-1)
+    output_t, row_score = mlp(outgoing, vectors, w_up, w_down, columns)
     output = output_t.T
     return (output.reshape(samples, new_count, piece_width), row_score.reshape(samples, new_count))
 

time: 143 us -> 138 us (0.965)
  Pallas kernels: 126 us -> 120 us
  other arithmetic: 4.43 us -> 6.12 us
    pallas_call x1, Pallas kernels: 79.7 us -> 76 us  [mlp(): pl.pallas_call(lambda *refs: mlp_kernel(n_page, n_blk, *refs), out_shape=...]
    pallas_call x1, Pallas kernels: 46.6 us -> 44.2 us  [attention_out(): pl.pallas_call(lambda *refs: attention_out_kernel(n_page, n_blk, heads, *...]
    concatenate x0 -> x1, other arithmetic: none -> 1.74 us  [body(): outgoing = jnp.concatenate([scaled16, res_pieces], axis=-1)]
where the time goes in v10:
time: 138 us
  Pallas kernels  120 us (87%)
  local copies, waits for them, and re-layouts  10.8 us (8%)
  other arithmetic  6.12 us (4%)
    pallas_call x1, Pallas kernels, mlp(): pl.pallas_call(lambda *refs: mlp_kernel(n_page, n_blk, *refs), out_shape=...  76 us
    pallas_call x1, Pallas kernels, attention_out(): pl.pallas_call(lambda *refs: attention_out_kernel(n_page, n_blk, heads, *...  44.2 us
    unnamed x17, local copies, waits for them, and re-layouts  2.9 us

profile of v10, /device:TPU:1, one launch (start us, length us, event | category | flops | bytes accessed | tf_op | source)
XLA Modules:
  0.0 137.8 jit_solution(15105566306134195517)
XLA Ops:
  0.6 0.7 dynamic-slice_convert_fusion
  1.3 0.8 dynamic-slice_convert_fusion.1
  2.1 0.3 dynamic_update_slice.3.refs_8_
  2.5 0.8 dynamic_slice.12
  3.2 0.1 broadcast_in_dim.28
  3.3 0.1 reshape.196
  3.4 0.6 fusion.10
  4.0 0.8 eq.32
  4.8 0.2 select_reduce_fusion
  5.0 0.7 select_reduce_fusion.1
  5.7 0.1 fusion.4
  5.8 0.7 select_n.79.refs_4_
  6.5 0.7 broadcast_in_dim.12
  7.2 0.7 reshape_reshape.4.refs_3_
  7.9 44.2 %shard_map.176 = (f32[16,8,448]{2,1,0:T(8,128)}, f32[16,8,448]{2,1,0:T(8,128)}) custom-call(bf16[128,128]{1,0:T(8,128)(2,1)} %bitcast.10, bf16[1024,256]{1,0:T(8,128)(2,1)} %bitcast.7, bf16[1024,256]{1,0:T(8,128)(2,1)} %bitcast.8, s32[128,1]{1,0:T(8,128)} %reshape_reshape.4.refs_3_, s32[1,1024]{1,0:T(1,128)} %select_n.79.refs_4_, ...), custom_call_target="tpu_custom_call" | custom-call | tf_op jit(solution)/shard_map/pallas_call | solution.py:417
  52.1 0.0 copy-start.2
  52.1 0.0 copy-start.3
  52.2 0.0 copy-start.4
  52.2 0.0 copy-start.5
  52.2 0.0 copy-start.6
  52.2 1.0 constant_dynamic-slice_fusion
  53.2 1.7 %pad_maximum_fusion.refs_0_ = f32[16,8,462]{2,1,0:T(8,128)} fusion(f32[16,8,14]{2,1,0:T(8,128)S(1)} %constant_dynamic-slice_fusion, f32[16,8,448]{2,1,0:T(8,128)} %get-tuple-element.6), kind=kLoop, calls=%fused_computation | loop fusion | flops 59136 | bytes 473088 | tf_op jit(solution)/shard_map/concatenate | solution.py:586
  54.9 1.5 %copy.50.refs_3_ = bf16[896,448]{1,0:T(8,128)(2,1)} copy(bf16[896,448]{0,1:T(8,128)(2,1)S(1)} %copy-done.1) | data formatting | bytes 1605632 | tf_op args[14]
  56.5 0.6 reshape.195.refs_1_
  57.1 0.7 copy.51.refs_4_
  57.8 76.0 %shard_map.177 = (bf16[14,128]{1,0:T(8,128)(2,1)}, f32[1,128]{1,0:T(1,128)}) custom-call(f32[16,8,462]{2,1,0:T(8,128)} %pad_maximum_fusion.refs_0_, f32[1,1920]{1,0:T(1,128)} %reshape.195.refs_1_, bf16[448,896]{1,0:T(8,128)(2,1)} %refs_2_.1, bf16[896,448]{1,0:T(8,128)(2,1)} %copy.50.refs_3_, f32[14,2]{1,0:T(8,128)} %copy.51.refs_4_), custom_call_target="tpu_custom_call" | custom-call | tf_op jit(solution)/shard_map/pallas_call | solution.py:445
  133.8 0.8 copy.52
  134.6 0.7 copy.53
  135.3 0.5 broadcast.237
  135.8 1.3 reduce.3
  137.0 0.1 reshape.192
  137.2 0.6 copy.54
  (16 shorter events, 0.1 us)
Async XLA Ops:
  2.5 5.4 %copy-start = (f32[8,7168]{1,0:T(8,128)}, f32[8,7168]{1,0:T(8,128)S(1)}, u32[]{:S(2)}) copy-start(f32[8,7168]{1,0:T(8,128)S(1)} %dynamic_update_slice.3.refs_8_) | copy-start | bytes 688132
  7.9 47.0 %copy-start.1 = (bf16[896,448]{0,1:T(8,128)(2,1)S(1)}, bf16[896,448]{0,1:T(8,128)(2,1)}, u32[]{:S(2)}) copy-start(bf16[896,448]{0,1:T(8,128)(2,1)} %param.31) | copy-start | bytes 2408452
  52.1 4.3 %copy-start.2 = (bf16[896]{0:T(1024)(128)(2,1)S(1)}, bf16[896]{0:T(1024)(128)(2,1)}, u32[]{:S(2)}) copy-start(bf16[896]{0:T(1024)(128)(2,1)} %param.30) | copy-start | bytes 5380
  52.1 4.3 %copy-start.3 = (bf16[448]{0:T(512)(128)(2,1)S(1)}, bf16[448]{0:T(512)(128)(2,1)}, u32[]{:S(2)}) copy-start(bf16[448]{0:T(512)(128)(2,1)} %param.28) | copy-start | bytes 2692
  52.2 4.3 %copy-start.4 = (bf16[448]{0:T(512)(128)(2,1)S(1)}, bf16[448]{0:T(512)(128)(2,1)}, u32[]{:S(2)}) copy-start(bf16[448]{0:T(512)(128)(2,1)} %param.27) | copy-start | bytes 2692
  52.2 4.9 %copy-start.5 = (bf16[14]{0:T(256)(128)(2,1)S(1)}, bf16[14]{0:T(256)(128)(2,1)}, u32[]{:S(2)}) copy-start(bf16[14]{0:T(256)(128)(2,1)} %param.33) | copy-start | bytes 88
  52.2 4.9 %copy-start.6 = (bf16[14]{0:T(256)(128)(2,1)S(1)}, bf16[14]{0:T(256)(128)(2,1)}, u32[]{:S(2)}) copy-start(bf16[14]{0:T(256)(128)(2,1)} %param.32) | copy-start | bytes 88

commit v11 on v10

--- a/solution.py
+++ b/solution.py
@@ -83,12 +83,23 @@
     buf[me_blk] = x_ref[me_blk]
     send_round("blk", n_blk, lambda peer: x_ref.at[peer], buf, sems.at[0], sems.at[1])
     output = (slot_sum(buf, n_blk) + res_t + bias).astype(jnp.bfloat16)
-    out_ref[...] = output
+    lanes = output.shape[1]
+    spread = lanes // 2
+    source = lax.broadcasted_iota(jnp.int32, (lanes, lanes), 0)
+    target = lax.broadcasted_iota(jnp.int32, (lanes, lanes), 1)
+    order = (source == (target % spread) * 2 + target // spread).astype(jnp.float32)
+
+    def reorder(value):
+        return jnp.dot(value, order, precision=lax.Precision.HIGHEST, preferred_element_type=jnp.float32)
+
+    out_ref[...] = reorder(output.astype(jnp.float32)).astype(jnp.bfloat16)
     blk_buf[me_blk] = jnp.sum(output.astype(jnp.float32) * score_w, axis=0, keepdims=True)
     send_round("blk", n_blk, lambda peer: blk_buf.at[me_blk], blk_buf, sems.at[2], sems.at[3])
     page_buf[me_page] = slot_sum(blk_buf, n_blk)
     send_round("page", n_page, lambda peer: page_buf.at[me_page], page_buf, sems.at[4], sems.at[5])
-    score_ref[...] = slot_sum(page_buf, n_page)
+    score = reorder(slot_sum(page_buf, n_page))
+    score_ref[0:1, :] = score[:, :spread]
+    score_ref[1:2, :] = score[:, spread:]
 
 
 def softmax_rows(scores, visible):
@@ -446,7 +457,7 @@
         lambda *refs: mlp_kernel(n_page, n_blk, *refs),
         out_shape=(
             jax.ShapeDtypeStruct((width, rows), jnp.bfloat16),
-            jax.ShapeDtypeStruct((1, rows), jnp.float32),
+            jax.ShapeDtypeStruct((2, rows // 2), jnp.float32),
         ),
         in_specs=vmem_specs(5),
         out_specs=tuple(vmem_specs(2)),
@@ -585,8 +596,8 @@
     columns = jnp.stack([b_down.astype(jnp.float32), w_score.astype(jnp.float32)], axis=1)
     outgoing = jnp.concatenate([scaled16, res_pieces], axis=-1)
     output_t, row_score = mlp(outgoing, vectors, w_up, w_down, columns)
-    output = output_t.T
-    return (output.reshape(samples, new_count, piece_width), row_score.reshape(samples, new_count))
+    output = output_t.reshape(piece_width, new_count, samples).transpose(2, 1, 0)
+    return (output, row_score.T)
 
 
 def solution(mesh):

time: 138 us -> 139 us (level)
    unnamed x17 -> x6, local copies, waits for them, and re-layouts: 2.9 us -> 3.48 us
where the time goes in v11:
time: 139 us
  Pallas kernels  121 us (87%)
  local copies, waits for them, and re-layouts  11.2 us (8%)
  other arithmetic  6.23 us (4%)
    pallas_call x1, Pallas kernels, mlp(): pl.pallas_call(lambda *refs: mlp_kernel(n_page, n_blk, *refs), out_shape=...  76.3 us
    pallas_call x1, Pallas kernels, attention_out(): pl.pallas_call(lambda *refs: attention_out_kernel(n_page, n_blk, heads, *...  44.2 us
    unnamed x6, local copies, waits for them, and re-layouts  3.48 us

profile of v11, /device:TPU:1, one launch (start us, length us, event | category | flops | bytes accessed | tf_op | source)
XLA Modules:
  0.0 138.7 jit_solution(15212653334148877367)
XLA Ops:
  0.6 0.7 dynamic_slice.12
  1.4 0.8 eq.32
  2.1 0.2 select_reduce_fusion
  2.3 0.7 select_reduce_fusion.1
  3.1 0.8 dynamic-slice_convert_fusion.1
  3.8 0.7 maximum_convert_fusion
  4.5 0.1 broadcast_in_dim.28
  4.6 0.1 reshape.192
  4.7 0.6 fusion.10
  5.3 0.1 fusion.4
  5.3 0.7 select_n.79.refs_4_
  6.0 0.7 copy.40.refs_4_
  6.7 0.7 dynamic-slice_convert_fusion
  7.4 0.7 fusion.13
  8.1 0.6 reshape.191.refs_1_
  8.7 0.7 broadcast_in_dim.12
  9.5 0.7 reshape_reshape.4.refs_3_
  10.2 0.3 dynamic_update_slice.3.refs_8_
  10.5 0.0 copy-start
  10.5 0.7 copy-done
  11.2 0.0 copy-start.1
  11.2 44.2 %shard_map.176 = (f32[16,8,448]{2,1,0:T(8,128)}, f32[16,8,448]{2,1,0:T(8,128)}) custom-call(bf16[128,128]{1,0:T(8,128)(2,1)} %bitcast.9, bf16[1024,256]{1,0:T(8,128)(2,1)} %bitcast.7, bf16[1024,256]{1,0:T(8,128)(2,1)} %bitcast.8, s32[128,1]{1,0:T(8,128)} %reshape_reshape.4.refs_3_, s32[1,1024]{1,0:T(1,128)} %select_n.79.refs_4_, ...), custom_call_target="tpu_custom_call" | custom-call | tf_op jit(solution)/shard_map/pallas_call | solution.py:428
  55.4 1.0 constant_dynamic-slice_fusion
  56.4 1.7 %pad_maximum_fusion.refs_0_ = f32[16,8,462]{2,1,0:T(8,128)} fusion(f32[16,8,14]{2,1,0:T(8,128)S(1)} %constant_dynamic-slice_fusion, f32[16,8,448]{2,1,0:T(8,128)} %get-tuple-element.6), kind=kLoop, calls=%fused_computation | loop fusion | flops 59136 | bytes 473088 | tf_op jit(solution)/shard_map/concatenate | solution.py:597
  58.2 0.0 copy-done.1
  58.2 1.5 %copy.39.refs_3_ = bf16[896,448]{1,0:T(8,128)(2,1)} copy(bf16[896,448]{0,1:T(8,128)(2,1)S(1)} %copy-done.1) | data formatting | bytes 1605632 | tf_op args[14]
  59.7 76.3 %shard_map.177 = (bf16[14,128]{1,0:T(8,128)(2,1)}, f32[2,64]{1,0:T(2,128)}) custom-call(f32[16,8,462]{2,1,0:T(8,128)} %pad_maximum_fusion.refs_0_, f32[1,1920]{1,0:T(1,128)} %reshape.191.refs_1_, bf16[448,896]{1,0:T(8,128)(2,1)} %refs_2_.1, bf16[896,448]{1,0:T(8,128)(2,1)} %copy.39.refs_3_, f32[14,2]{1,0:T(8,128)} %copy.40.refs_4_), custom_call_target="tpu_custom_call" | custom-call | tf_op jit(solution)/shard_map/pallas_call | solution.py:456
  136.1 1.4 reshape.188
  137.4 1.2 copy.43
  (5 shorter events, 0.1 us)
Async XLA Ops:
  10.5 0.7 copy-start
  11.2 47.0 %copy-start.1 = (bf16[896,448]{0,1:T(8,128)(2,1)S(1)}, bf16[896,448]{0,1:T(8,128)(2,1)}, u32[]{:S(2)}) copy-start(bf16[896,448]{0,1:T(8,128)(2,1)} %param.31) | copy-start | bytes 2408452

commit v12 on v10

--- a/solution.py
+++ b/solution.py
@@ -343,7 +343,7 @@
             gather_arrival(k).wait_recv()
 
     projected_t = lax.dot_general(
-        w_down_ref[...], hid_ref[...], (((0,), (1,)), ((), ())), preferred_element_type=jnp.float32
+        w_down_ref[...], hid_ref[...], (((1,), (1,)), ((), ())), preferred_element_type=jnp.float32
     )
     for j in range(n_blk):
         pieces[j] = projected_t[j * width:(j + 1) * width]
@@ -584,7 +584,7 @@
     ).reshape(1, -1)
     columns = jnp.stack([b_down.astype(jnp.float32), w_score.astype(jnp.float32)], axis=1)
     outgoing = jnp.concatenate([scaled16, res_pieces], axis=-1)
-    output_t, row_score = mlp(outgoing, vectors, w_up, w_down, columns)
+    output_t, row_score = mlp(outgoing, vectors, w_up, w_down.T, columns)
     output = output_t.T
     return (output.reshape(samples, new_count, piece_width), row_score.reshape(samples, new_count))
 

time: 138 us -> 137 us (level)
  local copies, waits for them, and re-layouts: 10.8 us -> 9.21 us
    unnamed x17 -> x14, local copies, waits for them, and re-layouts: 2.9 us -> 1.37 us
where the time goes in v12:
time: 137 us; the launch traced here: 136 us
  Pallas kernels  120 us (88%)
  local copies, waits for them, and re-layouts  9.21 us (7%)
  other arithmetic  6.12 us (4%)
    pallas_call x1, Pallas kernels, mlp(): pl.pallas_call(lambda *refs: mlp_kernel(n_page, n_blk, *refs), out_shape=...  75.9 us
    pallas_call x1, Pallas kernels, attention_out(): pl.pallas_call(lambda *refs: attention_out_kernel(n_page, n_blk, heads, *...  44.2 us

profile of v12, /device:TPU:1, one launch (start us, length us, event | category | flops | bytes accessed | tf_op | source)
XLA Modules:
  0.0 136.2 jit_solution(13119106927097960494)
XLA Ops:
  0.6 0.7 dynamic-slice_convert_fusion
  1.3 0.8 dynamic-slice_convert_fusion.1
  2.1 0.3 dynamic_update_slice.3.refs_8_
  2.5 0.8 dynamic_slice.12
  3.2 0.1 broadcast_in_dim.28
  3.3 0.1 reshape.196
  3.4 0.6 fusion.10
  4.0 0.8 eq.32
  4.8 0.2 select_reduce_fusion
  5.0 0.7 select_reduce_fusion.1
  5.7 0.1 fusion.4
  5.8 0.7 select_n.79.refs_4_
  6.5 0.7 broadcast_in_dim.12
  7.2 0.7 reshape_reshape.4.refs_3_
  7.9 0.0 copy-done
  7.9 0.0 copy-start.4
  7.9 0.0 copy-start.5
  7.9 44.2 %shard_map.176 = (f32[16,8,448]{2,1,0:T(8,128)}, f32[16,8,448]{2,1,0:T(8,128)}) custom-call(bf16[128,128]{1,0:T(8,128)(2,1)} %bitcast.12, bf16[1024,256]{1,0:T(8,128)(2,1)} %bitcast.9, bf16[1024,256]{1,0:T(8,128)(2,1)} %bitcast.10, s32[128,1]{1,0:T(8,128)} %reshape_reshape.4.refs_3_, s32[1,1024]{1,0:T(1,128)} %select_n.79.refs_4_, ...), custom_call_target="tpu_custom_call" | custom-call | tf_op jit(solution)/shard_map/pallas_call | solution.py:417
  52.1 1.0 constant_dynamic-slice_fusion
  53.1 1.7 %pad_maximum_fusion.refs_0_ = f32[16,8,462]{2,1,0:T(8,128)} fusion(f32[16,8,14]{2,1,0:T(8,128)S(1)} %constant_dynamic-slice_fusion, f32[16,8,448]{2,1,0:T(8,128)} %get-tuple-element.6), kind=kLoop, calls=%fused_computation | loop fusion | flops 59136 | bytes 473088 | tf_op jit(solution)/shard_map/concatenate | solution.py:586
  54.9 0.0 copy-done.1
  54.9 0.0 copy-done.2
  54.9 0.0 copy-done.3
  54.9 0.6 reshape.195.refs_1_
  55.5 0.7 copy.46.refs_4_
  56.2 75.9 %shard_map.177 = (bf16[14,128]{1,0:T(8,128)(2,1)}, f32[1,128]{1,0:T(1,128)}) custom-call(f32[16,8,462]{2,1,0:T(8,128)} %pad_maximum_fusion.refs_0_, f32[1,1920]{1,0:T(1,128)} %reshape.195.refs_1_, bf16[448,896]{1,0:T(8,128)(2,1)} %refs_2_.1, bf16[448,896]{1,0:T(8,128)(2,1)} %bitcast.8, f32[14,2]{1,0:T(8,128)} %copy.46.refs_4_), custom_call_target="tpu_custom_call" | custom-call | tf_op jit(solution)/shard_map/pallas_call | solution.py:445
  132.1 0.8 copy.47
  132.9 0.7 copy.48
  133.6 0.5 broadcast.237
  134.1 1.3 reduce.3
  135.4 0.1 reshape.192
  135.6 0.6 copy.49
  (13 shorter events, 0.1 us)
Async XLA Ops:
  2.5 5.4 %copy-start = (f32[8,7168]{1,0:T(8,128)}, f32[8,7168]{1,0:T(8,128)S(1)}, u32[]{:S(2)}) copy-start(f32[8,7168]{1,0:T(8,128)S(1)} %dynamic_update_slice.3.refs_8_) | copy-start | bytes 688132
  7.9 47.0 %copy-start.1 = (bf16[896]{0:T(1024)(128)(2,1)S(1)}, bf16[896]{0:T(1024)(128)(2,1)}, u32[]{:S(2)}) copy-start(bf16[896]{0:T(1024)(128)(2,1)} %param.30) | copy-start | bytes 5380
  7.9 47.0 %copy-start.2 = (bf16[448]{0:T(512)(128)(2,1)S(1)}, bf16[448]{0:T(512)(128)(2,1)}, u32[]{:S(2)}) copy-start(bf16[448]{0:T(512)(128)(2,1)} %param.28) | copy-start | bytes 2692
  7.9 47.0 %copy-start.3 = (bf16[448]{0:T(512)(128)(2,1)S(1)}, bf16[448]{0:T(512)(128)(2,1)}, u32[]{:S(2)}) copy-start(bf16[448]{0:T(512)(128)(2,1)} %param.27) | copy-start | bytes 2692
  7.9 47.6 %copy-start.4 = (bf16[14]{0:T(256)(128)(2,1)S(1)}, bf16[14]{0:T(256)(128)(2,1)}, u32[]{:S(2)}) copy-start(bf16[14]{0:T(256)(128)(2,1)} %param.33) | copy-start | bytes 88
  7.9 47.6 %copy-start.5 = (bf16[14]{0:T(256)(128)(2,1)S(1)}, bf16[14]{0:T(256)(128)(2,1)}, u32[]{:S(2)}) copy-start(bf16[14]{0:T(256)(128)(2,1)} %param.32) | copy-start | bytes 88

commit v13 on v12

--- a/solution.py
+++ b/solution.py
@@ -238,20 +238,19 @@
     centred = residual - row_mean
     inverse_std = lax.rsqrt(jnp.mean(centred * centred, axis=-1, keepdims=True) + 1e-05)
     scaled = centred * inverse_std
-    group = scaled_ref.shape[2]
+    group = res_ref.shape[2]
+    scaled_ref[...] = jnp.zeros(scaled_ref.shape, jnp.float32)
     for q in range(n_page):
-        scaled_ref[q] = scaled[:, q * group:(q + 1) * group]
+        scaled_ref[q, :, 0:group] = scaled[:, q * group:(q + 1) * group]
         res_ref[q] = residual[:, q * group:(q + 1) * group]
 
-def mlp_kernel(n_page, n_blk, x_ref, vec_ref, w_ref, w_down_ref, col_ref, out_ref, score_ref,
+def mlp_kernel(n_page, n_blk, features, x_ref, vec_ref, w_ref, w_down_ref, col_ref, out_ref, score_ref,
                recv, up_s, red, hid_ref, pieces, out_buf, blk_buf, page_buf, sems):
     me = lax.axis_index("page")
     recv[me] = x_ref[me]
-    enter([("page", n_page), ("blk", n_blk)])
     send_round("page", n_page, lambda peer: x_ref.at[peer], recv, sems.at[0], sems.at[1])
     width = col_ref.shape[0]
     lanes_in = x_ref.shape[2]
-    features = lanes_in - width
     pad = -(-features // 128) * 128
     gain = vec_ref[:, 0:features]
     bias = vec_ref[:, pad:pad + features]
@@ -358,6 +357,28 @@
     columns = col_ref[...]
     output_phase(n_blk, n_page, pieces, res_t, columns[:, 0:1], columns[:, 1:2], out_ref, score_ref,
                  out_buf, blk_buf, page_buf, sems.at[6:12])
+
+
+def layer_kernel(n_page, n_blk, heads, features, q_ref, kv_ref, tkv_ref, row_code_ref, key_code_ref,
+                 t_lo_ref, t_hi_ref, w_ref, stream_ref, vec_ref, w_up_ref, w_down_ref, col_ref,
+                 out_ref, score_ref, res16, sc16, part_ref, recv1, full, res_s, red1, gat, sems1,
+                 recv2, up_s, red2, hid_ref, pieces, out_buf, blk_buf, page_buf, sems2):
+    attention_out_kernel(n_page, n_blk, heads, q_ref, kv_ref, tkv_ref, row_code_ref, key_code_ref,
+                         t_lo_ref, t_hi_ref, w_ref, stream_ref, res16, sc16, part_ref, recv1, full,
+                         res_s, red1, gat, sems1)
+    me_blk = lax.axis_index("blk")
+    width = col_ref.shape[0]
+    lanes_in = sc16.shape[2]
+    source = lax.broadcasted_iota(jnp.int32, (features, lanes_in), 0)
+    target = lax.broadcasted_iota(jnp.int32, (features, lanes_in), 1)
+    chosen = (target >= features) & (target < features + width) & (source == target - features + me_blk * width)
+    place = chosen.astype(jnp.float32)
+    for q in range(n_page):
+        sc16[q] = sc16[q] + jnp.dot(
+            res16[q], place, precision=lax.Precision.HIGHEST, preferred_element_type=jnp.float32
+        )
+    mlp_kernel(n_page, n_blk, features, sc16, vec_ref, w_up_ref, w_down_ref, col_ref, out_ref, score_ref,
+               recv2, up_s, red2, hid_ref, pieces, out_buf, blk_buf, page_buf, sems2)
 
 
 CALL_IDS = {}
@@ -463,6 +484,53 @@
         ],
         compiler_params=pltpu.CompilerParams(collective_id=next_id("both"), has_side_effects=True),
     )(outgoing, vectors, w_up, w_down, columns)
+
+
+def layer(queries, kv, tkv, row_code, key_code, t_lo, t_hi, w_out, stream, head_dim,
+          vectors, w_up, w_down_t, columns, features):
+    n_page = lax.axis_size("page")
+    n_blk = lax.axis_size("blk")
+    rows, width = stream.shape
+    heads = kv.shape[1] // (2 * head_dim)
+    lanes = 128 * (-(-width // (128 * n_blk)))
+    n_chunk = width // lanes
+    assert n_chunk * lanes == width
+    part_shape = (n_page, heads * rows, 2 * head_dim)
+    lanes_in = -(-(features + columns.shape[0]) // 128) * 128
+    all_rows = rows * n_page
+    ff = w_up.shape[1]
+    block = 2 * all_rows // n_page
+    piece = columns.shape[0]
+    return pl.pallas_call(
+        lambda *refs: layer_kernel(n_page, n_blk, heads, features, *refs),
+        out_shape=(
+            jax.ShapeDtypeStruct((piece, all_rows), jnp.bfloat16),
+            jax.ShapeDtypeStruct((1, all_rows), jnp.float32),
+        ),
+        in_specs=vmem_specs(13),
+        out_specs=tuple(vmem_specs(2)),
+        scratch_shapes=[
+            pltpu.VMEM((n_page, rows, features), jnp.float32),
+            pltpu.VMEM((n_page, rows, lanes_in), jnp.float32),
+            pltpu.VMEM(part_shape, jnp.float32),
+            pltpu.VMEM(part_shape, jnp.float32),
+            pltpu.VMEM((rows, width), jnp.float32),
+            pltpu.VMEM((rows, width), jnp.float32),
+            pltpu.VMEM((n_blk, rows, lanes), jnp.float32),
+            pltpu.VMEM((n_chunk, rows, lanes), jnp.float32),
+            pltpu.SemaphoreType.DMA((6, max(n_blk, n_page))),
+            pltpu.VMEM((n_page, rows, lanes_in), jnp.float32),
+            pltpu.VMEM((all_rows, ff), jnp.bfloat16),
+            pltpu.VMEM((n_page, block, ff), jnp.bfloat16),
+            pltpu.VMEM((all_rows, ff), jnp.bfloat16),
+            pltpu.VMEM((n_blk, piece, all_rows), jnp.float32),
+            pltpu.VMEM((n_blk, piece, all_rows), jnp.float32),
+            pltpu.VMEM((n_blk, 1, all_rows), jnp.float32),
+            pltpu.VMEM((n_page, 1, all_rows), jnp.float32),
+            pltpu.SemaphoreType.DMA((12, max(n_page, n_blk))),
+        ],
+        compiler_params=pltpu.CompilerParams(collective_id=next_id("both"), has_side_effects=True),
+    )(queries, kv, tkv, row_code, key_code, t_lo, t_hi, w_out, stream, vectors, w_up, w_down_t, columns)
 
 
 def output_and_score(x, res, bias, score_w):
@@ -558,7 +626,18 @@
     stream_full = lax.dynamic_update_slice_in_dim(
         jnp.zeros((rows_own, width), jnp.float32), own_stream + own_bias, column, 1
     )
-    residual16, scaled16 = attention_out(
+    feature_count = ln_gain.shape[0]
+    piece_width = b_down.shape[0]
+    pad = -(-feature_count // 128) * 128
+    vectors = jnp.concatenate(
+        [
+            jnp.pad(ln_gain.astype(jnp.float32), (0, pad - feature_count)),
+            jnp.pad(ln_bias.astype(jnp.float32), (0, pad - feature_count)),
+            b_up.astype(jnp.float32),
+        ]
+    ).reshape(1, -1)
+    columns = jnp.stack([b_down.astype(jnp.float32), w_score.astype(jnp.float32)], axis=1)
+    output_t, row_score = layer(
         queries.reshape(samples * new_count, heads_dev * head_dim),
         prompt_kv.reshape(slots_dev * page_len, heads_dev * 2 * head_dim),
         tail_kv.reshape(own_count * tail_max, heads_dev * 2 * head_dim),
@@ -569,22 +648,12 @@
         w_out,
         stream_full,
         head_dim,
-    )
-
-    feature_count = ln_gain.shape[0]
-    piece_width = b_down.shape[0]
-    res_pieces = lax.dynamic_slice_in_dim(residual16, blk_pos * piece_width, piece_width, 2)
-    pad = -(-feature_count // 128) * 128
-    vectors = jnp.concatenate(
-        [
-            jnp.pad(ln_gain.astype(jnp.float32), (0, pad - feature_count)),
-            jnp.pad(ln_bias.astype(jnp.float32), (0, pad - feature_count)),
-            b_up.astype(jnp.float32),
-        ]
-    ).reshape(1, -1)
-    columns = jnp.stack([b_down.astype(jnp.float32), w_score.astype(jnp.float32)], axis=1)
-    outgoing = jnp.concatenate([scaled16, res_pieces], axis=-1)
-    output_t, row_score = mlp(outgoing, vectors, w_up, w_down.T, columns)
+        vectors,
+        w_up,
+        w_down.T,
+        columns,
+        feature_count,
+    )
     output = output_t.T
     return (output.reshape(samples, new_count, piece_width), row_score.reshape(samples, new_count))
 

time: 137 us -> 131 us (0.956)
  Pallas kernels: 120 us -> 116 us
    pallas_call x2 -> x1, Pallas kernels: 120 us -> 116 us  [layer(): pl.pallas_call(lambda *refs: layer_kernel(n_page, n_blk, heads, features,...]
    concatenate x1 -> x0, other arithmetic: 1.74 us -> none  [body(): outgoing = jnp.concatenate([scaled16, res_pieces], axis=-1)]
where the time goes in v13:
time: 131 us
  Pallas kernels  116 us (89%)
  local copies, waits for them, and re-layouts  8.21 us (6%)
  other arithmetic  5.8 us (4%)
    pallas_call x1, Pallas kernels, layer(): pl.pallas_call(lambda *refs: layer_kernel(n_page, n_blk, heads, features,...  116 us

profile of v13, /device:TPU:1, one launch (start us, length us, event | category | flops | bytes accessed | tf_op | source)
XLA Modules:
  0.0 130.9 jit_solution(3863057439982729932)
XLA Ops:
  0.6 0.7 dynamic-slice_convert_fusion
  1.3 0.8 dynamic-slice_convert_fusion.1
  2.1 0.3 dynamic_update_slice.3.refs_8_
  2.5 0.0 copy-start
  2.5 0.8 dynamic_slice.9
  3.2 0.1 broadcast_in_dim.28
  3.3 0.1 reshape.196
  3.4 0.6 fusion.10
  4.0 0.8 eq.32
  4.8 0.2 select_reduce_fusion
  5.0 0.7 select_reduce_fusion.1
  5.7 0.1 fusion.4
  5.8 0.7 select_n.76.refs_4_
  6.5 0.7 broadcast_in_dim.12
  7.2 0.7 reshape_reshape.4.refs_3_
  7.9 0.7 fusion.13
  8.6 0.6 reshape.195.refs_9_
  9.2 0.7 maximum_convert_fusion
  9.9 0.7 copy.46.refs_12_
  10.6 0.0 copy-done
  10.6 116.2 %shard_map.176 = (bf16[14,128]{1,0:T(8,128)(2,1)}, f32[1,128]{1,0:T(1,128)}) custom-call(bf16[128,128]{1,0:T(8,128)(2,1)} %bitcast.12, bf16[1024,256]{1,0:T(8,128)(2,1)} %bitcast.9, bf16[1024,256]{1,0:T(8,128)(2,1)} %bitcast.10, s32[128,1]{1,0:T(8,128)} %reshape_reshape.4.refs_3_, s32[1,1024]{1,0:T(1,128)} %select_n.76.refs_4_, ...), custom_call_target="tpu_custom_call" | custom-call | tf_op jit(solution)/shard_map/pallas_call | solution.py:504
  126.8 0.8 copy.47
  127.6 0.7 copy.48
  128.3 0.5 broadcast.237
  128.8 1.3 reduce.3
  130.1 0.1 reshape.192
  130.2 0.6 copy.49
  (5 shorter events, 0.1 us)
Async XLA Ops:
  2.5 8.1 %copy-start = (f32[8,7168]{1,0:T(8,128)}, f32[8,7168]{1,0:T(8,128)S(1)}, u32[]{:S(2)}) copy-start(f32[8,7168]{1,0:T(8,128)S(1)} %dynamic_update_slice.3.refs_8_) | copy-start | bytes 688132

commit v14 on v13

--- a/solution.py
+++ b/solution.py
@@ -349,10 +349,9 @@
     pick = (
         lax.broadcasted_iota(jnp.int32, (width, lanes_in), 1)
         == lax.broadcasted_iota(jnp.int32, (width, lanes_in), 0) + features
-    ).astype(jnp.float32)
+    ).astype(jnp.bfloat16)
     res_t = lax.dot_general(
-        pick, arrived, (((1,), (1,)), ((), ())),
-        precision=lax.Precision.HIGHEST, preferred_element_type=jnp.float32,
+        pick, arrived.astype(jnp.bfloat16), (((1,), (1,)), ((), ())), preferred_element_type=jnp.float32
     )
     columns = col_ref[...]
     output_phase(n_blk, n_page, pieces, res_t, columns[:, 0:1], columns[:, 1:2], out_ref, score_ref,
@@ -372,10 +371,10 @@
     source = lax.broadcasted_iota(jnp.int32, (features, lanes_in), 0)
     target = lax.broadcasted_iota(jnp.int32, (features, lanes_in), 1)
     chosen = (target >= features) & (target < features + width) & (source == target - features + me_blk * width)
-    place = chosen.astype(jnp.float32)
+    place = chosen.astype(jnp.bfloat16)
     for q in range(n_page):
         sc16[q] = sc16[q] + jnp.dot(
-            res16[q], place, precision=lax.Precision.HIGHEST, preferred_element_type=jnp.float32
+            res16[q].astype(jnp.bfloat16), place, preferred_element_type=jnp.float32
         )
     mlp_kernel(n_page, n_blk, features, sc16, vec_ref, w_up_ref, w_down_ref, col_ref, out_ref, score_ref,
                recv2, up_s, red2, hid_ref, pieces, out_buf, blk_buf, page_buf, sems2)

time: 131 us -> 128 us (0.977)
  Pallas kernels: 116 us -> 113 us
    pallas_call x1, Pallas kernels: 116 us -> 113 us  [layer(): pl.pallas_call(lambda *refs: layer_kernel(n_page, n_blk, heads, features,...]
where the time goes in v14:
time: 128 us
  Pallas kernels  113 us (88%)
  local copies, waits for them, and re-layouts  8.21 us (6%)
  other arithmetic  5.8 us (5%)
    pallas_call x1, Pallas kernels, layer(): pl.pallas_call(lambda *refs: layer_kernel(n_page, n_blk, heads, features,...  113 us

profile of v14, /device:TPU:1, one launch (start us, length us, event | category | flops | bytes accessed | tf_op | source)
XLA Modules:
  0.0 127.9 jit_solution(5102371109200382116)
XLA Ops:
  0.6 0.7 dynamic-slice_convert_fusion
  1.3 0.8 dynamic-slice_convert_fusion.1
  2.1 0.3 dynamic_update_slice.3.refs_8_
  2.5 0.0 copy-start
  2.5 0.8 dynamic_slice.9
  3.2 0.1 broadcast_in_dim.28
  3.3 0.1 reshape.196
  3.4 0.6 fusion.10
  4.0 0.8 eq.32
  4.8 0.2 select_reduce_fusion
  5.0 0.7 select_reduce_fusion.1
  5.7 0.1 fusion.4
  5.8 0.7 select_n.76.refs_4_
  6.5 0.7 broadcast_in_dim.12
  7.2 0.7 reshape_reshape.4.refs_3_
  7.9 0.7 fusion.13
  8.6 0.6 reshape.195.refs_9_
  9.2 0.7 maximum_convert_fusion
  9.9 0.7 copy.46.refs_12_
  10.6 0.0 copy-done
  10.6 113.3 %shard_map.176 = (bf16[14,128]{1,0:T(8,128)(2,1)}, f32[1,128]{1,0:T(1,128)}) custom-call(bf16[128,128]{1,0:T(8,128)(2,1)} %bitcast.12, bf16[1024,256]{1,0:T(8,128)(2,1)} %bitcast.9, bf16[1024,256]{1,0:T(8,128)(2,1)} %bitcast.10, s32[128,1]{1,0:T(8,128)} %reshape_reshape.4.refs_3_, s32[1,1024]{1,0:T(1,128)} %select_n.76.refs_4_, ...), custom_call_target="tpu_custom_call" | custom-call | tf_op jit(solution)/shard_map/pallas_call | solution.py:503
  123.9 0.8 copy.47
  124.7 0.7 copy.48
  125.4 0.5 broadcast.237
  125.9 1.3 %reduce.3 = f32[128]{0:T(128)S(1)} reduce(f32[1,128]{1,0:T(1,128)} %get-tuple-element.5, f32[]{:T(128)} %broadcast.237), dimensions={0}, to_apply=%get-tuple-element.5.reduce_sub_computation.3 | reduce | bytes 1028 | tf_op jit(solution)/shard_map/pallas_call | solution.py:503
  127.2 0.1 reshape.192
  127.3 0.6 copy.49
  (5 shorter events, 0.1 us)
Async XLA Ops:
  2.5 8.1 %copy-start = (f32[8,7168]{1,0:T(8,128)}, f32[8,7168]{1,0:T(8,128)S(1)}, u32[]{:S(2)}) copy-start(f32[8,7168]{1,0:T(8,128)S(1)} %dynamic_update_slice.3.refs_8_) | copy-start | bytes 688132

commit v15 on v14

--- a/solution.py
+++ b/solution.py
@@ -372,10 +372,11 @@
     target = lax.broadcasted_iota(jnp.int32, (features, lanes_in), 1)
     chosen = (target >= features) & (target < features + width) & (source == target - features + me_blk * width)
     place = chosen.astype(jnp.bfloat16)
+    rows = res16.shape[1]
+    stacked = jnp.concatenate([res16[q] for q in range(n_page)], axis=0).astype(jnp.bfloat16)
+    placed = jnp.dot(stacked, place, preferred_element_type=jnp.float32)
     for q in range(n_page):
-        sc16[q] = sc16[q] + jnp.dot(
-            res16[q].astype(jnp.bfloat16), place, preferred_element_type=jnp.float32
-        )
+        sc16[q] = sc16[q] + placed[q * rows:(q + 1) * rows]
     mlp_kernel(n_page, n_blk, features, sc16, vec_ref, w_up_ref, w_down_ref, col_ref, out_ref, score_ref,
                recv2, up_s, red2, hid_ref, pieces, out_buf, blk_buf, page_buf, sems2)
 

time: 128 us -> 128 us (level)
  no operation moved by 1% of the time
where the time goes in v15:
time: 128 us
  Pallas kernels  113 us (88%)
  local copies, waits for them, and re-layouts  8.21 us (6%)
  other arithmetic  5.8 us (5%)
    pallas_call x1, Pallas kernels, layer(): pl.pallas_call(lambda *refs: layer_kernel(n_page, n_blk, heads, features,...  113 us

profile of v15, /device:TPU:1, one launch (start us, length us, event | category | flops | bytes accessed | tf_op | source)
XLA Modules:
  0.0 127.6 jit_solution(3811925328946290393)
XLA Ops:
  0.6 0.7 dynamic-slice_convert_fusion
  1.3 0.8 dynamic-slice_convert_fusion.1
  2.1 0.3 dynamic_update_slice.3.refs_8_
  2.5 0.0 copy-start
  2.5 0.8 dynamic_slice.9
  3.2 0.1 broadcast_in_dim.28
  3.3 0.1 reshape.196
  3.4 0.6 fusion.10
  4.0 0.8 eq.32
  4.8 0.2 select_reduce_fusion
  5.0 0.7 select_reduce_fusion.1
  5.7 0.1 fusion.4
  5.8 0.7 select_n.76.refs_4_
  6.5 0.7 broadcast_in_dim.12
  7.2 0.7 reshape_reshape.4.refs_3_
  7.9 0.7 fusion.13
  8.6 0.6 reshape.195.refs_9_
  9.2 0.7 maximum_convert_fusion
  9.9 0.7 copy.46.refs_12_
  10.6 0.0 copy-done
  10.6 112.9 %shard_map.176 = (bf16[14,128]{1,0:T(8,128)(2,1)}, f32[1,128]{1,0:T(1,128)}) custom-call(bf16[128,128]{1,0:T(8,128)(2,1)} %bitcast.12, bf16[1024,256]{1,0:T(8,128)(2,1)} %bitcast.9, bf16[1024,256]{1,0:T(8,128)(2,1)} %bitcast.10, s32[128,1]{1,0:T(8,128)} %reshape_reshape.4.refs_3_, s32[1,1024]{1,0:T(1,128)} %select_n.76.refs_4_, ...), custom_call_target="tpu_custom_call" | custom-call | tf_op jit(solution)/shard_map/pallas_call | solution.py:504
  123.5 0.8 copy.47
  124.3 0.7 copy.48
  125.0 0.5 broadcast.237
  125.5 1.3 %reduce.3 = f32[128]{0:T(128)S(1)} reduce(f32[1,128]{1,0:T(1,128)} %get-tuple-element.5, f32[]{:T(128)} %broadcast.237), dimensions={0}, to_apply=%get-tuple-element.5.reduce_sub_computation.3 | reduce | bytes 1028 | tf_op jit(solution)/shard_map/pallas_call | solution.py:504
  126.8 0.1 reshape.192
  127.0 0.6 copy.49
  (5 shorter events, 0.1 us)
Async XLA Ops:
  2.5 8.1 %copy-start = (f32[8,7168]{1,0:T(8,128)}, f32[8,7168]{1,0:T(8,128)S(1)}, u32[]{:S(2)}) copy-start(f32[8,7168]{1,0:T(8,128)S(1)} %dynamic_update_slice.3.refs_8_) | copy-start | bytes 688132
